TPU v7x, 768 devices: a whole 4x8x12 slice. The times are simulated.
768 devices in a mesh: gx: 8 (over x, core), gy: 8 (over y), gz: 12 (over z).
Axes of the slice: x: 4, y: 8, z: 12, core: 2. Of those that a mesh axis runs over, the one named last changes fastest.
Arguments:
- right_side: float32 [64, 64, 1536], P('gx', 'gy', 'gz'), may hold values from -8 to 8
- geometry: float32 [4, 64, 64, 1536], P(None, 'gx', 'gy', 'gz'), may hold values from 0.02 to 0.2
- element_shape_class: int32 [8, 8, 192], P('gx', 'gy', 'gz'), may hold values from 0 to 31
- fdm_vectors: float32 [32, 3, 10, 10], replicated, may hold values from -1 to 2
- fdm_values: float32 [32, 3, 10], replicated, may hold values from 0.3 to 10
Outputs:
- solution: float32 [64, 64, 1536], P('gx', 'gy', 'gz')
- residual: float32 [64, 64, 1536], P('gx', 'gy', 'gz')
All inputs are finite; a program needn't handle non-finite values.
Results may differ from a plain program's by a relative error of at most 0.0003.
Values sent between devices are 32-bit elements; how exact they have to be, the bound alone decides.
No kernel may reach another device: no remote copies, remote signals or barrier semaphores. Data moves between devices by JAX's collectives and lax.ppermute only.
A program may use at most 32 MiB of HBM per device.

v0:
```python
import functools

import jax
import jax.numpy as jnp
import numpy as np
from jax import lax
from jax.experimental import pallas as pl
from jax.experimental.pallas import tpu as pltpu
from jax.sharding import PartitionSpec as P

HIGHEST = lax.Precision.HIGHEST
LANES = 128
REACH = 4
CHUNKS = ((0, 24), (24, 24), (48, 24), (72, 28))


def swap_ends(block, axis, dim, width):
    count = lax.axis_size(axis)
    forward = [(i, i + 1) for i in range(count - 1)]
    backward = [(target, source) for source, target in forward]
    length = block.shape[dim]
    low = lax.ppermute(lax.slice_in_dim(block, length - width, length, axis=dim), axis, forward)
    high = lax.ppermute(lax.slice_in_dim(block, 0, width, axis=dim), axis, backward)
    return low, high


def cut(block, start, stop, dim):
    return lax.slice_in_dim(block, start, stop, axis=dim)


def extend_one(field, axis, dim, add):
    low, high = swap_ends(field, axis, dim, 2)
    first, last = cut(field, 0, 1, dim), cut(field, 7, 8, dim)
    if add:
        first = first + cut(low, 1, 2, dim)
        last = last + cut(high, 0, 1, dim)
    return jnp.concatenate(
        [cut(low, 0, 1, dim), first, cut(field, 1, 7, dim), last, cut(high, 1, 2, dim)], axis=dim
    )


def derivative_table():
    points = np.array(
        [
            -1.0,
            -0.8717401485096066,
            -0.5917001814331423,
            -0.2092992179024789,
            0.2092992179024789,
            0.5917001814331423,
            0.8717401485096066,
            1.0,
        ]
    )
    previous = np.ones(8)
    current = points * 1.0
    for order in range(1, 7):
        following = ((2 * order + 1) * points * current - order * previous) / (order + 1)
        previous = current
        current = following
    spacing = points[:, None] - points[None, :] + np.eye(8)
    off_diagonal = current[:, None] / (current[None, :] * spacing)
    positions = np.arange(8)
    end_values = np.where(positions == 0, -14.0, 0.0) + np.where(positions == 7, 14.0, 0.0)
    return np.where(np.eye(8) > 0, np.eye(8) * end_values[None, :], off_diagonal)


def fold_one(block, axis, dim):
    low, high = swap_ends(block, axis, dim, 2)
    return jnp.concatenate(
        [
            cut(block, 1, 3, dim) + low,
            cut(block, 3, 7, dim),
            cut(block, 7, 9, dim) + high,
        ],
        axis=dim,
    )


def own_lanes(count):
    lane = lax.broadcasted_iota(jnp.int32, (1, LANES), 1)
    return (lane >= REACH) & (lane < REACH + count)


def solve_step(source, target, table, base, transposed, scale=None):
    for start, size in CHUNKS:
        entries = [source[pl.ds(10 * start + k, size, stride=10), :] for k in range(10)]
        for out in range(10):
            total = None
            for k in range(10):
                row = base + (10 * out + k if transposed else 10 * k + out)
                term = table[row : row + 1, :] * entries[k]
                total = term if total is None else total + term
            if scale is not None:
                total = total / (table[300 + out : 301 + out, :] + scale[start : start + size, :])
            target[pl.ds(100 * out + start, size), :] = total


def solve_kernel(count, shared, field, low, high, table, valid, *refs):
    if shared:
        folded, inner, size_row, assembled, blocks, left, right, pair = refs
    else:
        folded, inner, blocks, left, right, pair = refs
    blocks[pl.ds(1000, 40), :] = jnp.zeros((40, LANES), jnp.float32)
    left[pl.ds(1000, 40), :] = jnp.zeros((40, LANES), jnp.float32)
    right[pl.ds(1000, 40), :] = jnp.zeros((40, LANES), jnp.float32)
    for a in range(10):
        for b in range(10):
            if b == 0:
                nodes = low[a, 0]
            elif b == 9:
                nodes = high[a, 1]
            else:
                nodes = field[a, b - 1]
                if shared and b == 1:
                    nodes = nodes + low[a, 1]
                if shared and b == 8:
                    nodes = nodes + high[a, 0]
                if shared and 1 <= a <= 8:
                    assembled[pl.ds(64 * (a - 1) + 8 * (b - 1), 8), :] = nodes
            blocks[pl.ds(100 * a + 10 * b + 1, 8), :] = nodes
    blocks[pl.ds(0, 100, stride=10), :] = pltpu.roll(
        blocks[pl.ds(7, 100, stride=10), :], 1, 1
    )
    blocks[pl.ds(9, 100, stride=10), :] = pltpu.roll(
        blocks[pl.ds(2, 100, stride=10), :], LANES - 1, 1
    )
    for n in range(10):
        pair[pl.ds(10 * n, 10), :] = table[310 + n : 311 + n, :] + table[320:330, :]
    solve_step(blocks, left, table, 200, False)
    solve_step(left, right, table, 100, False)
    solve_step(right, left, table, 0, False, pair)
    solve_step(left, right, table, 200, True)
    solve_step(right, left, table, 100, True)
    solve_step(left, right, table, 0, True)
    exists = valid[...] > 0.0
    own = own_lanes(count)
    unit = 1.0
    if shared:
        largest = jnp.zeros((8, LANES), jnp.float32)
        for row in range(0, 1000, 8):
            largest = jnp.maximum(largest, jnp.abs(blocks[row : row + 8, :]))
        size = jnp.max(jnp.where(own, largest, 0.0))
        unit = 1.0 / jnp.where(size > 0.0, size, 1.0)
        size_row[...] = jnp.full((1, LANES), size, jnp.float32)
    total = jnp.zeros((8, LANES), jnp.float32)
    for row in range(0, 1000, 8):
        total = total + (blocks[row : row + 8, :] * unit) * (right[row : row + 8, :] * unit)
    inner[...] = jnp.sum(jnp.where(own, total, 0.0), axis=0, keepdims=True)

    def entry(c):
        return jnp.where(exists, right[pl.ds(c, 100, stride=10), :], 0.0)

    first, second, second_last, last = entry(0), entry(1), entry(8), entry(9)
    right[pl.ds(1, 100, stride=10), :] = second + pltpu.roll(second_last, 1, 1)
    right[pl.ds(2, 100, stride=10), :] = entry(2) + pltpu.roll(last, 1, 1)
    right[pl.ds(7, 100, stride=10), :] = entry(7) + pltpu.roll(first, LANES - 1, 1)
    right[pl.ds(8, 100, stride=10), :] = second_last + pltpu.roll(second, LANES - 1, 1)
    for a in range(10):
        for b in range(10):
            folded[a, b] = right[pl.ds(100 * a + 10 * b + 1, 8), :]


def block_solve(field, low, high, table, valid, count, shared):
    row = jax.ShapeDtypeStruct((1, LANES), jnp.float32)
    outs = [jax.ShapeDtypeStruct((10, 10, 8, LANES), jnp.float32), row]
    if shared:
        outs += [row, jax.ShapeDtypeStruct((512, LANES), jnp.float32)]
    return pl.pallas_call(
        functools.partial(solve_kernel, count, shared),
        out_shape=outs,
        scratch_shapes=[pltpu.VMEM((1040, LANES), jnp.float32)] * 3
        + [pltpu.VMEM((104, LANES), jnp.float32)],
        name="block_solve_shared" if shared else "block_solve_first",
    )(field, low, high, table, valid)


def both_ways(nodes, metric, derivative):
    slopes = []
    for a in range(8):
        total = None
        for i in range(8):
            if derivative[a, i] != 0.0:
                term = float(derivative[a, i]) * nodes[i]
                total = term if total is None else total + term
        slopes.append(metric[a] * total)
    outs = []
    for i in range(8):
        total = None
        for a in range(8):
            if derivative[a, i] != 0.0:
                term = float(derivative[a, i]) * slopes[a]
                total = term if total is None else total + term
        outs.append(total)
    return outs


def to_lines(sources, count):
    lane = lax.broadcasted_iota(jnp.int32, (LANES, LANES), 0)
    place = lax.broadcasted_iota(jnp.int32, (LANES, LANES), 1)
    total = jnp.zeros((64 * len(sources), LANES), jnp.float32)
    for k in range(8):
        pick = (
            (place == 8 * (lane - REACH) + k) & (lane >= REACH) & (lane < REACH + count)
        ).astype(jnp.bfloat16)
        rest = jnp.concatenate([s[pl.ds(k, 64, stride=8), :] for s in sources], axis=0)
        rest = jnp.where(own_lanes(count), rest, 0.0)
        for _ in range(3):
            part = rest.astype(jnp.bfloat16)
            total = total + jnp.dot(part, pick, preferred_element_type=jnp.float32)
            rest = rest - part.astype(jnp.float32)
    return total


def apply_local(derivative, folded, low, high, geometry, field, image):
    for x in range(8):
        for y in range(8):
            nodes = folded[x + 1, y]
            if x < 2:
                nodes = nodes + low[x, y]
            if x > 5:
                nodes = nodes + high[x - 6, y]
            field[pl.ds(64 * x + 8 * y, 8), :] = nodes
    for row in range(0, 512, 8):
        image[row : row + 8, :] = geometry[1536 + row : 1544 + row, :] * field[row : row + 8, :]
    for line in range(8):
        for dim in range(3):
            if dim == 0:
                spots = [pl.ds(64 * i + 8 * line, 8) for i in range(8)]
                places = spots
            elif dim == 1:
                spots = [pl.ds(64 * line + 8 * i, 8) for i in range(8)]
                places = [pl.ds(512 + 64 * line + 8 * i, 8) for i in range(8)]
            else:
                spots = [pl.ds(64 * line + i, 8, stride=8) for i in range(8)]
                places = [pl.ds(1024 + 64 * line + i, 8, stride=8) for i in range(8)]
            outs = both_ways(
                [field[s, :] for s in spots], [geometry[s, :] for s in places], derivative
            )
            for spot, out in zip(spots, outs):
                image[spot, :] = image[spot, :] + out


def first_operator_kernel(count, derivative, folded, low, high, geometry, field, image, inner):
    apply_local(derivative, folded, low, high, geometry, field, image)
    total = jnp.zeros((8, LANES), jnp.float32)
    for row in range(0, 512, 8):
        total = total + field[row : row + 8, :] * image[row : row + 8, :]
    inner[...] = jnp.sum(jnp.where(own_lanes(count), total, 0.0), axis=0, keepdims=True)
    first = image[pl.ds(0, 64, stride=8), :]
    last = image[pl.ds(7, 64, stride=8), :]
    image[pl.ds(0, 64, stride=8), :] = first + pltpu.roll(last, 1, 1)
    image[pl.ds(7, 64, stride=8), :] = last + pltpu.roll(first, LANES - 1, 1)


def first_operator(folded, low, high, geometry, count):
    full = jax.ShapeDtypeStruct((512, LANES), jnp.float32)
    return pl.pallas_call(
        functools.partial(first_operator_kernel, count, derivative_table()),
        out_shape=[full, full, jax.ShapeDtypeStruct((1, LANES), jnp.float32)],
        name="first_operator",
    )(folded, low, high, geometry)


def spread(values):
    lane = lax.broadcasted_iota(jnp.int32, (1, LANES), 1)
    row = jnp.zeros((1, LANES), jnp.float32)
    for place, value in enumerate(values):
        row = jnp.where(lane == place, value, row)
    return row


def second_operator_kernel(
    count, derivative, folded, low, high, geometry, rho, d, g, size, lines, payload, field, image
):
    apply_local(derivative, folded, low, high, geometry, field, image)
    largest = size[0, 0]
    unit = 1.0 / jnp.where(largest > 0.0, largest, 1.0)
    own = own_lanes(count)
    total = jnp.zeros((8, LANES), jnp.float32)
    for row in range(0, 512, 8):
        total = total + (field[row : row + 8, :] * unit) * (image[row : row + 8, :] * unit)
    h = jnp.sum(jnp.where(own, total, 0.0))
    row = spread([jnp.sum(rho[...]), jnp.sum(d[...]), jnp.sum(g[...]), h, largest])
    payload[...] = jnp.broadcast_to(row, payload.shape)
    lines[...] = to_lines([field, image], count)


def second_operator(folded, low, high, geometry, rho, d, g, size, count, devices):
    return pl.pallas_call(
        functools.partial(second_operator_kernel, count, derivative_table()),
        out_shape=[
            jax.ShapeDtypeStruct((128, LANES), jnp.float32),
            jax.ShapeDtypeStruct((devices, LANES), jnp.float32),
        ],
        scratch_shapes=[pltpu.VMEM((512, LANES), jnp.float32)] * 2,
        name="second_operator",
    )(folded, low, high, geometry, rho, d, g, size)


def lines_kernel(count, one, two, lines):
    lines[...] = to_lines([one, two], count)


def as_lines(one, two, count):
    return pl.pallas_call(
        functools.partial(lines_kernel, count),
        out_shape=jax.ShapeDtypeStruct((128, LANES), jnp.float32),
        name="as_lines",
    )(one, two)


def combine(rows, first):
    size_each = rows[:, first + 4 : first + 5]
    size = jnp.max(size_each)
    ratio = size_each / jnp.where(size > 0.0, size, 1.0)
    factor = ratio * ratio
    return (
        jnp.sum(rows[:, first : first + 1]),
        jnp.sum(rows[:, first + 1 : first + 2]),
        jnp.sum(rows[:, first + 2 : first + 3] * factor),
        jnp.sum(rows[:, first + 3 : first + 4] * factor),
        size,
    )


def middle_kernel(spot, gathered, image, out):
    values = combine(gathered[...], 0)
    lane = lax.broadcasted_iota(jnp.int32, (1, LANES), 1)
    scalars = jnp.zeros((1, LANES), jnp.float32)
    for place, value in enumerate(values):
        scalars = jnp.where(lane == 64 + place, value, scalars)
    line = lax.broadcasted_iota(jnp.int32, (64, LANES), 0)
    across = lax.broadcasted_iota(jnp.int32, (64, LANES), 1)
    first = jnp.sum(jnp.where(line == across, image[:, 0:1], 0.0), axis=0, keepdims=True)
    last = jnp.sum(
        jnp.where(line == across, image[:, LANES - 1 : LANES], 0.0), axis=0, keepdims=True
    )
    target = lax.broadcasted_iota(jnp.int32, out.shape, 0)
    me = spot[0]
    out[...] = scalars + jnp.where(
        target == me + 1, last, jnp.where(target == me - 1, first, 0.0)
    )


def middle(spot, gathered, image, devices):
    smem = pl.BlockSpec(memory_space=pltpu.SMEM)
    vmem = pl.BlockSpec(memory_space=pltpu.VMEM)
    return pl.pallas_call(
        middle_kernel,
        out_shape=jax.ShapeDtypeStruct((devices, LANES), jnp.float32),
        in_specs=[smem, vmem, vmem],
        out_specs=vmem,
        name="middle",
    )(spot, gathered, image)


def finish_kernel(spot, gathered, image, second, first, right_side, solution_out, residual_out):
    rows = gathered[...]
    rho, d, g_scaled, h_scaled, size = combine(rows, 64)
    me = spot[0]
    source = lax.broadcasted_iota(jnp.int32, rows.shape, 0)
    before = jnp.sum(jnp.where(source == me - 1, rows, 0.0), axis=0, keepdims=True)
    after = jnp.sum(jnp.where(source == me + 1, rows, 0.0), axis=0, keepdims=True)
    line = lax.broadcasted_iota(jnp.int32, (64, LANES), 0)
    across = lax.broadcasted_iota(jnp.int32, (64, LANES), 1)
    before = jnp.sum(jnp.where(line == across, before, 0.0), axis=1, keepdims=True)
    after = jnp.sum(jnp.where(line == across, after, 0.0), axis=1, keepdims=True)
    t = image[...]
    behind = pltpu.roll(t, 1, 1)
    ahead = pltpu.roll(t, LANES - 1, 1)
    t = t + jnp.where(
        across % 8 == 7,
        jnp.where(across == LANES - 1, after, ahead),
        jnp.where(across % 8 == 0, jnp.where(across == 0, before, behind), 0.0),
    )
    def splat(value):
        return jnp.full((1, LANES), value, jnp.float32)

    rho, d = splat(rho), splat(d)
    alpha_one = rho / d
    reach = alpha_one * splat(size)
    g = reach * reach * splat(g_scaled)
    h = reach * reach * splat(h_scaled)
    stretch = g / rho
    alpha_two = (g - rho) / (h - stretch * g / alpha_one)
    along = alpha_one + alpha_two * stretch
    turn = alpha_one * alpha_two
    solution_out[...] = along * first[0:64, :] - turn * second[0:64, :]
    residual_out[...] = right_side[...] - along * first[64:128, :] + turn * t


def finish(spot, gathered, image, second, first, right_side):
    smem = pl.BlockSpec(memory_space=pltpu.SMEM)
    vmem = pl.BlockSpec(memory_space=pltpu.VMEM)
    full = jax.ShapeDtypeStruct((64, LANES), jnp.float32)
    return pl.pallas_call(
        finish_kernel,
        out_shape=[full, full],
        in_specs=[smem] + [vmem] * 5,
        out_specs=[vmem, vmem],
        name="finish",
    )(spot, gathered, image, second, first, right_side)


def exchange(rows, axes):
    return lax.all_to_all(rows, axes, 0, 0, tiled=True)


def shared_sum(field, axis, dim):
    low, high = swap_ends(field, axis, dim, 1)
    return jnp.concatenate(
        [cut(field, 0, 1, dim) + low, cut(field, 1, 7, dim), cut(field, 7, 8, dim) + high],
        axis=dim,
    )


def on_lanes(field):
    split = field.reshape(field.shape[:-1] + (field.shape[-1] // 8, 8))
    turned = jnp.swapaxes(split, -1, -2)
    return jnp.pad(turned, [(0, 0)] * (turned.ndim - 1) + [(0, LANES - turned.shape[-1])])


def on_device(right_side, geometry, element_shape_class, fdm_vectors, fdm_values):
    count = element_shape_class.shape[2]
    classes = fdm_vectors.shape[0]
    depth = lax.axis_size("gz")
    plane = lax.axis_size("gx") * lax.axis_size("gy")
    me = lax.axis_index("gz")
    ends = 8 * REACH

    def deepen(field):
        low, high = swap_ends(field, "gz", field.ndim - 1, ends)
        return jnp.concatenate([low, field, high], axis=field.ndim - 1)

    class_line = jnp.repeat(element_shape_class.reshape(1, 1, -1), 8, axis=2).astype(jnp.float32)
    class_lines = jnp.broadcast_to(class_line, (1, 8, 8 * count))
    deep = deepen(jnp.concatenate([right_side, class_lines], axis=0))
    metric = on_lanes(deepen(geometry)).reshape(4 * 512, LANES)
    deep_class = deep[8, 0, ::8].astype(jnp.int32)
    deep_class = jnp.pad(deep_class, (0, LANES - deep_class.shape[0]))
    element = jnp.arange(LANES, dtype=jnp.int32) - REACH + me * count
    valid = ((element >= 0) & (element < depth * count)).astype(jnp.float32)[None, :]
    onehot = (jnp.arange(classes, dtype=jnp.int32)[:, None] == deep_class[None, :]).astype(
        jnp.float32
    )
    entries = jnp.concatenate(
        [fdm_vectors.reshape(classes, 300), fdm_values.reshape(classes, 30)], axis=1
    )
    table = lax.dot_general(
        entries, onehot, (((0,), (0,)), ((), ())), precision=HIGHEST
    )
    field = extend_one(on_lanes(deep[:8]), "gx", 0, False)
    low, high = swap_ends(field, "gy", 1, 2)
    folded, rho = block_solve(field, low, high, table, valid, count, False)
    folded = fold_one(folded, "gy", 1)
    low, high = swap_ends(folded, "gx", 0, 2)
    p, image, d = first_operator(folded, low, high, metric, count)
    field = extend_one(image.reshape(8, 8, 8, LANES), "gx", 0, True)
    low, high = swap_ends(field, "gy", 1, 2)
    folded, g, size, q = block_solve(field, low, high, table, valid, count, True)
    first = as_lines(p, q, count)
    folded = fold_one(folded, "gy", 1)
    low, high = swap_ends(folded, "gx", 0, 2)
    second, payload = second_operator(folded, low, high, metric, rho, d, g, size, count, plane)
    image = shared_sum(second[64:].reshape(8, 8, LANES), "gx", 0)
    image = shared_sum(image, "gy", 1).reshape(64, LANES)
    payload, image = lax.optimization_barrier((payload, image))
    spot = me.astype(jnp.int32).reshape(1)
    gathered = exchange(payload, ("gx", "gy"))
    gathered = exchange(middle(spot, gathered, image, depth), "gz")
    answer, left = finish(
        spot, gathered, image, second, first, right_side.reshape(64, LANES)
    )
    return (answer.reshape(8, 8, LANES), left.reshape(8, 8, LANES))


def solution(mesh):
    placed = (P("gx", "gy", "gz"), P(None, "gx", "gy", "gz"), P("gx", "gy", "gz"), P(), P())
    return jax.shard_map(
        on_device,
        mesh=mesh,
        in_specs=placed,
        out_specs=(P("gx", "gy", "gz"), P("gx", "gy", "gz")),
        check_vma=False,
    )
```

profile of v0, /device:TPU:1, one launch (start us, length us, event | category | flops | bytes accessed | tf_op | source)
XLA Modules:
  0.0 196.9 jit_solution(7090159255474930649)
XLA Ops:
  2.4 4.8 %collective-permute-start = (f32[9,8,32]{2,1,0:T(8,128)S(1)}, f32[9,8,32]{2,1,0:T(8,128)S(1)}, u32[]{:S(2)}, u32[]{:S(2)}) collective-permute-start(f32[9,8,32]{2,1,0:T(8,128)S(1)} %get-tuple-element.56), channel_id=1, source_target_pairs={{0,1},{1,2},{2,3},{3,4},{4,5},{5,6},{6,7},{7,8},{8,9},{9,10},{10,1... | collective-permute-start | bytes 27656 | tf_op jit(solution)/shard_map/ppermute | solution.py:22
  14.1 4.8 %collective-permute-start.2 = (f32[2,8,8,128]{3,2,1,0:T(8,128)S(1)}, f32[2,8,8,128]{3,2,1,0:T(8,128)S(1)}, u32[]{:S(2)}, u32[]{:S(2)}) collective-permute-start(f32[2,8,8,128]{3,2,1,0:T(8,128)S(1)} %get-tuple-element.48), channel_id=1, source_target_pairs={{0,96},{96,192},{192,288},{288,384},{384,480},{480,576},{576,672},... | collective-permute-start | bytes 196616 | tf_op jit(solution)/shard_map/ppermute | solution.py:22
  18.9 5.9 %collective-permute-start.3 = (f32[2,8,8,128]{3,2,1,0:T(8,128)S(1)}, f32[2,8,8,128]{3,2,1,0:T(8,128)S(1)}, u32[]{:S(2)}, u32[]{:S(2)}) collective-permute-start(f32[2,8,8,128]{3,2,1,0:T(8,128)S(1)} %get-tuple-element.49), channel_id=1, source_target_pairs={{96,0},{192,96},{288,192},{384,288},{480,384},{576,480},{672,576},... | collective-permute-start | bytes 196616 | tf_op jit(solution)/shard_map/ppermute | solution.py:23
  27.0 4.0 %collective-permute-start.4 = (f32[10,2,8,128]{3,2,1,0:T(8,128)S(1)}, f32[10,2,8,128]{3,2,1,0:T(8,128)S(1)}, u32[]{:S(2)}, u32[]{:S(2)}) collective-permute-start(f32[10,2,8,128]{3,2,1,0:T(8,128)S(1)} %get-tuple-element.45), channel_id=1, source_target_pairs={{0,12},{12,24},{24,36},{36,48},{48,60},{60,72},{72,84},{1,13},{13,... | collective-permute-start | bytes 245768 | tf_op jit(solution)/shard_map/ppermute | solution.py:22
  33.3 4.2 %block_solve_first.1 = (f32[10,10,8,128]{3,2,1,0:T(8,128)}, f32[1,128]{1,0:T(1,128)}) custom-call(f32[10,8,8,128]{3,2,1,0:T(8,128)} %copy-done, f32[10,2,8,128]{3,2,1,0:T(8,128)} %copy-done.7, f32[10,2,8,128]{3,2,1,0:T(8,128)} %copy-done.5, f32[330,128]{1,0:T(8,128)} %fusion.table, f32[1,128]{1,0:T(1,128)} %and_convert_fusion.valid), custom_call_target="tpu_custom_call" | custom-call | tf_op jit(solution)/shard_map/block_solve_first/pallas_call | solution.py:169
  38.4 3.5 %collective-permute-start.6 = (f32[10,2,8,128]{3,2,1,0:T(8,128)S(1)}, f32[10,2,8,128]{3,2,1,0:T(8,128)S(1)}, u32[]{:S(2)}, u32[]{:S(2)}) collective-permute-start(f32[10,2,8,128]{3,2,1,0:T(8,128)S(1)} %slice.176), channel_id=1, source_target_pairs={{0,12},{12,24},{24,36},{36,48},{48,60},{60,72},{72,84},{1,13},{13,... | collective-permute-start | bytes 245768 | tf_op jit(solution)/shard_map/ppermute | solution.py:22
  45.8 3.6 %collective-permute-start.10 = (f32[4,8,8,32]{3,2,1,0:T(8,128)S(1)}, f32[4,8,8,32]{3,2,1,0:T(8,128)S(1)}, u32[]{:S(2)}, u32[]{:S(2)}) collective-permute-start(f32[4,8,8,32]{3,2,1,0:T(8,128)S(1)} %get-tuple-element.50), channel_id=1, source_target_pairs={{0,1},{1,2},{2,3},{3,4},{4,5},{5,6},{6,7},{7,8},{8,9},{9,10},{10,1... | collective-permute-start | bytes 98312 | tf_op jit(solution)/shard_map/ppermute | solution.py:22
  53.4 3.9 %collective-permute-start.9 = (f32[2,8,8,128]{3,2,1,0:T(8,128)}, f32[2,8,8,128]{3,2,1,0:T(8,128)S(1)}, u32[]{:S(2)}, u32[]{:S(2)}) collective-permute-start(f32[2,8,8,128]{3,2,1,0:T(8,128)} %get-tuple-element.42), channel_id=1, source_target_pairs={{96,0},{192,96},{288,192},{384,288},{480,384},{576,480},{672,576},... | collective-permute-start | bytes 196616 | tf_op jit(solution)/shard_map/ppermute | solution.py:23
  57.3 2.2 %collective-permute-start.8 = (f32[2,8,8,128]{3,2,1,0:T(8,128)}, f32[2,8,8,128]{3,2,1,0:T(8,128)}, u32[]{:S(2)}, u32[]{:S(2)}) collective-permute-start(f32[2,8,8,128]{3,2,1,0:T(8,128)} %get-tuple-element.43), channel_id=1, source_target_pairs={{0,96},{96,192},{192,288},{288,384},{384,480},{480,576},{576,672},... | collective-permute-start | bytes 196616 | tf_op jit(solution)/shard_map/ppermute | solution.py:22
  60.3 2.0 %reshape.92 = f32[4,8,8,24,8]{4,3,2,1,0:T(8,128)S(1)} reshape(f32[4,8,8,192]{3,2,1,0:T(8,128)} %pad_maximum_fusion.3) | data formatting | bytes 393216 | tf_op jit(solution)/shard_map/reshape | solution.py:419
  62.3 1.9 copy.21
  64.3 2.4 %pad.14.clone = f32[4,8,8,8,128]{4,3,2,1,0:T(8,128)} pad(f32[4,8,8,8,24]{4,3,2,1,0:T(8,128)} %copy.21, f32[]{:T(128)} %constant.2.clone.1), padding=0_0x0_0x0_0x0_0x0_104 | pad | bytes 1245188 | tf_op jit(solution)/shard_map/jit(_pad)/pad | solution.py:421
  67.3 3.1 %first_operator.1 = (f32[512,128]{1,0:T(8,128)}, f32[512,128]{1,0:T(8,128)}, f32[1,128]{1,0:T(1,128)}) custom-call(f32[10,8,8,128]{3,2,1,0:T(8,128)} %copy-done.1, f32[2,8,8,128]{3,2,1,0:T(8,128)} %collective-permute-done.8.low, f32[2,8,8,128]{3,2,1,0:T(8,128)} %copy-done.9, f32[2048,128]{1,0:T(8,128)} %bitcast.45), custom_call_target="tpu_custom_call" | custom-call | tf_op jit(solution)/shard_map/first_operator/pallas_call | solution.py:258
  71.2 2.6 %collective-permute-start.12 = (f32[2,8,8,128]{3,2,1,0:T(8,128)S(1)}, f32[2,8,8,128]{3,2,1,0:T(8,128)S(1)}, u32[]{:S(2)}, u32[]{:S(2)}) collective-permute-start(f32[2,8,8,128]{3,2,1,0:T(8,128)S(1)} %bitcast.53), channel_id=1, source_target_pairs={{0,96},{96,192},{192,288},{288,384},{384,480},{480,576},{576,672},... | collective-permute-start | bytes 196616 | tf_op jit(solution)/shard_map/ppermute | solution.py:22
  74.7 1.9 collective-permute-start.13
  77.5 2.8 %collective-permute-done.13 = f32[2,8,8,128]{3,2,1,0:T(8,128)S(1)} collective-permute-done((f32[2,8,8,128]{3,2,1,0:T(8,128)S(1)}, f32[2,8,8,128]{3,2,1,0:T(8,128)S(1)}, u32[]{:S(2)}, u32[]{:S(2)}) %collective-permute-start.13) | collective-permute-done | bytes 65568 | tf_op jit(solution)/shard_map/ppermute | solution.py:23
  82.4 5.3 %collective-permute-start.14 = (f32[10,2,8,128]{3,2,1,0:T(8,128)S(1)}, f32[10,2,8,128]{3,2,1,0:T(8,128)S(1)}, u32[]{:S(2)}, u32[]{:S(2)}) collective-permute-start(f32[10,2,8,128]{3,2,1,0:T(8,128)S(1)} %get-tuple-element.41), channel_id=1, source_target_pairs={{0,12},{12,24},{24,36},{36,48},{48,60},{60,72},{72,84},{1,13},{13,... | collective-permute-start | bytes 245768 | tf_op jit(solution)/shard_map/ppermute | solution.py:22
  89.8 4.3 %block_solve_shared.1 = (f32[10,10,8,128]{3,2,1,0:T(8,128)}, f32[1,128]{1,0:T(1,128)}, f32[1,128]{1,0:T(1,128)}, f32[512,128]{1,0:T(8,128)}) custom-call(f32[10,8,8,128]{3,2,1,0:T(8,128)} %copy-done.4, f32[10,2,8,128]{3,2,1,0:T(8,128)} %copy-done.8, f32[10,2,8,128]{3,2,1,0:T(8,128)} %copy-done.6, f32[330,128]{1,0:T(8,128)} %fusion.table, ...), custom_call_target="tpu_custom_call" | custom-call | tf_op jit(solution)/shard_map/block_solve_shared/pallas_call | solution.py:169
  95.0 3.7 %collective-permute-start.16 = (f32[10,2,8,128]{3,2,1,0:T(8,128)S(1)}, f32[10,2,8,128]{3,2,1,0:T(8,128)S(1)}, u32[]{:S(2)}, u32[]{:S(2)}) collective-permute-start(f32[10,2,8,128]{3,2,1,0:T(8,128)S(1)} %slice.201), channel_id=1, source_target_pairs={{0,12},{12,24},{24,36},{36,48},{48,60},{60,72},{72,84},{1,13},{13,... | collective-permute-start | bytes 245768 | tf_op jit(solution)/shard_map/ppermute | solution.py:22
  103.4 4.3 %collective-permute-done.17 = f32[10,2,8,128]{3,2,1,0:T(8,128)S(1)} collective-permute-done((f32[10,2,8,128]{3,2,1,0:T(8,128)S(1)}, f32[10,2,8,128]{3,2,1,0:T(8,128)S(1)}, u32[]{:S(2)}, u32[]{:S(2)}) %collective-permute-start.17) | collective-permute-done | bytes 81952 | tf_op jit(solution)/shard_map/ppermute | solution.py:23
  108.7 2.3 %collective-permute-start.19 = (f32[2,8,8,128]{3,2,1,0:T(8,128)S(1)}, f32[2,8,8,128]{3,2,1,0:T(8,128)S(1)}, u32[]{:S(2)}, u32[]{:S(2)}) collective-permute-start(f32[2,8,8,128]{3,2,1,0:T(8,128)S(1)} %get-tuple-element.38), channel_id=1, source_target_pairs={{96,0},{192,96},{288,192},{384,288},{480,384},{576,480},{672,576},... | collective-permute-start | bytes 196616 | tf_op jit(solution)/shard_map/ppermute | solution.py:23
  111.0 4.7 %collective-permute-start.18 = (f32[2,8,8,128]{3,2,1,0:T(8,128)S(1)}, f32[2,8,8,128]{3,2,1,0:T(8,128)S(1)}, u32[]{:S(2)}, u32[]{:S(2)}) collective-permute-start(f32[2,8,8,128]{3,2,1,0:T(8,128)S(1)} %get-tuple-element.39), channel_id=1, source_target_pairs={{0,96},{96,192},{192,288},{288,384},{384,480},{480,576},{576,672},... | collective-permute-start | bytes 196616 | tf_op jit(solution)/shard_map/ppermute | solution.py:22
  117.7 3.2 %second_operator.1 = (f32[128,128]{1,0:T(8,128)}, f32[64,128]{1,0:T(8,128)}) custom-call(f32[10,8,8,128]{3,2,1,0:T(8,128)} %copy-done.2, f32[2,8,8,128]{3,2,1,0:T(8,128)} %copy-done.11, f32[2,8,8,128]{3,2,1,0:T(8,128)} %copy-done.10, f32[2048,128]{1,0:T(8,128)} %bitcast.46, f32[1,128]{1,0:T(1,128)} %get-tuple-element.20.rho, f32[1,128]{1,0:T(1,128)} %get-tuple-element.21.d, ...), custom_call_target="tpu_custom_call" | custom-call | tf_op jit(solution)/shard_map/second_operator/pallas_call | solution.py:290
  121.6 4.3 %collective-permute-start.20 = (f32[1,8,128]{2,1,0:T(8,128)S(1)}, f32[1,8,128]{2,1,0:T(8,128)S(1)}, u32[]{:S(2)}, u32[]{:S(2)}) collective-permute-start(f32[1,8,128]{2,1,0:T(8,128)S(1)} %get-tuple-element.54), channel_id=1, source_target_pairs={{0,96},{96,192},{192,288},{288,384},{384,480},{480,576},{576,672},... | collective-permute-start | bytes 12296 | tf_op jit(solution)/shard_map/ppermute | solution.py:22
  128.5 2.3 %collective-permute-done.21 = f32[1,8,128]{2,1,0:T(8,128)S(1)} collective-permute-done((f32[1,8,128]{2,1,0:T(8,128)S(1)}, f32[1,8,128]{2,1,0:T(8,128)S(1)}, u32[]{:S(2)}, u32[]{:S(2)}) %collective-permute-start.21) | collective-permute-done | bytes 4128 | tf_op jit(solution)/shard_map/ppermute | solution.py:23
  131.5 5.2 %collective-permute-start.22 = (f32[8,1,128]{2,1,0:T(1,128)S(1)}, f32[8,1,128]{2,1,0:T(1,128)S(1)}, u32[]{:S(2)}, u32[]{:S(2)}) collective-permute-start(f32[8,1,128]{2,1,0:T(1,128)S(1)} %pad_maximum_fusion.6), channel_id=1, source_target_pairs={{0,12},{12,24},{24,36},{36,48},{48,60},{60,72},{72,84},{1,13},{13,... | collective-permute-start | bytes 12296 | tf_op jit(solution)/shard_map/ppermute | solution.py:22
  138.8 4.3 %collective-permute-done.23 = f32[8,1,128]{2,1,0:T(1,128)S(1)} collective-permute-done((f32[8,1,128]{2,1,0:T(1,128)S(1)}, f32[8,1,128]{2,1,0:T(1,128)S(1)}, u32[]{:S(2)}, u32[]{:S(2)}) %collective-permute-start.23) | collective-permute-done | bytes 4128 | tf_op jit(solution)/shard_map/ppermute | solution.py:23
  143.7 23.8 %all_to_all.22 = f32[64,1,128]{2,1,0:T(1,128)} all-to-all(f32[64,1,128]{2,1,0:T(1,128)} %bitcast.56), channel_id=1, replica_groups=mesh['gx'=8,'gy'=8,'gz'=12] {'gx','gy'}, dimensions={0} | all-to-all | bytes 65536 | tf_op jit(solution)/shard_map/all_to_all | solution.py:407
  170.6 14.9 %all-to-all-start.1 = ((f32[12,1,128]{2,1,0:T(1,128)}), f32[12,1,128]{2,1,0:T(1,128)S(1)}, u32[]{:S(2)}, u32[]{:S(2)}) async-start(f32[12,1,128]{2,1,0:T(1,128)} %copy.19), calls=%async_computation.1 | async-start | bytes 12288 | tf_op jit(solution)/shard_map/all_to_all | solution.py:407
  185.5 2.0 %as_lines.1.first = f32[128,128]{1,0:T(8,128)} custom-call(f32[512,128]{1,0:T(8,128)} %get-tuple-element.28.one, f32[512,128]{1,0:T(8,128)} %get-tuple-element.29.two), custom_call_target="tpu_custom_call" | custom-call | tf_op jit(solution)/shard_map/as_lines/pallas_call | solution.py:306
  187.6 6.8 %all-to-all-done.1 = f32[12,1,128]{2,1,0:T(1,128)S(1)} async-done(((f32[12,1,128]{2,1,0:T(1,128)}), f32[12,1,128]{2,1,0:T(1,128)S(1)}, u32[]{:S(2)}, u32[]{:S(2)}) %all-to-all-start.1) | async-done | bytes 6176 | tf_op jit(solution)/shard_map/all_to_all | solution.py:407
  195.0 1.9 finish.1
  (110 shorter events, 48.6 us)
Async XLA Ops:
  2.4 8.6 %collective-permute-start = (f32[9,8,32]{2,1,0:T(8,128)S(1)}, f32[9,8,32]{2,1,0:T(8,128)S(1)}, u32[]{:S(2)}, u32[]{:S(2)}) collective-permute-start(f32[9,8,32]{2,1,0:T(8,128)S(1)} %get-tuple-element.56), channel_id=1, source_target_pairs={{0,1},{1,2},{2,3},{3,4},{4,5},{5,6},{6,7},{7,8},{8,9},{9,10},{10,1... | collective-permute-start | bytes 27656 | tf_op jit(solution)/shard_map/ppermute | solution.py:22
  7.2 5.3 %collective-permute-start.1 = (f32[9,8,32]{2,1,0:T(8,128)S(1)}, f32[9,8,32]{2,1,0:T(8,128)S(1)}, u32[]{:S(2)}, u32[]{:S(2)}) collective-permute-start(f32[9,8,32]{2,1,0:T(8,128)S(1)} %get-tuple-element.57), channel_id=1, source_target_pairs={{1,0},{2,1},{3,2},{4,3},{5,4},{6,5},{7,6},{8,7},{9,8},{10,9},{11,1... | collective-permute-start | bytes 27656 | tf_op jit(solution)/shard_map/ppermute | solution.py:23
  10.8 34.9 %copy-start.3 = (f32[4,8,8,128]{3,2,1,0:T(8,128)S(1)}, f32[4,8,8,128]{3,2,1,0:T(8,128)}, u32[]{:S(2)}) copy-start(f32[4,8,8,128]{3,2,1,0:T(8,128)} %param.6) | copy-start | bytes 393220
  14.1 10.8 %collective-permute-start.2 = (f32[2,8,8,128]{3,2,1,0:T(8,128)S(1)}, f32[2,8,8,128]{3,2,1,0:T(8,128)S(1)}, u32[]{:S(2)}, u32[]{:S(2)}) collective-permute-start(f32[2,8,8,128]{3,2,1,0:T(8,128)S(1)} %get-tuple-element.48), channel_id=1, source_target_pairs={{0,96},{96,192},{192,288},{288,384},{384,480},{480,576},{576,672},... | collective-permute-start | bytes 196616 | tf_op jit(solution)/shard_map/ppermute | solution.py:22
  18.9 6.7 %collective-permute-start.3 = (f32[2,8,8,128]{3,2,1,0:T(8,128)S(1)}, f32[2,8,8,128]{3,2,1,0:T(8,128)S(1)}, u32[]{:S(2)}, u32[]{:S(2)}) collective-permute-start(f32[2,8,8,128]{3,2,1,0:T(8,128)S(1)} %get-tuple-element.49), channel_id=1, source_target_pairs={{96,0},{192,96},{288,192},{384,288},{480,384},{576,480},{672,576},... | collective-permute-start | bytes 196616 | tf_op jit(solution)/shard_map/ppermute | solution.py:23
  25.7 6.8 %copy-start = (f32[10,8,8,128]{3,2,1,0:T(8,128)}, f32[10,8,8,128]{3,2,1,0:T(8,128)S(1)}, u32[]{:S(2)}) copy-start(f32[10,8,8,128]{3,2,1,0:T(8,128)S(1)} %pad_maximum_fusion.field) | copy-start | bytes 983044
  25.7 6.3 %collective-permute-start.5 = (f32[10,2,8,128]{3,2,1,0:T(8,128)S(1)}, f32[10,2,8,128]{3,2,1,0:T(8,128)S(1)}, u32[]{:S(2)}, u32[]{:S(2)}) collective-permute-start(f32[10,2,8,128]{3,2,1,0:T(8,128)S(1)} %get-tuple-element.44), channel_id=1, source_target_pairs={{12,0},{24,12},{36,24},{48,36},{60,48},{72,60},{84,72},{13,1},{25,... | collective-permute-start | bytes 245768 | tf_op jit(solution)/shard_map/ppermute | solution.py:23
  27.0 5.5 %collective-permute-start.4 = (f32[10,2,8,128]{3,2,1,0:T(8,128)S(1)}, f32[10,2,8,128]{3,2,1,0:T(8,128)S(1)}, u32[]{:S(2)}, u32[]{:S(2)}) collective-permute-start(f32[10,2,8,128]{3,2,1,0:T(8,128)S(1)} %get-tuple-element.45), channel_id=1, source_target_pairs={{0,12},{12,24},{24,36},{36,48},{48,60},{60,72},{72,84},{1,13},{13,... | collective-permute-start | bytes 245768 | tf_op jit(solution)/shard_map/ppermute | solution.py:22
  38.4 5.0 %collective-permute-start.6 = (f32[10,2,8,128]{3,2,1,0:T(8,128)S(1)}, f32[10,2,8,128]{3,2,1,0:T(8,128)S(1)}, u32[]{:S(2)}, u32[]{:S(2)}) collective-permute-start(f32[10,2,8,128]{3,2,1,0:T(8,128)S(1)} %slice.176), channel_id=1, source_target_pairs={{0,12},{12,24},{24,36},{36,48},{48,60},{60,72},{72,84},{1,13},{13,... | collective-permute-start | bytes 245768 | tf_op jit(solution)/shard_map/ppermute | solution.py:22
  44.4 7.3 %collective-permute-start.7 = (f32[10,2,8,128]{3,2,1,0:T(8,128)S(1)}, f32[10,2,8,128]{3,2,1,0:T(8,128)S(1)}, u32[]{:S(2)}, u32[]{:S(2)}) collective-permute-start(f32[10,2,8,128]{3,2,1,0:T(8,128)S(1)} %get-tuple-element.37), channel_id=1, source_target_pairs={{12,0},{24,12},{36,24},{48,36},{60,48},{72,60},{84,72},{13,1},{25,... | collective-permute-start | bytes 245768 | tf_op jit(solution)/shard_map/ppermute | solution.py:23
  45.8 13.7 %collective-permute-start.10 = (f32[4,8,8,32]{3,2,1,0:T(8,128)S(1)}, f32[4,8,8,32]{3,2,1,0:T(8,128)S(1)}, u32[]{:S(2)}, u32[]{:S(2)}) collective-permute-start(f32[4,8,8,32]{3,2,1,0:T(8,128)S(1)} %get-tuple-element.50), channel_id=1, source_target_pairs={{0,1},{1,2},{2,3},{3,4},{4,5},{5,6},{6,7},{7,8},{8,9},{9,10},{10,1... | collective-permute-start | bytes 98312 | tf_op jit(solution)/shard_map/ppermute | solution.py:22
  49.4 10.0 %collective-permute-start.11 = (f32[4,8,8,32]{3,2,1,0:T(8,128)S(1)}, f32[4,8,8,32]{3,2,1,0:T(8,128)S(1)}, u32[]{:S(2)}, u32[]{:S(2)}) collective-permute-start(f32[4,8,8,32]{3,2,1,0:T(8,128)S(1)} %get-tuple-element.51), channel_id=1, source_target_pairs={{1,0},{2,1},{3,2},{4,3},{5,4},{6,5},{7,6},{8,7},{9,8},{10,9},{11,1... | collective-permute-start | bytes 98312 | tf_op jit(solution)/shard_map/ppermute | solution.py:23
  52.6 11.7 %copy-start.1 = (f32[10,8,8,128]{3,2,1,0:T(8,128)}, f32[10,8,8,128]{3,2,1,0:T(8,128)S(1)}, u32[]{:S(2)}) copy-start(f32[10,8,8,128]{3,2,1,0:T(8,128)S(1)} %pad_maximum_fusion.1.folded) | copy-start | bytes 983044
  53.4 13.3 %collective-permute-start.9 = (f32[2,8,8,128]{3,2,1,0:T(8,128)}, f32[2,8,8,128]{3,2,1,0:T(8,128)S(1)}, u32[]{:S(2)}, u32[]{:S(2)}) collective-permute-start(f32[2,8,8,128]{3,2,1,0:T(8,128)} %get-tuple-element.42), channel_id=1, source_target_pairs={{96,0},{192,96},{288,192},{384,288},{480,384},{576,480},{672,576},... | collective-permute-start | bytes 196616 | tf_op jit(solution)/shard_map/ppermute | solution.py:23
  57.3 9.4 %collective-permute-start.8 = (f32[2,8,8,128]{3,2,1,0:T(8,128)}, f32[2,8,8,128]{3,2,1,0:T(8,128)}, u32[]{:S(2)}, u32[]{:S(2)}) collective-permute-start(f32[2,8,8,128]{3,2,1,0:T(8,128)} %get-tuple-element.43), channel_id=1, source_target_pairs={{0,96},{96,192},{192,288},{288,384},{384,480},{480,576},{576,672},... | collective-permute-start | bytes 196616 | tf_op jit(solution)/shard_map/ppermute | solution.py:22
  71.2 5.5 %collective-permute-start.12 = (f32[2,8,8,128]{3,2,1,0:T(8,128)S(1)}, f32[2,8,8,128]{3,2,1,0:T(8,128)S(1)}, u32[]{:S(2)}, u32[]{:S(2)}) collective-permute-start(f32[2,8,8,128]{3,2,1,0:T(8,128)S(1)} %bitcast.53), channel_id=1, source_target_pairs={{0,96},{96,192},{192,288},{288,384},{384,480},{480,576},{576,672},... | collective-permute-start | bytes 196616 | tf_op jit(solution)/shard_map/ppermute | solution.py:22
  74.7 5.6 %collective-permute-start.13 = (f32[2,8,8,128]{3,2,1,0:T(8,128)S(1)}, f32[2,8,8,128]{3,2,1,0:T(8,128)S(1)}, u32[]{:S(2)}, u32[]{:S(2)}) collective-permute-start(f32[2,8,8,128]{3,2,1,0:T(8,128)S(1)} %bitcast.52), channel_id=1, source_target_pairs={{96,0},{192,96},{288,192},{384,288},{480,384},{576,480},{672,576},... | collective-permute-start | bytes 196616 | tf_op jit(solution)/shard_map/ppermute | solution.py:23
  81.1 8.1 %copy-start.4 = (f32[10,8,8,128]{3,2,1,0:T(8,128)}, f32[10,8,8,128]{3,2,1,0:T(8,128)S(1)}, u32[]{:S(2)}) copy-start(f32[10,8,8,128]{3,2,1,0:T(8,128)S(1)} %slice_dynamic-update-slice_fusion.field) | copy-start | bytes 983044
  81.1 6.6 %collective-permute-start.15 = (f32[10,2,8,128]{3,2,1,0:T(8,128)S(1)}, f32[10,2,8,128]{3,2,1,0:T(8,128)S(1)}, u32[]{:S(2)}, u32[]{:S(2)}) collective-permute-start(f32[10,2,8,128]{3,2,1,0:T(8,128)S(1)} %get-tuple-element.40), channel_id=1, source_target_pairs={{12,0},{24,12},{36,24},{48,36},{60,48},{72,60},{84,72},{13,1},{25,... | collective-permute-start | bytes 245768 | tf_op jit(solution)/shard_map/ppermute | solution.py:23
  82.4 6.8 %collective-permute-start.14 = (f32[10,2,8,128]{3,2,1,0:T(8,128)S(1)}, f32[10,2,8,128]{3,2,1,0:T(8,128)S(1)}, u32[]{:S(2)}, u32[]{:S(2)}) collective-permute-start(f32[10,2,8,128]{3,2,1,0:T(8,128)S(1)} %get-tuple-element.41), channel_id=1, source_target_pairs={{0,12},{12,24},{24,36},{36,48},{48,60},{60,72},{72,84},{1,13},{13,... | collective-permute-start | bytes 245768 | tf_op jit(solution)/shard_map/ppermute | solution.py:22
  87.7 1.5 copy-start.6
  95.0 5.2 %collective-permute-start.16 = (f32[10,2,8,128]{3,2,1,0:T(8,128)S(1)}, f32[10,2,8,128]{3,2,1,0:T(8,128)S(1)}, u32[]{:S(2)}, u32[]{:S(2)}) collective-permute-start(f32[10,2,8,128]{3,2,1,0:T(8,128)S(1)} %slice.201), channel_id=1, source_target_pairs={{0,12},{12,24},{24,36},{36,48},{48,60},{60,72},{72,84},{1,13},{13,... | collective-permute-start | bytes 245768 | tf_op jit(solution)/shard_map/ppermute | solution.py:22
  101.2 6.6 %collective-permute-start.17 = (f32[10,2,8,128]{3,2,1,0:T(8,128)S(1)}, f32[10,2,8,128]{3,2,1,0:T(8,128)S(1)}, u32[]{:S(2)}, u32[]{:S(2)}) collective-permute-start(f32[10,2,8,128]{3,2,1,0:T(8,128)S(1)} %get-tuple-element.35), channel_id=1, source_target_pairs={{12,0},{24,12},{36,24},{48,36},{60,48},{72,60},{84,72},{13,1},{25,... | collective-permute-start | bytes 245768 | tf_op jit(solution)/shard_map/ppermute | solution.py:23
  108.7 8.4 %copy-start.2 = (f32[10,8,8,128]{3,2,1,0:T(8,128)}, f32[10,8,8,128]{3,2,1,0:T(8,128)S(1)}, u32[]{:S(2)}) copy-start(f32[10,8,8,128]{3,2,1,0:T(8,128)S(1)} %pad_maximum_fusion.2.folded) | copy-start | bytes 983044
  108.7 7.0 %collective-permute-start.19 = (f32[2,8,8,128]{3,2,1,0:T(8,128)S(1)}, f32[2,8,8,128]{3,2,1,0:T(8,128)S(1)}, u32[]{:S(2)}, u32[]{:S(2)}) collective-permute-start(f32[2,8,8,128]{3,2,1,0:T(8,128)S(1)} %get-tuple-element.38), channel_id=1, source_target_pairs={{96,0},{192,96},{288,192},{384,288},{480,384},{576,480},{672,576},... | collective-permute-start | bytes 196616 | tf_op jit(solution)/shard_map/ppermute | solution.py:23
  111.0 6.1 %collective-permute-start.18 = (f32[2,8,8,128]{3,2,1,0:T(8,128)S(1)}, f32[2,8,8,128]{3,2,1,0:T(8,128)S(1)}, u32[]{:S(2)}, u32[]{:S(2)}) collective-permute-start(f32[2,8,8,128]{3,2,1,0:T(8,128)S(1)} %get-tuple-element.39), channel_id=1, source_target_pairs={{0,96},{96,192},{192,288},{288,384},{384,480},{480,576},{576,672},... | collective-permute-start | bytes 196616 | tf_op jit(solution)/shard_map/ppermute | solution.py:22
  115.8 1.3 copy-start.10
  121.6 6.9 %collective-permute-start.20 = (f32[1,8,128]{2,1,0:T(8,128)S(1)}, f32[1,8,128]{2,1,0:T(8,128)S(1)}, u32[]{:S(2)}, u32[]{:S(2)}) collective-permute-start(f32[1,8,128]{2,1,0:T(8,128)S(1)} %get-tuple-element.54), channel_id=1, source_target_pairs={{0,96},{96,192},{192,288},{288,384},{384,480},{480,576},{576,672},... | collective-permute-start | bytes 12296 | tf_op jit(solution)/shard_map/ppermute | solution.py:22
  125.9 4.9 %collective-permute-start.21 = (f32[1,8,128]{2,1,0:T(8,128)S(1)}, f32[1,8,128]{2,1,0:T(8,128)S(1)}, u32[]{:S(2)}, u32[]{:S(2)}) collective-permute-start(f32[1,8,128]{2,1,0:T(8,128)S(1)} %get-tuple-element.55), channel_id=1, source_target_pairs={{96,0},{192,96},{288,192},{384,288},{480,384},{576,480},{672,576},... | collective-permute-start | bytes 12296 | tf_op jit(solution)/shard_map/ppermute | solution.py:23
  131.5 6.0 %collective-permute-start.22 = (f32[8,1,128]{2,1,0:T(1,128)S(1)}, f32[8,1,128]{2,1,0:T(1,128)S(1)}, u32[]{:S(2)}, u32[]{:S(2)}) collective-permute-start(f32[8,1,128]{2,1,0:T(1,128)S(1)} %pad_maximum_fusion.6), channel_id=1, source_target_pairs={{0,12},{12,24},{24,36},{36,48},{48,60},{60,72},{72,84},{1,13},{13,... | collective-permute-start | bytes 12296 | tf_op jit(solution)/shard_map/ppermute | solution.py:22
  137.5 5.6 %collective-permute-start.23 = (f32[8,1,128]{2,1,0:T(1,128)S(1)}, f32[8,1,128]{2,1,0:T(1,128)S(1)}, u32[]{:S(2)}, u32[]{:S(2)}) collective-permute-start(f32[8,1,128]{2,1,0:T(1,128)S(1)} %get-tuple-element.33), channel_id=1, source_target_pairs={{12,0},{24,12},{36,24},{48,36},{60,48},{72,60},{84,72},{13,1},{25,... | collective-permute-start | bytes 12296 | tf_op jit(solution)/shard_map/ppermute | solution.py:23
  170.6 23.8 %all-to-all-start.1 = ((f32[12,1,128]{2,1,0:T(1,128)}), f32[12,1,128]{2,1,0:T(1,128)S(1)}, u32[]{:S(2)}, u32[]{:S(2)}) async-start(f32[12,1,128]{2,1,0:T(1,128)} %copy.19), calls=%async_computation.1 | async-start | bytes 12288 | tf_op jit(solution)/shard_map/all_to_all | solution.py:407
  (5 other events, 3.1 us)
where the time goes:
time: 199 us; the launch traced here: 197 us
  starting transfers between devices  88.7 us (45%)
  waiting for transfers between devices  29.8 us (15%)
  blocking collectives  23.8 us (12%)
  local copies, waits for them, and re-layouts  21.4 us (11%)
  Pallas kernels  20.5 us (10%)
  other arithmetic  10.5 us (5%)
    ppermute x12, starting transfers between devices, swap_ends(): lax.ppermute(lax.slice_in_dim(block, length - width, length, axis=dim), a...  48.8 us
    ppermute x12, starting transfers between devices, swap_ends(): lax.ppermute(lax.slice_in_dim(block, 0, width, axis=dim), axis, backward)  24.9 us
    all_to_all x1, blocking collectives, exchange(): return lax.all_to_all(rows, axes, 0, 0, tiled=True)  23.8 us
    ppermute x12, waiting for transfers between devices, swap_ends(): lax.ppermute(lax.slice_in_dim(block, 0, width, axis=dim), axis, backward)  16.2 us
    all_to_all x1, starting transfers between devices, exchange(): return lax.all_to_all(rows, axes, 0, 0, tiled=True)  14.9 us
    pallas_call x2, Pallas kernels, block_solve(): pl.pallas_call(functools.partial(solve_kernel, count, shared), out_shape=...  8.5 us
    unnamed x30, local copies, waits for them, and re-layouts  6.94 us
    ppermute x12, waiting for transfers between devices, swap_ends(): lax.ppermute(lax.slice_in_dim(block, length - width, length, axis=dim), a...  6.85 us
  transfers between devices with their start and end apart: 25, of which 13 were waited for; matrix products, arithmetic and copies ran while one was open for 8% of the time, Pallas kernels for 1%

commit v1 on v0

v1 whole, which is shorter than its diff:
```python
import functools

import jax
import jax.numpy as jnp
import numpy as np
from jax import lax
from jax.experimental import pallas as pl
from jax.experimental.pallas import tpu as pltpu
from jax.sharding import PartitionSpec as P

HIGHEST = lax.Precision.HIGHEST
LANES = 128
REACH = 4
CHUNKS = ((0, 24), (24, 24), (48, 24), (72, 28))


def swap(backward_part, forward_part, axis):
    count = lax.axis_size(axis)
    forward = [(i, i + 1) for i in range(count - 1)]
    backward = [(target, source) for source, target in forward]
    return lax.ppermute(forward_part, axis, forward), lax.ppermute(backward_part, axis, backward)


def derivative_table():
    points = np.array(
        [
            -1.0,
            -0.8717401485096066,
            -0.5917001814331423,
            -0.2092992179024789,
            0.2092992179024789,
            0.5917001814331423,
            0.8717401485096066,
            1.0,
        ]
    )
    previous = np.ones(8)
    current = points * 1.0
    for order in range(1, 7):
        following = ((2 * order + 1) * points * current - order * previous) / (order + 1)
        previous = current
        current = following
    spacing = points[:, None] - points[None, :] + np.eye(8)
    off_diagonal = current[:, None] / (current[None, :] * spacing)
    positions = np.arange(8)
    end_values = np.where(positions == 0, -14.0, 0.0) + np.where(positions == 7, 14.0, 0.0)
    return np.where(np.eye(8) > 0, np.eye(8) * end_values[None, :], off_diagonal)


def own_lanes(count):
    lane = lax.broadcasted_iota(jnp.int32, (1, LANES), 1)
    return (lane >= REACH) & (lane < REACH + count)


def solve_step(source, target, table, base, transposed, scale=None):
    for start, size in CHUNKS:
        entries = [source[pl.ds(10 * start + k, size, stride=10), :] for k in range(10)]
        for out in range(10):
            total = None
            for k in range(10):
                row = base + (10 * out + k if transposed else 10 * k + out)
                term = table[row : row + 1, :] * entries[k]
                total = term if total is None else total + term
            if scale is not None:
                total = total / (table[300 + out : 301 + out, :] + scale[start : start + size, :])
            target[pl.ds(100 * out + start, size), :] = total


def extended_first(a, y, field, low, high, shared):
    if a == 0:
        return low[0, y]
    if a == 9:
        return high[1, y]
    nodes = field[pl.ds(64 * (a - 1) + 8 * y, 8), :]
    if shared and a == 1:
        nodes = nodes + low[1, y]
    if shared and a == 8:
        nodes = nodes + high[0, y]
    return nodes


def second_edges_kernel(shared, field, low, high, backward, forward):
    for a in range(10):
        for y in range(2):
            backward[a, y] = extended_first(a, y, field, low, high, shared)
            forward[a, y] = extended_first(a, 6 + y, field, low, high, shared)


def second_edges(field, low, high, shared):
    return pl.pallas_call(
        functools.partial(second_edges_kernel, shared),
        out_shape=[jax.ShapeDtypeStruct((10, 2, 8, LANES), jnp.float32)] * 2,
        name="second_edges",
    )(field, low, high)


def solve_kernel(count, shared, field, low, high, below, above, table, valid, *refs):
    if shared:
        folded, rims, backward, forward, inner, size_row, assembled, blocks, left, right, pair = refs
    else:
        folded, rims, backward, forward, inner, blocks, left, right, pair = refs
    blocks[pl.ds(1000, 40), :] = jnp.zeros((40, LANES), jnp.float32)
    left[pl.ds(1000, 40), :] = jnp.zeros((40, LANES), jnp.float32)
    right[pl.ds(1000, 40), :] = jnp.zeros((40, LANES), jnp.float32)
    for a in range(10):
        for b in range(10):
            if b == 0:
                nodes = below[a, 0]
            elif b == 9:
                nodes = above[a, 1]
            else:
                nodes = extended_first(a, b - 1, field, low, high, shared)
                if shared and b == 1:
                    nodes = nodes + below[a, 1]
                if shared and b == 8:
                    nodes = nodes + above[a, 0]
                if shared and 1 <= a <= 8:
                    assembled[pl.ds(64 * (a - 1) + 8 * (b - 1), 8), :] = nodes
            blocks[pl.ds(100 * a + 10 * b + 1, 8), :] = nodes
    blocks[pl.ds(0, 100, stride=10), :] = pltpu.roll(
        blocks[pl.ds(7, 100, stride=10), :], 1, 1
    )
    blocks[pl.ds(9, 100, stride=10), :] = pltpu.roll(
        blocks[pl.ds(2, 100, stride=10), :], LANES - 1, 1
    )
    for n in range(10):
        pair[pl.ds(10 * n, 10), :] = table[310 + n : 311 + n, :] + table[320:330, :]
    solve_step(blocks, left, table, 200, False)
    solve_step(left, right, table, 100, False)
    solve_step(right, left, table, 0, False, pair)
    solve_step(left, right, table, 200, True)
    solve_step(right, left, table, 100, True)
    solve_step(left, right, table, 0, True)
    exists = valid[...] > 0.0
    own = own_lanes(count)
    unit = 1.0
    if shared:
        largest = jnp.zeros((8, LANES), jnp.float32)
        for row in range(0, 1000, 8):
            largest = jnp.maximum(largest, jnp.abs(blocks[row : row + 8, :]))
        size = jnp.max(jnp.where(own, largest, 0.0))
        unit = 1.0 / jnp.where(size > 0.0, size, 1.0)
        size_row[...] = jnp.full((1, LANES), size, jnp.float32)
    total = jnp.zeros((8, LANES), jnp.float32)
    for row in range(0, 1000, 8):
        total = total + (blocks[row : row + 8, :] * unit) * (right[row : row + 8, :] * unit)
    inner[...] = jnp.sum(jnp.where(own, total, 0.0), axis=0, keepdims=True)

    def entry(c):
        return jnp.where(exists, right[pl.ds(c, 100, stride=10), :], 0.0)

    first, second, second_last, last = entry(0), entry(1), entry(8), entry(9)
    right[pl.ds(1, 100, stride=10), :] = second + pltpu.roll(second_last, 1, 1)
    right[pl.ds(2, 100, stride=10), :] = entry(2) + pltpu.roll(last, 1, 1)
    right[pl.ds(7, 100, stride=10), :] = entry(7) + pltpu.roll(first, LANES - 1, 1)
    right[pl.ds(8, 100, stride=10), :] = second_last + pltpu.roll(second, LANES - 1, 1)
    for a in range(10):
        for b in range(10):
            nodes = right[pl.ds(100 * a + 10 * b + 1, 8), :]
            folded[a, b] = nodes
            if b < 2:
                backward[a, b] = nodes
            if b > 7:
                forward[a, b - 8] = nodes
            if a < 2:
                rims[a, b] = nodes
            if a > 7:
                rims[a - 6, b] = nodes


def block_solve(field, low, high, below, above, table, valid, count, shared):
    row = jax.ShapeDtypeStruct((1, LANES), jnp.float32)
    edge = jax.ShapeDtypeStruct((10, 2, 8, LANES), jnp.float32)
    outs = [
        jax.ShapeDtypeStruct((10, 10, 8, LANES), jnp.float32),
        jax.ShapeDtypeStruct((4, 10, 8, LANES), jnp.float32),
        edge,
        edge,
        row,
    ]
    if shared:
        outs += [row, jax.ShapeDtypeStruct((512, LANES), jnp.float32)]
    return pl.pallas_call(
        functools.partial(solve_kernel, count, shared),
        out_shape=outs,
        scratch_shapes=[pltpu.VMEM((1040, LANES), jnp.float32)] * 3
        + [pltpu.VMEM((104, LANES), jnp.float32)],
        name="block_solve_shared" if shared else "block_solve_first",
    )(field, low, high, below, above, table, valid)


def folded_second(values, a, y, at, below, above):
    nodes = values[a, y + 1]
    if y < 2:
        nodes = nodes + below[at, y]
    if y > 5:
        nodes = nodes + above[at, y - 6]
    return nodes


def first_edges_kernel(rims, below, above, backward, forward):
    for a in range(2):
        for y in range(8):
            backward[a, y] = folded_second(rims, a, y, a, below, above)
            forward[a, y] = folded_second(rims, a + 2, y, a + 8, below, above)


def first_edges(rims, below, above):
    return pl.pallas_call(
        first_edges_kernel,
        out_shape=[jax.ShapeDtypeStruct((2, 8, 8, LANES), jnp.float32)] * 2,
        name="first_edges",
    )(rims, below, above)


def both_ways(nodes, metric, derivative):
    slopes = []
    for a in range(8):
        total = None
        for i in range(8):
            if derivative[a, i] != 0.0:
                term = float(derivative[a, i]) * nodes[i]
                total = term if total is None else total + term
        slopes.append(metric[a] * total)
    outs = []
    for i in range(8):
        total = None
        for a in range(8):
            if derivative[a, i] != 0.0:
                term = float(derivative[a, i]) * slopes[a]
                total = term if total is None else total + term
        outs.append(total)
    return outs


def to_lines(sources, count):
    lane = lax.broadcasted_iota(jnp.int32, (LANES, LANES), 0)
    place = lax.broadcasted_iota(jnp.int32, (LANES, LANES), 1)
    total = jnp.zeros((64 * len(sources), LANES), jnp.float32)
    for k in range(8):
        pick = (
            (place == 8 * (lane - REACH) + k) & (lane >= REACH) & (lane < REACH + count)
        ).astype(jnp.bfloat16)
        rest = jnp.concatenate([s[pl.ds(k, 64, stride=8), :] for s in sources], axis=0)
        rest = jnp.where(own_lanes(count), rest, 0.0)
        for _ in range(3):
            part = rest.astype(jnp.bfloat16)
            total = total + jnp.dot(part, pick, preferred_element_type=jnp.float32)
            rest = rest - part.astype(jnp.float32)
    return total


def in_parts(values):
    parts = []
    for _ in range(3):
        part = values.astype(jnp.bfloat16)
        parts.append(part)
        values = values - part.astype(jnp.float32)
    return parts


def spread_lines(lines, lane_of_element, out, base=None):
    count, length = lines.shape
    node = lax.broadcasted_iota(jnp.int32, (length, 2 * LANES), 0)
    place = lax.broadcasted_iota(jnp.int32, (length, 2 * LANES), 1)
    parts = in_parts(lines)
    for k in range(0, 8, 2):
        wanted = lane_of_element(node // 8) + LANES * (node % 8 - k)
        pick = ((node % 8 >= k) & (node % 8 < k + 2) & (place == wanted)).astype(jnp.bfloat16)
        total = None
        for part in parts:
            term = jnp.dot(part, pick, preferred_element_type=jnp.float32)
            total = term if total is None else total + term
        for half in range(2):
            value = total[:, half * LANES : (half + 1) * LANES]
            spot = pl.ds(k + half, count, stride=8)
            out[spot, :] = value if base is None else value + base[spot, :]


def own_lines_kernel(right_side, geometry, field, metric):
    spread_lines(right_side[...], lambda e: e + REACH, field)
    spread_lines(geometry[...], lambda e: e + REACH, metric)


def own_lines(right_side, geometry):
    return pl.pallas_call(
        own_lines_kernel,
        out_shape=[
            jax.ShapeDtypeStruct((512, LANES), jnp.float32),
            jax.ShapeDtypeStruct((2048, LANES), jnp.float32),
        ],
        name="own_lines",
    )(right_side, geometry)


def end_lines_kernel(count, with_edges, ends, own, out, *edges):
    spread_lines(ends[...], lambda e: jnp.where(e < REACH, e, e + count), out, own)
    if with_edges:
        backward, forward = edges
        for x in range(2):
            for y in range(8):
                backward[x, y] = out[pl.ds(64 * x + 8 * y, 8), :]
                forward[x, y] = out[pl.ds(64 * (6 + x) + 8 * y, 8), :]


def end_lines(ends, own, count, with_edges):
    outs = [jax.ShapeDtypeStruct(own.shape, jnp.float32)]
    if with_edges:
        outs += [jax.ShapeDtypeStruct((2, 8, 8, LANES), jnp.float32)] * 2
    return pl.pallas_call(
        functools.partial(end_lines_kernel, count, with_edges),
        out_shape=outs,
        name="end_lines_field" if with_edges else "end_lines_metric",
    )(ends, own)


def apply_local(derivative, folded, below, above, low, high, geometry, field, image):
    for x in range(8):
        for y in range(8):
            nodes = folded_second(folded, x + 1, y, x + 1, below, above)
            if x < 2:
                nodes = nodes + low[x, y]
            if x > 5:
                nodes = nodes + high[x - 6, y]
            field[pl.ds(64 * x + 8 * y, 8), :] = nodes
    for row in range(0, 512, 8):
        image[row : row + 8, :] = geometry[1536 + row : 1544 + row, :] * field[row : row + 8, :]
    for line in range(8):
        for dim in range(3):
            if dim == 0:
                spots = [pl.ds(64 * i + 8 * line, 8) for i in range(8)]
                places = spots
            elif dim == 1:
                spots = [pl.ds(64 * line + 8 * i, 8) for i in range(8)]
                places = [pl.ds(512 + 64 * line + 8 * i, 8) for i in range(8)]
            else:
                spots = [pl.ds(64 * line + i, 8, stride=8) for i in range(8)]
                places = [pl.ds(1024 + 64 * line + i, 8, stride=8) for i in range(8)]
            outs = both_ways(
                [field[s, :] for s in spots], [geometry[s, :] for s in places], derivative
            )
            for spot, out in zip(spots, outs):
                image[spot, :] = image[spot, :] + out


def first_operator_kernel(
    count, derivative, folded, below, above, low, high, geometry, field, image, backward, forward, inner
):
    apply_local(derivative, folded, below, above, low, high, geometry, field, image)
    total = jnp.zeros((8, LANES), jnp.float32)
    for row in range(0, 512, 8):
        total = total + field[row : row + 8, :] * image[row : row + 8, :]
    inner[...] = jnp.sum(jnp.where(own_lanes(count), total, 0.0), axis=0, keepdims=True)
    first = image[pl.ds(0, 64, stride=8), :]
    last = image[pl.ds(7, 64, stride=8), :]
    image[pl.ds(0, 64, stride=8), :] = first + pltpu.roll(last, 1, 1)
    image[pl.ds(7, 64, stride=8), :] = last + pltpu.roll(first, LANES - 1, 1)
    for x in range(2):
        for y in range(8):
            backward[x, y] = image[pl.ds(64 * x + 8 * y, 8), :]
            forward[x, y] = image[pl.ds(64 * (6 + x) + 8 * y, 8), :]


def first_operator(folded, below, above, low, high, geometry, count):
    full = jax.ShapeDtypeStruct((512, LANES), jnp.float32)
    edge = jax.ShapeDtypeStruct((2, 8, 8, LANES), jnp.float32)
    return pl.pallas_call(
        functools.partial(first_operator_kernel, count, derivative_table()),
        out_shape=[full, full, edge, edge, jax.ShapeDtypeStruct((1, LANES), jnp.float32)],
        name="first_operator",
    )(folded, below, above, low, high, geometry)


def second_operator_kernel(
    count,
    derivative,
    spot,
    folded,
    below,
    above,
    low,
    high,
    geometry,
    rho,
    d,
    g,
    size,
    lines,
    payload,
    field,
    image,
):
    apply_local(derivative, folded, below, above, low, high, geometry, field, image)
    largest = jnp.max(size[...])
    unit = 1.0 / jnp.where(largest > 0.0, largest, 1.0)
    own = own_lanes(count)
    total = jnp.zeros((8, LANES), jnp.float32)
    for row in range(0, 512, 8):
        total = total + (field[row : row + 8, :] * unit) * (image[row : row + 8, :] * unit)
    h = jnp.sum(jnp.where(own, total, 0.0))
    lane = lax.broadcasted_iota(jnp.int32, (1, LANES), 1)
    scalars = jnp.zeros((1, LANES), jnp.float32)
    sums = (jnp.sum(rho[...]), jnp.sum(d[...]), jnp.sum(g[...]), h, largest)
    for place, value in enumerate(sums):
        scalars = jnp.where(lane == 64 + place, value, scalars)
    both = to_lines([field, image], count)
    lines[...] = both
    line = lax.broadcasted_iota(jnp.int32, (64, LANES), 0)
    across = lax.broadcasted_iota(jnp.int32, (64, LANES), 1)
    first = jnp.sum(jnp.where(line == across, both[64:, 0:1], 0.0), axis=0, keepdims=True)
    last = jnp.sum(
        jnp.where(line == across, both[64:, LANES - 1 : LANES], 0.0), axis=0, keepdims=True
    )
    target = lax.broadcasted_iota(jnp.int32, payload.shape, 0)
    me = spot[2]
    payload[...] = scalars + jnp.where(
        target == me + 1, last, jnp.where(target == me - 1, first, 0.0)
    )


SMEM = pl.BlockSpec(memory_space=pltpu.SMEM)
VMEM = pl.BlockSpec(memory_space=pltpu.VMEM)


def second_operator(spot, folded, below, above, low, high, geometry, sums, count, devices):
    return pl.pallas_call(
        functools.partial(second_operator_kernel, count, derivative_table()),
        out_shape=[
            jax.ShapeDtypeStruct((128, LANES), jnp.float32),
            jax.ShapeDtypeStruct((devices, LANES), jnp.float32),
        ],
        in_specs=[SMEM] + [VMEM] * 10,
        out_specs=[VMEM, VMEM],
        scratch_shapes=[pltpu.VMEM((512, LANES), jnp.float32)] * 2,
        name="second_operator",
    )(spot, folded, below, above, low, high, geometry, *sums)


def lines_kernel(count, one, two, lines):
    lines[...] = to_lines([one, two], count)


def as_lines(one, two, count):
    return pl.pallas_call(
        functools.partial(lines_kernel, count),
        out_shape=jax.ShapeDtypeStruct((128, LANES), jnp.float32),
        name="as_lines",
    )(one, two)


def combine(columns):
    size = jnp.max(columns[4])
    ratio = columns[4] / jnp.where(size > 0.0, size, 1.0)
    factor = ratio * ratio
    return (
        jnp.sum(columns[0]),
        jnp.sum(columns[1]),
        jnp.sum(columns[2] * factor),
        jnp.sum(columns[3] * factor),
        size,
    )


NEIGHBOURS = [(dx, dy) for dx in (-1, 0, 1) for dy in (-1, 0, 1) if (dx, dy) != (0, 0)]


def middle_kernel(sizes, spot, gathered, lines, image, out):
    rows = gathered[...]
    values = combine([rows[:, 64 + i : 65 + i] for i in range(5)])
    source = lax.broadcasted_iota(jnp.int32, rows.shape, 0)
    before = jnp.sum(jnp.where(source == spot[2] - 1, rows, 0.0), axis=0, keepdims=True)
    after = jnp.sum(jnp.where(source == spot[2] + 1, rows, 0.0), axis=0, keepdims=True)
    line = lax.broadcasted_iota(jnp.int32, (64, LANES), 0)
    across = lax.broadcasted_iota(jnp.int32, (64, LANES), 1)
    before = jnp.sum(jnp.where(line == across, before, 0.0), axis=1, keepdims=True)
    after = jnp.sum(jnp.where(line == across, after, 0.0), axis=1, keepdims=True)
    t = lines[64:, :]
    behind = pltpu.roll(t, 1, 1)
    ahead = pltpu.roll(t, LANES - 1, 1)
    image[...] = t + jnp.where(
        across % 8 == 7,
        jnp.where(across == LANES - 1, after, ahead),
        jnp.where(across % 8 == 0, jnp.where(across == 0, before, behind), 0.0),
    )
    row = lax.broadcasted_iota(jnp.int32, (8, LANES), 0)
    lane = lax.broadcasted_iota(jnp.int32, (8, LANES), 1)
    scalars = jnp.zeros((8, LANES), jnp.float32)
    for place, value in enumerate(values):
        scalars = jnp.where(row == place, value, scalars)
    scalars = jnp.where(lane == 8, scalars, 0.0)
    for device in range(sizes[0] * sizes[1]):
        out[pl.ds(8 * device, 8), :] = scalars
    for dx, dy in NEIGHBOURS:
        x, y = spot[0] + dx, spot[1] + dy
        at_x, at_y = (7 if dx > 0 else 0), (7 if dy > 0 else 0)
        if dy == 0:
            face = image[pl.ds(8 * at_x, 8), :]
        elif dx == 0:
            face = image[pl.ds(at_y, 8, stride=8), :]
        else:
            face = jnp.broadcast_to(image[pl.ds(8 * at_x + at_y, 1), :], (8, LANES))
        tile = jnp.where(lane == 8, scalars, face)

        @pl.when((x >= 0) & (x < sizes[0]) & (y >= 0) & (y < sizes[1]))
        def _():
            out[pl.ds(pl.multiple_of(8 * (x * sizes[1] + y), 8), 8), :] = tile


def middle(spot, gathered, lines, sizes):
    return pl.pallas_call(
        functools.partial(middle_kernel, sizes),
        out_shape=[
            jax.ShapeDtypeStruct((64, LANES), jnp.float32),
            jax.ShapeDtypeStruct((8 * sizes[0] * sizes[1], LANES), jnp.float32),
        ],
        in_specs=[SMEM, VMEM, VMEM],
        out_specs=[VMEM, VMEM],
        name="middle",
    )(spot, gathered, lines)


def finish_kernel(
    sizes, spot, gathered, image, second, first, right_side, solution_out, residual_out, t
):
    plane = sizes[0] * sizes[1]
    columns = [gathered[pl.ds(i, plane, stride=8), :][:, 8:9] for i in range(5)]
    rho, d, g_scaled, h_scaled, size = combine(columns)
    t[...] = image[...]
    lane = lax.broadcasted_iota(jnp.int32, (8, LANES), 1)
    for dx, dy in NEIGHBOURS:
        x, y = spot[0] + dx, spot[1] + dy
        inside = (x >= 0) & (x < sizes[0]) & (y >= 0) & (y < sizes[1])
        source = jnp.where(inside, x * sizes[1] + y, 0)
        tile = gathered[pl.ds(pl.multiple_of(8 * source, 8), 8), :]
        tile = jnp.where(lane == 8, pltpu.roll(tile, 1, 1), tile)
        tile = jnp.where(inside, tile, 0.0)
        at_x, at_y = (7 if dx > 0 else 0), (7 if dy > 0 else 0)
        if dy == 0:
            spots = pl.ds(8 * at_x, 8)
        elif dx == 0:
            spots = pl.ds(at_y, 8, stride=8)
        else:
            spots = pl.ds(8 * at_x + at_y, 1)
            tile = tile[0:1, :]
        t[spots, :] = t[spots, :] + tile

    def splat(value):
        return jnp.full((1, LANES), value, jnp.float32)

    rho, d = splat(rho), splat(d)
    alpha_one = rho / d
    reach = alpha_one * splat(size)
    g = reach * reach * splat(g_scaled)
    h = reach * reach * splat(h_scaled)
    stretch = g / rho
    alpha_two = (g - rho) / (h - stretch * g / alpha_one)
    along = alpha_one + alpha_two * stretch
    turn = alpha_one * alpha_two
    solution_out[...] = along * first[0:64, :] - turn * second[0:64, :]
    residual_out[...] = right_side[...] - along * first[64:128, :] + turn * t[...]


def finish(spot, gathered, image, second, first, right_side, sizes):
    full = jax.ShapeDtypeStruct((64, LANES), jnp.float32)
    return pl.pallas_call(
        functools.partial(finish_kernel, sizes),
        out_shape=[full, full],
        in_specs=[SMEM] + [VMEM] * 5,
        out_specs=[VMEM, VMEM],
        scratch_shapes=[pltpu.VMEM((64, LANES), jnp.float32)],
        name="finish",
    )(spot, gathered, image, second, first, right_side)


def exchange(rows, axes):
    return lax.all_to_all(rows, axes, 0, 0, tiled=True)


def on_device(right_side, geometry, element_shape_class, fdm_vectors, fdm_values):
    count = element_shape_class.shape[2]
    classes = fdm_vectors.shape[0]
    depth = lax.axis_size("gz")
    sizes = (lax.axis_size("gx"), lax.axis_size("gy"))
    spot = jnp.stack([lax.axis_index(a).astype(jnp.int32) for a in ("gx", "gy", "gz")])
    ends = 8 * REACH
    lines = right_side.reshape(64, LANES)
    metric_lines = geometry.reshape(256, LANES)
    class_lines = jnp.broadcast_to(
        jnp.repeat(element_shape_class.reshape(1, -1), 8, axis=1).astype(jnp.float32),
        (8, 8 * count),
    )
    stack = jnp.concatenate([lines, class_lines, metric_lines], axis=0)
    low, high = swap(stack[:, :ends], stack[:, -ends:], "gz")
    own_field, own_metric = own_lines(lines, metric_lines)
    outer = jnp.concatenate([low, high], axis=1)
    deep_class = jnp.concatenate(
        [low[64, ::8], element_shape_class.reshape(-1).astype(jnp.float32), high[64, ::8]]
    ).astype(jnp.int32)
    deep_class = jnp.pad(deep_class, (0, LANES - deep_class.shape[0]))
    element = jnp.arange(LANES, dtype=jnp.int32) - REACH + spot[2] * count
    valid = ((element >= 0) & (element < depth * count)).astype(jnp.float32)[None, :]
    onehot = (jnp.arange(classes, dtype=jnp.int32)[:, None] == deep_class[None, :]).astype(
        jnp.float32
    )
    entries = jnp.concatenate(
        [fdm_vectors.reshape(classes, 300), fdm_values.reshape(classes, 30)], axis=1
    )
    table = lax.dot_general(
        entries, onehot, (((0,), (0,)), ((), ())), precision=HIGHEST
    )
    field, backward, forward = end_lines(outer[:64], own_field, count, True)
    low, high = swap(backward, forward, "gx")
    (metric,) = end_lines(outer[72:], own_metric, count, False)
    low, high, metric, table = lax.optimization_barrier((low, high, metric, table))
    below, above = swap(*second_edges(field, low, high, False), "gy")
    folded, rims, backward, forward, rho = block_solve(
        field, low, high, below, above, table, valid, count, False
    )
    below, above = swap(backward, forward, "gy")
    low, high = swap(*first_edges(rims, below, above), "gx")
    p, image, backward, forward, d = first_operator(
        folded, below, above, low, high, metric, count
    )
    low, high = swap(backward, forward, "gx")
    below, above = swap(*second_edges(image, low, high, True), "gy")
    folded, rims, backward, forward, g, size, q = block_solve(
        image, low, high, below, above, table, valid, count, True
    )
    below, above = swap(backward, forward, "gy")
    first = as_lines(p, q, count)
    below, above, first = lax.optimization_barrier((below, above, first))
    low, high = swap(*first_edges(rims, below, above), "gx")
    second, payload = second_operator(
        spot, folded, below, above, low, high, own_metric, (rho, d, g, size), count, depth
    )
    gathered = exchange(payload, "gz")
    image, tiles = middle(spot, gathered, second, sizes)
    gathered = exchange(tiles, ("gx", "gy"))
    answer, left = finish(spot, gathered, image, second, first, lines, sizes)
    return (answer.reshape(8, 8, LANES), left.reshape(8, 8, LANES))


def solution(mesh):
    placed = (P("gx", "gy", "gz"), P(None, "gx", "gy", "gz"), P("gx", "gy", "gz"), P(), P())
    return jax.shard_map(
        on_device,
        mesh=mesh,
        in_specs=placed,
        out_specs=(P("gx", "gy", "gz"), P("gx", "gy", "gz")),
        check_vma=False,
    )
```

time: 199 us -> 174 us (0.87)
  starting transfers between devices: 88.7 us -> 50.8 us
  blocking collectives: 23.8 us -> 42.6 us
  Pallas kernels: 20.5 us -> 35.8 us
  local copies, waits for them, and re-layouts: 21.4 us -> 7.04 us
  other arithmetic: 10.5 us -> 4.21 us
    ppermute x24 -> x18, starting transfers between devices: 73.7 us -> 50.8 us  [the longest x9 33 us: swap(): lax.ppermute(forward_part, axis, forward)]
    all_to_all x1 -> x2, blocking collectives: 23.8 us -> 42.6 us  [exchange(): return lax.all_to_all(rows, axes, 0, 0, tiled=True)]
    all_to_all x1 -> x0, starting transfers between devices: 14.9 us -> none  [exchange(): return lax.all_to_all(rows, axes, 0, 0, tiled=True)]
    pallas_call x2 -> x9, Pallas kernels: 3.73 us -> 18.4 us  [the longest x2 5.04 us: end_lines(): pl.pallas_call(functools.partial(end_lines_kernel, count, with_edges), ou...]
    slice x18 -> x3, local copies, waits for them, and re-layouts: 7.9 us -> 0.28 us  [the longest x1 0.1 us: on_device(): low, high = swap(stack[:, :ends], stack[:, -ends:], 'gz')]
    ppermute x24 -> x18, waiting for transfers between devices: 23 us -> 30.1 us  [the longest x9 28.7 us: swap(): lax.ppermute(backward_part, axis, backward)]
    all_to_all x1 -> x0, waiting for transfers between devices: 6.82 us -> none  [exchange(): return lax.all_to_all(rows, axes, 0, 0, tiled=True)]
    add x7 -> x0, other arithmetic: 4.47 us -> none  [the longest x2 1.96 us: fold_one(): cut(block, 1, 3, dim) + low]
  transfers between devices with their start and end apart: 25 -> 18, of which waited for: 13 -> 11; matrix products, arithmetic and copies ran while one was open for 8% -> 2% of each run, Pallas kernels for 1% -> 4%
where the time goes in v1:
time: 174 us; the launch traced here: 173 us
  starting transfers between devices  50.8 us (29%)
  blocking collectives  42.6 us (24%)
  Pallas kernels  35.8 us (21%)
  waiting for transfers between devices  30.1 us (17%)
  local copies, waits for them, and re-layouts  7.04 us (4%)
  other arithmetic  4.21 us (2%)
    all_to_all x2, blocking collectives, exchange(): return lax.all_to_all(rows, axes, 0, 0, tiled=True)  42.6 us
    ppermute x9, starting transfers between devices, swap(): lax.ppermute(forward_part, axis, forward)  33 us
    ppermute x9, waiting for transfers between devices, swap(): lax.ppermute(backward_part, axis, backward)  28.7 us
    ppermute x9, starting transfers between devices, swap(): lax.ppermute(backward_part, axis, backward)  17.9 us
    pallas_call x2, Pallas kernels, block_solve(): pl.pallas_call(functools.partial(solve_kernel, count, shared), out_shape=...  8.74 us
    unnamed x39, local copies, waits for them, and re-layouts  5.68 us
    pallas_call x2, Pallas kernels, end_lines(): pl.pallas_call(functools.partial(end_lines_kernel, count, with_edges), ou...  5.04 us
  transfers between devices with their start and end apart: 18, of which 11 were waited for; matrix products, arithmetic and copies ran while one was open for 2% of the time, Pallas kernels for 4%

profile of v1, /device:TPU:1, one launch (start us, length us, event | category | flops | bytes accessed | tf_op | source)
XLA Modules:
  0.0 172.6 jit_solution(1657967019113926065)
XLA Ops:
  2.5 5.0 %collective-permute-start = (f32[328,32]{1,0:T(8,128)S(1)}, f32[328,32]{1,0:T(8,128)S(1)}, u32[]{:S(2)}, u32[]{:S(2)}) collective-permute-start(f32[328,32]{1,0:T(8,128)S(1)} %get-tuple-element.88), channel_id=1, source_target_pairs={{0,1},{1,2},{2,3},{3,4},{4,5},{5,6},{6,7},{7,8},{8,9},{9,10},{10,1... | collective-permute-start | bytes 125960 | tf_op jit(solution)/shard_map/ppermute | solution.py:21
  8.8 2.7 %own_lines.1 = (f32[512,128]{1,0:T(8,128)}, f32[2048,128]{1,0:T(8,128)}) custom-call(f32[64,128]{1,0:T(8,128)} %bitcast.25, f32[256,128]{1,0:T(8,128)} %bitcast.23), custom_call_target="tpu_custom_call" | custom-call | tf_op jit(solution)/shard_map/own_lines/pallas_call | solution.py:286
  11.7 2.5 %collective-permute-done.1 = f32[328,32]{1,0:T(8,128)S(1)} collective-permute-done((f32[328,32]{1,0:T(8,128)S(1)}, f32[328,32]{1,0:T(8,128)S(1)}, u32[]{:S(2)}, u32[]{:S(2)}) %collective-permute-start.1) | collective-permute-done | bytes 42016 | tf_op jit(solution)/shard_map/ppermute | solution.py:21
  14.9 2.0 %end_lines_field.1 = (f32[512,128]{1,0:T(8,128)}, f32[2,8,8,128]{3,2,1,0:T(8,128)}, f32[2,8,8,128]{3,2,1,0:T(8,128)}) custom-call(f32[64,64]{1,0:T(8,128)} %pad_maximum_fusion.2.ends, f32[512,128]{1,0:T(8,128)} %get-tuple-element.45.own), custom_call_target="tpu_custom_call" | custom-call | tf_op jit(solution)/shard_map/end_lines_field/pallas_call | solution.py:310
  16.9 5.5 %collective-permute-start.2 = (f32[2,8,8,128]{3,2,1,0:T(8,128)}, f32[2,8,8,128]{3,2,1,0:T(8,128)S(1)}, u32[]{:S(2)}, u32[]{:S(2)}) collective-permute-start(f32[2,8,8,128]{3,2,1,0:T(8,128)} %get-tuple-element.47), channel_id=1, source_target_pairs={{0,96},{96,192},{192,288},{288,384},{384,480},{480,576},{576,672},... | collective-permute-start | bytes 196616 | tf_op jit(solution)/shard_map/ppermute | solution.py:21
  22.4 5.2 %collective-permute-start.3 = (f32[2,8,8,128]{3,2,1,0:T(8,128)}, f32[2,8,8,128]{3,2,1,0:T(8,128)S(1)}, u32[]{:S(2)}, u32[]{:S(2)}) collective-permute-start(f32[2,8,8,128]{3,2,1,0:T(8,128)} %get-tuple-element.48), channel_id=1, source_target_pairs={{96,0},{192,96},{288,192},{384,288},{480,384},{576,480},{672,576},... | collective-permute-start | bytes 196616 | tf_op jit(solution)/shard_map/ppermute | solution.py:21
  29.7 3.1 %end_lines_metric.1.geometry = f32[2048,128]{1,0:T(8,128)} custom-call(f32[256,64]{1,0:T(8,128)} %pad_maximum_fusion.1.ends, f32[2048,128]{1,0:T(8,128)} %get-tuple-element.49.own.geometry), custom_call_target="tpu_custom_call" | custom-call | tf_op jit(solution)/shard_map/end_lines_metric/pallas_call | solution.py:310
  38.4 4.1 %collective-permute-done.5.above = f32[10,2,8,128]{3,2,1,0:T(8,128)S(1)} collective-permute-done((f32[10,2,8,128]{3,2,1,0:T(8,128)}, f32[10,2,8,128]{3,2,1,0:T(8,128)S(1)}, u32[]{:S(2)}, u32[]{:S(2)}) %collective-permute-start.5) | collective-permute-done | bytes 81952 | tf_op jit(solution)/shard_map/ppermute | solution.py:21
  43.2 4.4 %block_solve_first.1 = (f32[10,10,8,128]{3,2,1,0:T(8,128)}, f32[4,10,8,128]{3,2,1,0:T(8,128)}, f32[10,2,8,128]{3,2,1,0:T(8,128)}, f32[10,2,8,128]{3,2,1,0:T(8,128)}, f32[1,128]{1,0:T(1,128)}) custom-call(f32[512,128]{1,0:T(8,128)} %get-tuple-element.46.field, f32[2,8,8,128]{3,2,1,0:T(8,128)} %copy-done.4, f32[2,8,8,128]{3,2,1,0:T(8,128)} %copy-done.5, ...), custom_call_target="tpu_custom_call" | custom-call | tf_op jit(solution)/shard_map/block_solve_first/pallas_call | solution.py:183
  50.9 4.6 %collective-permute-done.7.above = f32[10,2,8,128]{3,2,1,0:T(8,128)S(1)} collective-permute-done((f32[10,2,8,128]{3,2,1,0:T(8,128)}, f32[10,2,8,128]{3,2,1,0:T(8,128)S(1)}, u32[]{:S(2)}, u32[]{:S(2)}) %collective-permute-start.7) | collective-permute-done | bytes 81952 | tf_op jit(solution)/shard_map/ppermute | solution.py:21
  57.8 5.2 %collective-permute-start.8 = (f32[2,8,8,128]{3,2,1,0:T(8,128)}, f32[2,8,8,128]{3,2,1,0:T(8,128)S(1)}, u32[]{:S(2)}, u32[]{:S(2)}) collective-permute-start(f32[2,8,8,128]{3,2,1,0:T(8,128)} %get-tuple-element.59), channel_id=1, source_target_pairs={{0,96},{96,192},{192,288},{288,384},{384,480},{480,576},{576,672},... | collective-permute-start | bytes 196616 | tf_op jit(solution)/shard_map/ppermute | solution.py:21
  63.0 1.9 %collective-permute-start.9 = (f32[2,8,8,128]{3,2,1,0:T(8,128)}, f32[2,8,8,128]{3,2,1,0:T(8,128)S(1)}, u32[]{:S(2)}, u32[]{:S(2)}) collective-permute-start(f32[2,8,8,128]{3,2,1,0:T(8,128)} %get-tuple-element.60), channel_id=1, source_target_pairs={{96,0},{192,96},{288,192},{384,288},{480,384},{576,480},{672,576},... | collective-permute-start | bytes 196616 | tf_op jit(solution)/shard_map/ppermute | solution.py:21
  65.0 3.8 %collective-permute-done.9.high = f32[2,8,8,128]{3,2,1,0:T(8,128)S(1)} collective-permute-done((f32[2,8,8,128]{3,2,1,0:T(8,128)}, f32[2,8,8,128]{3,2,1,0:T(8,128)S(1)}, u32[]{:S(2)}, u32[]{:S(2)}) %collective-permute-start.9) | collective-permute-done | bytes 65568 | tf_op jit(solution)/shard_map/ppermute | solution.py:21
  69.5 3.2 %first_operator.1 = (f32[512,128]{1,0:T(8,128)}, f32[512,128]{1,0:T(8,128)}, f32[2,8,8,128]{3,2,1,0:T(8,128)}, f32[2,8,8,128]{3,2,1,0:T(8,128)}, f32[1,128]{1,0:T(1,128)}) custom-call(f32[10,10,8,128]{3,2,1,0:T(8,128)} %get-tuple-element.55.folded, f32[10,2,8,128]{3,2,1,0:T(8,128)} %copy-done.2, f32[10,2,8,128]{3,2,1,0:T(8,128)} %copy-done.3, ...), custom_call_target="tpu_custom_call" | custom-call | tf_op jit(solution)/shard_map/first_operator/pallas_call | solution.py:367
  72.7 2.0 %collective-permute-start.10 = (f32[2,8,8,128]{3,2,1,0:T(8,128)}, f32[2,8,8,128]{3,2,1,0:T(8,128)S(1)}, u32[]{:S(2)}, u32[]{:S(2)}) collective-permute-start(f32[2,8,8,128]{3,2,1,0:T(8,128)} %get-tuple-element.63), channel_id=1, source_target_pairs={{0,96},{96,192},{192,288},{288,384},{384,480},{480,576},{576,672},... | collective-permute-start | bytes 196616 | tf_op jit(solution)/shard_map/ppermute | solution.py:21
  74.6 2.4 %collective-permute-start.11 = (f32[2,8,8,128]{3,2,1,0:T(8,128)}, f32[2,8,8,128]{3,2,1,0:T(8,128)S(1)}, u32[]{:S(2)}, u32[]{:S(2)}) collective-permute-start(f32[2,8,8,128]{3,2,1,0:T(8,128)} %get-tuple-element.64), channel_id=1, source_target_pairs={{96,0},{192,96},{288,192},{384,288},{480,384},{576,480},{672,576},... | collective-permute-start | bytes 196616 | tf_op jit(solution)/shard_map/ppermute | solution.py:21
  77.0 3.4 %collective-permute-done.11.high = f32[2,8,8,128]{3,2,1,0:T(8,128)S(1)} collective-permute-done((f32[2,8,8,128]{3,2,1,0:T(8,128)}, f32[2,8,8,128]{3,2,1,0:T(8,128)S(1)}, u32[]{:S(2)}, u32[]{:S(2)}) %collective-permute-start.11) | collective-permute-done | bytes 65568 | tf_op jit(solution)/shard_map/ppermute | solution.py:21
  81.0 1.7 second_edges.3
  82.7 4.8 %collective-permute-start.12 = (f32[10,2,8,128]{3,2,1,0:T(8,128)}, f32[10,2,8,128]{3,2,1,0:T(8,128)S(1)}, u32[]{:S(2)}, u32[]{:S(2)}) collective-permute-start(f32[10,2,8,128]{3,2,1,0:T(8,128)} %get-tuple-element.65), channel_id=1, source_target_pairs={{0,12},{12,24},{24,36},{36,48},{48,60},{60,72},{72,84},{1,13},{13,... | collective-permute-start | bytes 245768 | tf_op jit(solution)/shard_map/ppermute | solution.py:21
  89.3 3.9 %collective-permute-done.13.above = f32[10,2,8,128]{3,2,1,0:T(8,128)S(1)} collective-permute-done((f32[10,2,8,128]{3,2,1,0:T(8,128)}, f32[10,2,8,128]{3,2,1,0:T(8,128)S(1)}, u32[]{:S(2)}, u32[]{:S(2)}) %collective-permute-start.13) | collective-permute-done | bytes 81952 | tf_op jit(solution)/shard_map/ppermute | solution.py:21
  93.9 4.4 %block_solve_shared.1 = (f32[10,10,8,128]{3,2,1,0:T(8,128)}, f32[4,10,8,128]{3,2,1,0:T(8,128)}, f32[10,2,8,128]{3,2,1,0:T(8,128)}, f32[10,2,8,128]{3,2,1,0:T(8,1...) custom-call(f32[512,128]{1,0:T(8,128)} %get-tuple-element.62.field, f32[2,8,8,128]{3,2,1,0:T(8,128)} %copy-done.6, ...), custom_call_target="tpu_custom_call" | custom-call | tf_op jit(solution)/shard_map/block_solve_shared/pallas_call | solution.py:183
  98.3 3.4 %collective-permute-start.14 = (f32[10,2,8,128]{3,2,1,0:T(8,128)}, f32[10,2,8,128]{3,2,1,0:T(8,128)S(1)}, u32[]{:S(2)}, u32[]{:S(2)}) collective-permute-start(f32[10,2,8,128]{3,2,1,0:T(8,128)} %get-tuple-element.68), channel_id=1, source_target_pairs={{0,12},{12,24},{24,36},{36,48},{48,60},{60,72},{72,84},{1,13},{13,... | collective-permute-start | bytes 245768 | tf_op jit(solution)/shard_map/ppermute | solution.py:21
  102.9 2.0 %as_lines.1.first = f32[128,128]{1,0:T(8,128)} custom-call(f32[512,128]{1,0:T(8,128)} %get-tuple-element.70.one, f32[512,128]{1,0:T(8,128)} %get-tuple-element.71.two), custom_call_target="tpu_custom_call" | custom-call | tf_op jit(solution)/shard_map/as_lines/pallas_call | solution.py:444
  105.0 3.1 %collective-permute-done.15.above = f32[10,2,8,128]{3,2,1,0:T(8,128)S(1)} collective-permute-done((f32[10,2,8,128]{3,2,1,0:T(8,128)}, f32[10,2,8,128]{3,2,1,0:T(8,128)S(1)}, u32[]{:S(2)}, u32[]{:S(2)}) %collective-permute-start.15) | collective-permute-done | bytes 81952 | tf_op jit(solution)/shard_map/ppermute | solution.py:21
  110.3 4.4 %collective-permute-start.16 = (f32[2,8,8,128]{3,2,1,0:T(8,128)}, f32[2,8,8,128]{3,2,1,0:T(8,128)S(1)}, u32[]{:S(2)}, u32[]{:S(2)}) collective-permute-start(f32[2,8,8,128]{3,2,1,0:T(8,128)} %get-tuple-element.75), channel_id=1, source_target_pairs={{0,96},{96,192},{192,288},{288,384},{384,480},{480,576},{576,672},... | collective-permute-start | bytes 196616 | tf_op jit(solution)/shard_map/ppermute | solution.py:21
  114.7 1.9 %collective-permute-start.17 = (f32[2,8,8,128]{3,2,1,0:T(8,128)}, f32[2,8,8,128]{3,2,1,0:T(8,128)S(1)}, u32[]{:S(2)}, u32[]{:S(2)}) collective-permute-start(f32[2,8,8,128]{3,2,1,0:T(8,128)} %get-tuple-element.76), channel_id=1, source_target_pairs={{96,0},{192,96},{288,192},{384,288},{480,384},{576,480},{672,576},... | collective-permute-start | bytes 196616 | tf_op jit(solution)/shard_map/ppermute | solution.py:21
  117.3 3.3 %collective-permute-done.17.high = f32[2,8,8,128]{3,2,1,0:T(8,128)S(1)} collective-permute-done((f32[2,8,8,128]{3,2,1,0:T(8,128)}, f32[2,8,8,128]{3,2,1,0:T(8,128)S(1)}, u32[]{:S(2)}, u32[]{:S(2)}) %collective-permute-start.17) | collective-permute-done | bytes 65568 | tf_op jit(solution)/shard_map/ppermute | solution.py:21
  121.1 3.4 %second_operator.1 = (f32[128,128]{1,0:T(8,128)}, f32[12,128]{1,0:T(8,128)}) custom-call(s32[3]{0:T(128)} %pad_add_fusion.spot, f32[10,10,8,128]{3,2,1,0:T(8,128)} %get-tuple-element.67.folded, f32[10,2,8,128]{3,2,1,0:T(8,128)} %copy-done, f32[10,2,8,128]{3,2,1,0:T(8,128)} %copy-done.1, f32[2,8,8,128]{3,2,1,0:T(8,128)} %copy-done.13, ...), custom_call_target="tpu_custom_call" | custom-call | tf_op jit(solution)/shard_map/second_operator/pallas_call | solution.py:426
  125.3 23.3 %all_to_all.22 = f32[12,1,128]{2,1,0:T(1,128)S(1)} all-to-all(f32[12,1,128]{2,1,0:T(1,128)S(1)} %copy.13), channel_id=1, replica_groups=mesh['gx'=8,'gy'=8,'gz'=12] {'gz'}, dimensions={0} | all-to-all | bytes 12288 | tf_op jit(solution)/shard_map/all_to_all | solution.py:576
  149.1 2.1 %middle.1 = (f32[64,128]{1,0:T(8,128)}, f32[512,128]{1,0:T(8,128)}) custom-call(s32[3]{0:T(128)} %pad_add_fusion.spot, f32[12,128]{1,0:T(8,128)} %bitcast.28, f32[128,128]{1,0:T(8,128)} %get-tuple-element.82.lines.second), custom_call_target="tpu_custom_call" | custom-call | tf_op jit(solution)/shard_map/middle/pallas_call | solution.py:510
  151.2 19.4 %all_to_all.23 = f32[64,8,128]{2,1,0:T(8,128)} all-to-all(f32[64,8,128]{2,1,0:T(8,128)} %bitcast.27), channel_id=1, replica_groups=mesh['gx'=8,'gy'=8,'gz'=12] {'gx','gy'}, dimensions={0} | all-to-all | bytes 524288 | tf_op jit(solution)/shard_map/all_to_all | solution.py:576
  170.6 2.0 %finish.1 = (f32[64,128]{1,0:T(8,128)}, f32[64,128]{1,0:T(8,128)}) custom-call(s32[3]{0:T(128)} %pad_add_fusion.spot, f32[512,128]{1,0:T(8,128)} %bitcast.21, f32[64,128]{1,0:T(8,128)} %get-tuple-element.84.image, f32[128,128]{1,0:T(8,128)} %get-tuple-element.82.lines.second, f32[128,128]{1,0:T(8,128)} %as_lines.1.first, f32[64,128]{1,0:T(8,128)} %bitcast.26), custom_call_target="tpu_custom_call" | custom-call | tf_op jit(solution)/shard_map/finish/pallas_call | solution.py:565
  (79 shorter events, 27.8 us)
Async XLA Ops:
  2.4 9.1 %copy-start.17 = (f32[32,3,10]{0,1,2:T(4,128)S(1)}, f32[32,3,10]{0,1,2:T(4,128)}, u32[]{:S(2)}) copy-start(f32[32,3,10]{0,1,2:T(4,128)} %param.9) | copy-start | bytes 11524
  2.5 9.1 %copy-start.8 = (f32[32,3,10,10]{0,1,3,2:T(4,128)S(1)}, f32[32,3,10,10]{0,1,3,2:T(4,128)}, u32[]{:S(2)}) copy-start(f32[32,3,10,10]{0,1,3,2:T(4,128)} %param.8) | copy-start | bytes 115204
  2.5 9.2 %collective-permute-start = (f32[328,32]{1,0:T(8,128)S(1)}, f32[328,32]{1,0:T(8,128)S(1)}, u32[]{:S(2)}, u32[]{:S(2)}) collective-permute-start(f32[328,32]{1,0:T(8,128)S(1)} %get-tuple-element.88), channel_id=1, source_target_pairs={{0,1},{1,2},{2,3},{3,4},{4,5},{5,6},{6,7},{7,8},{8,9},{9,10},{10,1... | collective-permute-start | bytes 125960 | tf_op jit(solution)/shard_map/ppermute | solution.py:21
  7.5 6.7 %collective-permute-start.1 = (f32[328,32]{1,0:T(8,128)S(1)}, f32[328,32]{1,0:T(8,128)S(1)}, u32[]{:S(2)}, u32[]{:S(2)}) collective-permute-start(f32[328,32]{1,0:T(8,128)S(1)} %get-tuple-element.89), channel_id=1, source_target_pairs={{1,0},{2,1},{3,2},{4,3},{5,4},{6,5},{7,6},{8,7},{9,8},{10,9},{11,1... | collective-permute-start | bytes 125960 | tf_op jit(solution)/shard_map/ppermute | solution.py:21
  16.9 15.8 %collective-permute-start.2 = (f32[2,8,8,128]{3,2,1,0:T(8,128)}, f32[2,8,8,128]{3,2,1,0:T(8,128)S(1)}, u32[]{:S(2)}, u32[]{:S(2)}) collective-permute-start(f32[2,8,8,128]{3,2,1,0:T(8,128)} %get-tuple-element.47), channel_id=1, source_target_pairs={{0,96},{96,192},{192,288},{288,384},{384,480},{480,576},{576,672},... | collective-permute-start | bytes 196616 | tf_op jit(solution)/shard_map/ppermute | solution.py:21
  22.4 10.3 %collective-permute-start.3 = (f32[2,8,8,128]{3,2,1,0:T(8,128)}, f32[2,8,8,128]{3,2,1,0:T(8,128)S(1)}, u32[]{:S(2)}, u32[]{:S(2)}) collective-permute-start(f32[2,8,8,128]{3,2,1,0:T(8,128)} %get-tuple-element.48), channel_id=1, source_target_pairs={{96,0},{192,96},{288,192},{384,288},{480,384},{576,480},{672,576},... | collective-permute-start | bytes 196616 | tf_op jit(solution)/shard_map/ppermute | solution.py:21
  32.7 0.6 copy-start.5
  35.0 3.4 %collective-permute-start.4 = (f32[10,2,8,128]{3,2,1,0:T(8,128)}, f32[10,2,8,128]{3,2,1,0:T(8,128)S(1)}, u32[]{:S(2)}, u32[]{:S(2)}) collective-permute-start(f32[10,2,8,128]{3,2,1,0:T(8,128)} %get-tuple-element.52), channel_id=1, source_target_pairs={{0,12},{12,24},{24,36},{36,48},{48,60},{60,72},{72,84},{1,13},{13,... | collective-permute-start | bytes 245768 | tf_op jit(solution)/shard_map/ppermute | solution.py:21
  36.3 6.3 %collective-permute-start.5 = (f32[10,2,8,128]{3,2,1,0:T(8,128)}, f32[10,2,8,128]{3,2,1,0:T(8,128)S(1)}, u32[]{:S(2)}, u32[]{:S(2)}) collective-permute-start(f32[10,2,8,128]{3,2,1,0:T(8,128)} %get-tuple-element.53), channel_id=1, source_target_pairs={{12,0},{24,12},{36,24},{48,36},{60,48},{72,60},{84,72},{13,1},{25,... | collective-permute-start | bytes 245768 | tf_op jit(solution)/shard_map/ppermute | solution.py:21
  38.4 4.1 %copy-start.10 = (f32[10,2,8,128]{3,2,1,0:T(8,128)}, f32[10,2,8,128]{3,2,1,0:T(8,128)S(1)}, u32[]{:S(2)}) copy-start(f32[10,2,8,128]{3,2,1,0:T(8,128)S(1)} %collective-permute-done.4.below) | copy-start | bytes 245764
  42.6 0.6 copy-start.12
  47.5 3.3 %collective-permute-start.6 = (f32[10,2,8,128]{3,2,1,0:T(8,128)}, f32[10,2,8,128]{3,2,1,0:T(8,128)S(1)}, u32[]{:S(2)}, u32[]{:S(2)}) collective-permute-start(f32[10,2,8,128]{3,2,1,0:T(8,128)} %get-tuple-element.56), channel_id=1, source_target_pairs={{0,12},{12,24},{24,36},{36,48},{48,60},{60,72},{72,84},{1,13},{13,... | collective-permute-start | bytes 245768 | tf_op jit(solution)/shard_map/ppermute | solution.py:21
  49.0 6.5 %collective-permute-start.7 = (f32[10,2,8,128]{3,2,1,0:T(8,128)}, f32[10,2,8,128]{3,2,1,0:T(8,128)S(1)}, u32[]{:S(2)}, u32[]{:S(2)}) collective-permute-start(f32[10,2,8,128]{3,2,1,0:T(8,128)} %get-tuple-element.57), channel_id=1, source_target_pairs={{12,0},{24,12},{36,24},{48,36},{60,48},{72,60},{84,72},{13,1},{25,... | collective-permute-start | bytes 245768 | tf_op jit(solution)/shard_map/ppermute | solution.py:21
  50.9 4.6 %copy-start.2 = (f32[10,2,8,128]{3,2,1,0:T(8,128)}, f32[10,2,8,128]{3,2,1,0:T(8,128)S(1)}, u32[]{:S(2)}) copy-start(f32[10,2,8,128]{3,2,1,0:T(8,128)S(1)} %collective-permute-done.6.below) | copy-start | bytes 245764
  55.5 0.6 copy-start.3
  57.8 7.2 %collective-permute-start.8 = (f32[2,8,8,128]{3,2,1,0:T(8,128)}, f32[2,8,8,128]{3,2,1,0:T(8,128)S(1)}, u32[]{:S(2)}, u32[]{:S(2)}) collective-permute-start(f32[2,8,8,128]{3,2,1,0:T(8,128)} %get-tuple-element.59), channel_id=1, source_target_pairs={{0,96},{96,192},{192,288},{288,384},{384,480},{480,576},{576,672},... | collective-permute-start | bytes 196616 | tf_op jit(solution)/shard_map/ppermute | solution.py:21
  63.0 5.8 %collective-permute-start.9 = (f32[2,8,8,128]{3,2,1,0:T(8,128)}, f32[2,8,8,128]{3,2,1,0:T(8,128)S(1)}, u32[]{:S(2)}, u32[]{:S(2)}) collective-permute-start(f32[2,8,8,128]{3,2,1,0:T(8,128)} %get-tuple-element.60), channel_id=1, source_target_pairs={{96,0},{192,96},{288,192},{384,288},{480,384},{576,480},{672,576},... | collective-permute-start | bytes 196616 | tf_op jit(solution)/shard_map/ppermute | solution.py:21
  65.0 3.9 %copy-start.15 = (f32[2,8,8,128]{3,2,1,0:T(8,128)}, f32[2,8,8,128]{3,2,1,0:T(8,128)S(1)}, u32[]{:S(2)}) copy-start(f32[2,8,8,128]{3,2,1,0:T(8,128)S(1)} %collective-permute-done.8.low) | copy-start | bytes 196612
  72.7 4.3 %collective-permute-start.10 = (f32[2,8,8,128]{3,2,1,0:T(8,128)}, f32[2,8,8,128]{3,2,1,0:T(8,128)S(1)}, u32[]{:S(2)}, u32[]{:S(2)}) collective-permute-start(f32[2,8,8,128]{3,2,1,0:T(8,128)} %get-tuple-element.63), channel_id=1, source_target_pairs={{0,96},{96,192},{192,288},{288,384},{384,480},{480,576},{576,672},... | collective-permute-start | bytes 196616 | tf_op jit(solution)/shard_map/ppermute | solution.py:21
  74.6 5.8 %collective-permute-start.11 = (f32[2,8,8,128]{3,2,1,0:T(8,128)}, f32[2,8,8,128]{3,2,1,0:T(8,128)S(1)}, u32[]{:S(2)}, u32[]{:S(2)}) collective-permute-start(f32[2,8,8,128]{3,2,1,0:T(8,128)} %get-tuple-element.64), channel_id=1, source_target_pairs={{96,0},{192,96},{288,192},{384,288},{480,384},{576,480},{672,576},... | collective-permute-start | bytes 196616 | tf_op jit(solution)/shard_map/ppermute | solution.py:21
  77.0 3.4 %copy-start.6 = (f32[2,8,8,128]{3,2,1,0:T(8,128)}, f32[2,8,8,128]{3,2,1,0:T(8,128)S(1)}, u32[]{:S(2)}) copy-start(f32[2,8,8,128]{3,2,1,0:T(8,128)S(1)} %collective-permute-done.10.low) | copy-start | bytes 196612
  82.7 6.6 %collective-permute-start.12 = (f32[10,2,8,128]{3,2,1,0:T(8,128)}, f32[10,2,8,128]{3,2,1,0:T(8,128)S(1)}, u32[]{:S(2)}, u32[]{:S(2)}) collective-permute-start(f32[10,2,8,128]{3,2,1,0:T(8,128)} %get-tuple-element.65), channel_id=1, source_target_pairs={{0,12},{12,24},{24,36},{36,48},{48,60},{60,72},{72,84},{1,13},{13,... | collective-permute-start | bytes 245768 | tf_op jit(solution)/shard_map/ppermute | solution.py:21
  87.6 5.7 %collective-permute-start.13 = (f32[10,2,8,128]{3,2,1,0:T(8,128)}, f32[10,2,8,128]{3,2,1,0:T(8,128)S(1)}, u32[]{:S(2)}, u32[]{:S(2)}) collective-permute-start(f32[10,2,8,128]{3,2,1,0:T(8,128)} %get-tuple-element.66), channel_id=1, source_target_pairs={{12,0},{24,12},{36,24},{48,36},{60,48},{72,60},{84,72},{13,1},{25,... | collective-permute-start | bytes 245768 | tf_op jit(solution)/shard_map/ppermute | solution.py:21
  89.3 3.9 %copy-start.9 = (f32[10,2,8,128]{3,2,1,0:T(8,128)}, f32[10,2,8,128]{3,2,1,0:T(8,128)S(1)}, u32[]{:S(2)}) copy-start(f32[10,2,8,128]{3,2,1,0:T(8,128)S(1)} %collective-permute-done.12.below) | copy-start | bytes 245764
  93.2 0.6 copy-start.11
  98.3 6.7 %collective-permute-start.14 = (f32[10,2,8,128]{3,2,1,0:T(8,128)}, f32[10,2,8,128]{3,2,1,0:T(8,128)S(1)}, u32[]{:S(2)}, u32[]{:S(2)}) collective-permute-start(f32[10,2,8,128]{3,2,1,0:T(8,128)} %get-tuple-element.68), channel_id=1, source_target_pairs={{0,12},{12,24},{24,36},{36,48},{48,60},{60,72},{72,84},{1,13},{13,... | collective-permute-start | bytes 245768 | tf_op jit(solution)/shard_map/ppermute | solution.py:21
  101.6 6.4 %collective-permute-start.15 = (f32[10,2,8,128]{3,2,1,0:T(8,128)}, f32[10,2,8,128]{3,2,1,0:T(8,128)S(1)}, u32[]{:S(2)}, u32[]{:S(2)}) collective-permute-start(f32[10,2,8,128]{3,2,1,0:T(8,128)} %get-tuple-element.69), channel_id=1, source_target_pairs={{12,0},{24,12},{36,24},{48,36},{60,48},{72,60},{84,72},{13,1},{25,... | collective-permute-start | bytes 245768 | tf_op jit(solution)/shard_map/ppermute | solution.py:21
  105.0 3.1 %copy-start = (f32[10,2,8,128]{3,2,1,0:T(8,128)}, f32[10,2,8,128]{3,2,1,0:T(8,128)S(1)}, u32[]{:S(2)}) copy-start(f32[10,2,8,128]{3,2,1,0:T(8,128)S(1)} %collective-permute-done.14.below) | copy-start | bytes 245764
  108.0 0.6 copy-start.1
  110.3 7.0 %collective-permute-start.16 = (f32[2,8,8,128]{3,2,1,0:T(8,128)}, f32[2,8,8,128]{3,2,1,0:T(8,128)S(1)}, u32[]{:S(2)}, u32[]{:S(2)}) collective-permute-start(f32[2,8,8,128]{3,2,1,0:T(8,128)} %get-tuple-element.75), channel_id=1, source_target_pairs={{0,96},{96,192},{192,288},{288,384},{384,480},{480,576},{576,672},... | collective-permute-start | bytes 196616 | tf_op jit(solution)/shard_map/ppermute | solution.py:21
  114.7 5.8 %collective-permute-start.17 = (f32[2,8,8,128]{3,2,1,0:T(8,128)}, f32[2,8,8,128]{3,2,1,0:T(8,128)S(1)}, u32[]{:S(2)}, u32[]{:S(2)}) collective-permute-start(f32[2,8,8,128]{3,2,1,0:T(8,128)} %get-tuple-element.76), channel_id=1, source_target_pairs={{96,0},{192,96},{288,192},{384,288},{480,384},{576,480},{672,576},... | collective-permute-start | bytes 196616 | tf_op jit(solution)/shard_map/ppermute | solution.py:21
  117.3 3.3 %copy-start.13 = (f32[2,8,8,128]{3,2,1,0:T(8,128)}, f32[2,8,8,128]{3,2,1,0:T(8,128)S(1)}, u32[]{:S(2)}) copy-start(f32[2,8,8,128]{3,2,1,0:T(8,128)S(1)} %collective-permute-done.16.low) | copy-start | bytes 196612
  (4 other events, 2.5 us)

commit v2 on v1

--- a/solution.py
+++ b/solution.py
@@ -11,6 +11,8 @@
 HIGHEST = lax.Precision.HIGHEST
 LANES = 128
 REACH = 4
+SMEM = pl.BlockSpec(memory_space=pltpu.SMEM)
+VMEM = pl.BlockSpec(memory_space=pltpu.VMEM)
 CHUNKS = ((0, 24), (24, 24), (48, 24), (72, 28))
 
 
@@ -47,6 +49,10 @@
     return np.where(np.eye(8) > 0, np.eye(8) * end_values[None, :], off_diagonal)
 
 
+def near(*arrays):
+    return [pltpu.with_memory_space_constraint(array, pltpu.VMEM) for array in arrays]
+
+
 def own_lanes(count):
     lane = lax.broadcasted_iota(jnp.int32, (1, LANES), 1)
     return (lane >= REACH) & (lane < REACH + count)
@@ -89,9 +95,11 @@
 def second_edges(field, low, high, shared):
     return pl.pallas_call(
         functools.partial(second_edges_kernel, shared),
-        out_shape=[jax.ShapeDtypeStruct((10, 2, 8, LANES), jnp.float32)] * 2,
+        out_shape=[pltpu.VMEM((10, 2, 8, LANES), jnp.float32)] * 2,
+        in_specs=[VMEM] * 3,
+        out_specs=[VMEM] * 2,
         name="second_edges",
-    )(field, low, high)
+    )(*near(field, low, high))
 
 
 def solve_kernel(count, shared, field, low, high, below, above, table, valid, *refs):
@@ -169,24 +177,26 @@
 
 
 def block_solve(field, low, high, below, above, table, valid, count, shared):
-    row = jax.ShapeDtypeStruct((1, LANES), jnp.float32)
-    edge = jax.ShapeDtypeStruct((10, 2, 8, LANES), jnp.float32)
+    row = pltpu.VMEM((1, LANES), jnp.float32)
+    edge = pltpu.VMEM((10, 2, 8, LANES), jnp.float32)
     outs = [
-        jax.ShapeDtypeStruct((10, 10, 8, LANES), jnp.float32),
-        jax.ShapeDtypeStruct((4, 10, 8, LANES), jnp.float32),
+        pltpu.VMEM((10, 10, 8, LANES), jnp.float32),
+        pltpu.VMEM((4, 10, 8, LANES), jnp.float32),
         edge,
         edge,
         row,
     ]
     if shared:
-        outs += [row, jax.ShapeDtypeStruct((512, LANES), jnp.float32)]
+        outs += [row, pltpu.VMEM((512, LANES), jnp.float32)]
     return pl.pallas_call(
         functools.partial(solve_kernel, count, shared),
         out_shape=outs,
         scratch_shapes=[pltpu.VMEM((1040, LANES), jnp.float32)] * 3
         + [pltpu.VMEM((104, LANES), jnp.float32)],
+        in_specs=[VMEM] * 7,
+        out_specs=[VMEM] * len(outs),
         name="block_solve_shared" if shared else "block_solve_first",
-    )(field, low, high, below, above, table, valid)
+    )(*near(field, low, high, below, above, table, valid))
 
 
 def folded_second(values, a, y, at, below, above):
@@ -208,9 +218,11 @@
 def first_edges(rims, below, above):
     return pl.pallas_call(
         first_edges_kernel,
-        out_shape=[jax.ShapeDtypeStruct((2, 8, 8, LANES), jnp.float32)] * 2,
+        out_shape=[pltpu.VMEM((2, 8, 8, LANES), jnp.float32)] * 2,
+        in_specs=[VMEM] * 3,
+        out_specs=[VMEM] * 2,
         name="first_edges",
-    )(rims, below, above)
+    )(*near(rims, below, above))
 
 
 def both_ways(nodes, metric, derivative):
@@ -286,11 +298,13 @@
     return pl.pallas_call(
         own_lines_kernel,
         out_shape=[
-            jax.ShapeDtypeStruct((512, LANES), jnp.float32),
-            jax.ShapeDtypeStruct((2048, LANES), jnp.float32),
+            pltpu.VMEM((512, LANES), jnp.float32),
+            pltpu.VMEM((2048, LANES), jnp.float32),
         ],
+        in_specs=[VMEM] * 2,
+        out_specs=[VMEM] * 2,
         name="own_lines",
-    )(right_side, geometry)
+    )(*near(right_side, geometry))
 
 
 def end_lines_kernel(count, with_edges, ends, own, out, *edges):
@@ -304,14 +318,16 @@
 
 
 def end_lines(ends, own, count, with_edges):
-    outs = [jax.ShapeDtypeStruct(own.shape, jnp.float32)]
+    outs = [pltpu.VMEM(own.shape, jnp.float32)]
     if with_edges:
-        outs += [jax.ShapeDtypeStruct((2, 8, 8, LANES), jnp.float32)] * 2
+        outs += [pltpu.VMEM((2, 8, 8, LANES), jnp.float32)] * 2
     return pl.pallas_call(
         functools.partial(end_lines_kernel, count, with_edges),
         out_shape=outs,
+        in_specs=[VMEM] * 2,
+        out_specs=[VMEM] * len(outs),
         name="end_lines_field" if with_edges else "end_lines_metric",
-    )(ends, own)
+    )(*near(ends, own))
 
 
 def apply_local(derivative, folded, below, above, low, high, geometry, field, image):
@@ -362,13 +378,15 @@
 
 
 def first_operator(folded, below, above, low, high, geometry, count):
-    full = jax.ShapeDtypeStruct((512, LANES), jnp.float32)
-    edge = jax.ShapeDtypeStruct((2, 8, 8, LANES), jnp.float32)
+    full = pltpu.VMEM((512, LANES), jnp.float32)
+    edge = pltpu.VMEM((2, 8, 8, LANES), jnp.float32)
     return pl.pallas_call(
         functools.partial(first_operator_kernel, count, derivative_table()),
-        out_shape=[full, full, edge, edge, jax.ShapeDtypeStruct((1, LANES), jnp.float32)],
+        out_shape=[full, full, edge, edge, pltpu.VMEM((1, LANES), jnp.float32)],
+        in_specs=[VMEM] * 6,
+        out_specs=[VMEM] * 5,
         name="first_operator",
-    )(folded, below, above, low, high, geometry)
+    )(*near(folded, below, above, low, high, geometry))
 
 
 def second_operator_kernel(
@@ -411,29 +429,23 @@
     last = jnp.sum(
         jnp.where(line == across, both[64:, LANES - 1 : LANES], 0.0), axis=0, keepdims=True
     )
-    target = lax.broadcasted_iota(jnp.int32, payload.shape, 0)
-    me = spot[2]
-    payload[...] = scalars + jnp.where(
-        target == me + 1, last, jnp.where(target == me - 1, first, 0.0)
-    )
-
-
-SMEM = pl.BlockSpec(memory_space=pltpu.SMEM)
-VMEM = pl.BlockSpec(memory_space=pltpu.VMEM)
+    for target in range(payload.shape[0]):
+        end = jnp.where(target == spot[2] + 1, last, jnp.where(target == spot[2] - 1, first, 0.0))
+        payload[target] = scalars + end
 
 
 def second_operator(spot, folded, below, above, low, high, geometry, sums, count, devices):
     return pl.pallas_call(
         functools.partial(second_operator_kernel, count, derivative_table()),
         out_shape=[
-            jax.ShapeDtypeStruct((128, LANES), jnp.float32),
-            jax.ShapeDtypeStruct((devices, LANES), jnp.float32),
+            pltpu.VMEM((128, LANES), jnp.float32),
+            pltpu.VMEM((devices, 1, LANES), jnp.float32),
         ],
         in_specs=[SMEM] + [VMEM] * 10,
         out_specs=[VMEM, VMEM],
         scratch_shapes=[pltpu.VMEM((512, LANES), jnp.float32)] * 2,
         name="second_operator",
-    )(spot, folded, below, above, low, high, geometry, *sums)
+    )(spot, *near(folded, below, above, low, high, geometry, *sums))
 
 
 def lines_kernel(count, one, two, lines):
@@ -443,9 +455,11 @@
 def as_lines(one, two, count):
     return pl.pallas_call(
         functools.partial(lines_kernel, count),
-        out_shape=jax.ShapeDtypeStruct((128, LANES), jnp.float32),
+        out_shape=pltpu.VMEM((128, LANES), jnp.float32),
+        in_specs=[VMEM] * 2,
+        out_specs=VMEM,
         name="as_lines",
-    )(one, two)
+    )(*near(one, two))
 
 
 def combine(columns):
@@ -464,8 +478,10 @@
 NEIGHBOURS = [(dx, dy) for dx in (-1, 0, 1) for dy in (-1, 0, 1) if (dx, dy) != (0, 0)]
 
 
-def middle_kernel(sizes, spot, gathered, lines, image, out):
-    rows = gathered[...]
+def middle_kernel(sizes, spot, gathered, lines, image, out, joined):
+    for device in range(gathered.shape[0]):
+        joined[pl.ds(device, 1), :] = gathered[device]
+    rows = joined[...]
     values = combine([rows[:, 64 + i : 65 + i] for i in range(5)])
     source = lax.broadcasted_iota(jnp.int32, rows.shape, 0)
     before = jnp.sum(jnp.where(source == spot[2] - 1, rows, 0.0), axis=0, keepdims=True)
@@ -510,13 +526,14 @@
     return pl.pallas_call(
         functools.partial(middle_kernel, sizes),
         out_shape=[
-            jax.ShapeDtypeStruct((64, LANES), jnp.float32),
-            jax.ShapeDtypeStruct((8 * sizes[0] * sizes[1], LANES), jnp.float32),
+            pltpu.VMEM((64, LANES), jnp.float32),
+            pltpu.VMEM((8 * sizes[0] * sizes[1], LANES), jnp.float32),
         ],
         in_specs=[SMEM, VMEM, VMEM],
         out_specs=[VMEM, VMEM],
+        scratch_shapes=[pltpu.VMEM((gathered.shape[0], LANES), jnp.float32)],
         name="middle",
-    )(spot, gathered, lines)
+    )(spot, *near(gathered, lines))
 
 
 def finish_kernel(
@@ -569,7 +586,7 @@
         out_specs=[VMEM, VMEM],
         scratch_shapes=[pltpu.VMEM((64, LANES), jnp.float32)],
         name="finish",
-    )(spot, gathered, image, second, first, right_side)
+    )(spot, *near(gathered, image, second, first, right_side))
 
 
 def exchange(rows, axes):

time: 174 us -> 153 us (0.88)
  Pallas kernels: 35.8 us -> 12.9 us
  local copies, waits for them, and re-layouts: 7.04 us -> 10.5 us
  other arithmetic: 4.21 us -> 2.46 us
    pallas_call x5, Pallas kernels: 10.1 us -> 2.29 us  [the longest x1 1.15 us: middle(): pl.pallas_call(functools.partial(middle_kernel, sizes), out_shape=[pltpu....]
    unnamed x39 -> x40, local copies, waits for them, and re-layouts: 5.68 us -> 9.85 us
    pallas_call x2, Pallas kernels: 5.04 us -> 1.01 us  [end_lines(): pl.pallas_call(functools.partial(end_lines_kernel, count, with_edges), ou...]
    pallas_call x2, Pallas kernels: 8.74 us -> 4.93 us  [block_solve(): pl.pallas_call(functools.partial(solve_kernel, count, shared), out_shape=...]
    pallas_call x2, Pallas kernels: 3.33 us -> 0.03 us  [second_edges(): pl.pallas_call(functools.partial(second_edges_kernel, shared), out_shape=...]
    pallas_call x1, Pallas kernels: 3.19 us -> 0.98 us  [first_operator(): pl.pallas_call(functools.partial(first_operator_kernel, count, derivative...]
  transfers between devices with their start and end apart: 18 -> 18, of which waited for: 11 -> 11; matrix products, arithmetic and copies ran while one was open for 2% -> 1% of each run, Pallas kernels for 4% -> 1%
where the time goes in v2:
time: 153 us; the launch traced here: 152 us
  starting transfers between devices  51.9 us (34%)
  blocking collectives  42.1 us (28%)
  waiting for transfers between devices  30.6 us (20%)
  Pallas kernels  12.9 us (8%)
  local copies, waits for them, and re-layouts  10.5 us (7%)
  other arithmetic  2.46 us (2%)
    all_to_all x2, blocking collectives, exchange(): return lax.all_to_all(rows, axes, 0, 0, tiled=True)  42.1 us
    ppermute x9, starting transfers between devices, swap(): lax.ppermute(forward_part, axis, forward)  34 us
    ppermute x9, waiting for transfers between devices, swap(): lax.ppermute(backward_part, axis, backward)  29 us
    ppermute x9, starting transfers between devices, swap(): lax.ppermute(backward_part, axis, backward)  17.9 us
    unnamed x40, local copies, waits for them, and re-layouts  9.85 us
    pallas_call x2, Pallas kernels, block_solve(): pl.pallas_call(functools.partial(solve_kernel, count, shared), out_shape=...  4.93 us
  transfers between devices with their start and end apart: 18, of which 11 were waited for; matrix products, arithmetic and copies ran while one was open for 1% of the time, Pallas kernels for 1%

profile of v2, /device:TPU:1, one launch (start us, length us, event | category | flops | bytes accessed | tf_op | source)
XLA Modules:
  0.0 151.9 jit_solution(17269474346365788127)
XLA Ops:
  2.5 5.0 %collective-permute-start = (f32[328,32]{1,0:T(8,128)S(1)}, f32[328,32]{1,0:T(8,128)S(1)}, u32[]{:S(2)}, u32[]{:S(2)}) collective-permute-start(f32[328,32]{1,0:T(8,128)S(1)} %get-tuple-element.88), channel_id=1, source_target_pairs={{0,1},{1,2},{2,3},{3,4},{4,5},{5,6},{6,7},{7,8},{8,9},{9,10},{10,1... | collective-permute-start | bytes 125960 | tf_op jit(solution)/shard_map/ppermute | solution.py:23
  7.5 1.3 collective-permute-start.1
  9.9 4.4 %collective-permute-done.1 = f32[328,32]{1,0:T(8,128)S(1)} collective-permute-done((f32[328,32]{1,0:T(8,128)S(1)}, f32[328,32]{1,0:T(8,128)S(1)}, u32[]{:S(2)}, u32[]{:S(2)}) %collective-permute-start.1) | collective-permute-done | bytes 42016 | tf_op jit(solution)/shard_map/ppermute | solution.py:23
  14.6 5.5 %collective-permute-start.2 = (f32[2,8,8,128]{3,2,1,0:T(8,128)S(1)}, f32[2,8,8,128]{3,2,1,0:T(8,128)S(1)}, u32[]{:S(2)}, u32[]{:S(2)}) collective-permute-start(f32[2,8,8,128]{3,2,1,0:T(8,128)S(1)} %get-tuple-element.47), channel_id=1, source_target_pairs={{0,96},{96,192},{192,288},{288,384},{384,480},{480,576},{576,672},... | collective-permute-start | bytes 196616 | tf_op jit(solution)/shard_map/ppermute | solution.py:23
  20.1 5.2 %collective-permute-start.3 = (f32[2,8,8,128]{3,2,1,0:T(8,128)S(1)}, f32[2,8,8,128]{3,2,1,0:T(8,128)S(1)}, u32[]{:S(2)}, u32[]{:S(2)}) collective-permute-start(f32[2,8,8,128]{3,2,1,0:T(8,128)S(1)} %get-tuple-element.48), channel_id=1, source_target_pairs={{96,0},{192,96},{288,192},{384,288},{480,384},{576,480},{672,576},... | collective-permute-start | bytes 196616 | tf_op jit(solution)/shard_map/ppermute | solution.py:23
  27.8 1.3 collective-permute-start.4
  29.1 1.3 collective-permute-start.5
  30.9 4.2 %collective-permute-done.5.above = f32[10,2,8,128]{3,2,1,0:T(8,128)S(1)} collective-permute-done((f32[10,2,8,128]{3,2,1,0:T(8,128)S(1)}, f32[10,2,8,128]{3,2,1,0:T(8,128)S(1)}, u32[]{:S(2)}, u32[]{:S(2)}) %collective-permute-start.5) | collective-permute-done | bytes 81952 | tf_op jit(solution)/shard_map/ppermute | solution.py:23
  35.2 2.4 %block_solve_first.1 = (f32[10,10,8,128]{3,2,1,0:T(8,128)S(1)}, f32[4,10,8,128]{3,2,1,0:T(8,128)S(1)}, f32[10,2,8,128]{3,2,1,0:T(8,128)S(1)}, f32[10,2,8,128]{3,2,1,0:T(8,128)S(1)}, f32[1,128]{1,0:T(1,128)S(1)}) custom-call(f32[512,128]{1,0:T(8,128)S(1)} %get-tuple-element.46.field, f32[2,8,8,128]{3,2,1,0:T(8,128)S(1)} %collective-permute-done.2.low, ...), custom_call_target="tpu_custom_call" | custom-call | tf_op jit(solution)/shard_map/block_solve_first/pallas_call | solution.py:191
  38.3 2.1 %collective-permute-start.6 = (f32[10,2,8,128]{3,2,1,0:T(8,128)S(1)}, f32[10,2,8,128]{3,2,1,0:T(8,128)S(1)}, u32[]{:S(2)}, u32[]{:S(2)}) collective-permute-start(f32[10,2,8,128]{3,2,1,0:T(8,128)S(1)} %get-tuple-element.56), channel_id=1, source_target_pairs={{0,12},{12,24},{24,36},{36,48},{48,60},{60,72},{72,84},{1,13},{13,... | collective-permute-start | bytes 245768 | tf_op jit(solution)/shard_map/ppermute | solution.py:23
  40.5 1.3 collective-permute-start.7
  42.7 4.0 %collective-permute-done.7.above = f32[10,2,8,128]{3,2,1,0:T(8,128)S(1)} collective-permute-done((f32[10,2,8,128]{3,2,1,0:T(8,128)S(1)}, f32[10,2,8,128]{3,2,1,0:T(8,128)S(1)}, u32[]{:S(2)}, u32[]{:S(2)}) %collective-permute-start.7) | collective-permute-done | bytes 81952 | tf_op jit(solution)/shard_map/ppermute | solution.py:23
  47.3 5.4 %collective-permute-start.8 = (f32[2,8,8,128]{3,2,1,0:T(8,128)S(1)}, f32[2,8,8,128]{3,2,1,0:T(8,128)S(1)}, u32[]{:S(2)}, u32[]{:S(2)}) collective-permute-start(f32[2,8,8,128]{3,2,1,0:T(8,128)S(1)} %get-tuple-element.59), channel_id=1, source_target_pairs={{0,96},{96,192},{192,288},{288,384},{384,480},{480,576},{576,672},... | collective-permute-start | bytes 196616 | tf_op jit(solution)/shard_map/ppermute | solution.py:23
  52.8 1.9 %collective-permute-start.9 = (f32[2,8,8,128]{3,2,1,0:T(8,128)S(1)}, f32[2,8,8,128]{3,2,1,0:T(8,128)S(1)}, u32[]{:S(2)}, u32[]{:S(2)}) collective-permute-start(f32[2,8,8,128]{3,2,1,0:T(8,128)S(1)} %get-tuple-element.60), channel_id=1, source_target_pairs={{96,0},{192,96},{288,192},{384,288},{480,384},{576,480},{672,576},... | collective-permute-start | bytes 196616 | tf_op jit(solution)/shard_map/ppermute | solution.py:23
  54.7 3.6 %collective-permute-done.9.high = f32[2,8,8,128]{3,2,1,0:T(8,128)S(1)} collective-permute-done((f32[2,8,8,128]{3,2,1,0:T(8,128)S(1)}, f32[2,8,8,128]{3,2,1,0:T(8,128)S(1)}, u32[]{:S(2)}, u32[]{:S(2)}) %collective-permute-start.9) | collective-permute-done | bytes 65568 | tf_op jit(solution)/shard_map/ppermute | solution.py:23
  63.1 1.9 %collective-permute-start.10 = (f32[2,8,8,128]{3,2,1,0:T(8,128)S(1)}, f32[2,8,8,128]{3,2,1,0:T(8,128)S(1)}, u32[]{:S(2)}, u32[]{:S(2)}) collective-permute-start(f32[2,8,8,128]{3,2,1,0:T(8,128)S(1)} %get-tuple-element.63), channel_id=1, source_target_pairs={{0,96},{96,192},{192,288},{288,384},{384,480},{480,576},{576,672},... | collective-permute-start | bytes 196616 | tf_op jit(solution)/shard_map/ppermute | solution.py:23
  65.1 2.4 %collective-permute-start.11 = (f32[2,8,8,128]{3,2,1,0:T(8,128)S(1)}, f32[2,8,8,128]{3,2,1,0:T(8,128)S(1)}, u32[]{:S(2)}, u32[]{:S(2)}) collective-permute-start(f32[2,8,8,128]{3,2,1,0:T(8,128)S(1)} %get-tuple-element.64), channel_id=1, source_target_pairs={{96,0},{192,96},{288,192},{384,288},{480,384},{576,480},{672,576},... | collective-permute-start | bytes 196616 | tf_op jit(solution)/shard_map/ppermute | solution.py:23
  67.5 3.2 %collective-permute-done.11.high = f32[2,8,8,128]{3,2,1,0:T(8,128)S(1)} collective-permute-done((f32[2,8,8,128]{3,2,1,0:T(8,128)S(1)}, f32[2,8,8,128]{3,2,1,0:T(8,128)S(1)}, u32[]{:S(2)}, u32[]{:S(2)}) %collective-permute-start.11) | collective-permute-done | bytes 65568 | tf_op jit(solution)/shard_map/ppermute | solution.py:23
  70.7 4.8 %collective-permute-start.12 = (f32[10,2,8,128]{3,2,1,0:T(8,128)S(1)}, f32[10,2,8,128]{3,2,1,0:T(8,128)S(1)}, u32[]{:S(2)}, u32[]{:S(2)}) collective-permute-start(f32[10,2,8,128]{3,2,1,0:T(8,128)S(1)} %get-tuple-element.65), channel_id=1, source_target_pairs={{0,12},{12,24},{24,36},{36,48},{48,60},{60,72},{72,84},{1,13},{13,... | collective-permute-start | bytes 245768 | tf_op jit(solution)/shard_map/ppermute | solution.py:23
  75.5 1.3 collective-permute-start.13
  77.0 4.0 %collective-permute-done.13.above = f32[10,2,8,128]{3,2,1,0:T(8,128)S(1)} collective-permute-done((f32[10,2,8,128]{3,2,1,0:T(8,128)S(1)}, f32[10,2,8,128]{3,2,1,0:T(8,128)S(1)}, u32[]{:S(2)}, u32[]{:S(2)}) %collective-permute-start.13) | collective-permute-done | bytes 81952 | tf_op jit(solution)/shard_map/ppermute | solution.py:23
  81.0 2.6 %block_solve_shared.1 = (f32[10,10,8,128]{3,2,1,0:T(8,128)S(1)}, f32[4,10,8,128]{3,2,1,0:T(8,128)S(1)}, f32[10,2,8,128]{3,2,1,0:T(8,128)S(1)}, f32[10,2,8,128]{3...) custom-call(f32[512,128]{1,0:T(8,128)S(1)} %get-tuple-element.62.field, ...), custom_call_target="tpu_custom_call" | custom-call | tf_op jit(solution)/shard_map/block_solve_shared/pallas_call | solution.py:191
  84.3 3.4 %collective-permute-start.14 = (f32[10,2,8,128]{3,2,1,0:T(8,128)S(1)}, f32[10,2,8,128]{3,2,1,0:T(8,128)S(1)}, u32[]{:S(2)}, u32[]{:S(2)}) collective-permute-start(f32[10,2,8,128]{3,2,1,0:T(8,128)S(1)} %get-tuple-element.68), channel_id=1, source_target_pairs={{0,12},{12,24},{24,36},{36,48},{48,60},{60,72},{72,84},{1,13},{13,... | collective-permute-start | bytes 245768 | tf_op jit(solution)/shard_map/ppermute | solution.py:23
  87.6 1.3 collective-permute-start.15
  91.2 2.5 %collective-permute-done.15.above = f32[10,2,8,128]{3,2,1,0:T(8,128)S(1)} collective-permute-done((f32[10,2,8,128]{3,2,1,0:T(8,128)S(1)}, f32[10,2,8,128]{3,2,1,0:T(8,128)S(1)}, u32[]{:S(2)}, u32[]{:S(2)}) %collective-permute-start.15) | collective-permute-done | bytes 81952 | tf_op jit(solution)/shard_map/ppermute | solution.py:23
  93.8 4.6 %collective-permute-start.16 = (f32[2,8,8,128]{3,2,1,0:T(8,128)S(1)}, f32[2,8,8,128]{3,2,1,0:T(8,128)S(1)}, u32[]{:S(2)}, u32[]{:S(2)}) collective-permute-start(f32[2,8,8,128]{3,2,1,0:T(8,128)S(1)} %get-tuple-element.75), channel_id=1, source_target_pairs={{0,96},{96,192},{192,288},{288,384},{384,480},{480,576},{576,672},... | collective-permute-start | bytes 196616 | tf_op jit(solution)/shard_map/ppermute | solution.py:23
  98.3 1.9 %collective-permute-start.17 = (f32[2,8,8,128]{3,2,1,0:T(8,128)S(1)}, f32[2,8,8,128]{3,2,1,0:T(8,128)S(1)}, u32[]{:S(2)}, u32[]{:S(2)}) collective-permute-start(f32[2,8,8,128]{3,2,1,0:T(8,128)S(1)} %get-tuple-element.76), channel_id=1, source_target_pairs={{96,0},{192,96},{288,192},{384,288},{480,384},{576,480},{672,576},... | collective-permute-start | bytes 196616 | tf_op jit(solution)/shard_map/ppermute | solution.py:23
  100.9 3.0 %collective-permute-done.17.high = f32[2,8,8,128]{3,2,1,0:T(8,128)S(1)} collective-permute-done((f32[2,8,8,128]{3,2,1,0:T(8,128)S(1)}, f32[2,8,8,128]{3,2,1,0:T(8,128)S(1)}, u32[]{:S(2)}, u32[]{:S(2)}) %collective-permute-start.17) | collective-permute-done | bytes 65568 | tf_op jit(solution)/shard_map/ppermute | solution.py:23
  104.9 2.1 %second_operator.1 = (f32[128,128]{1,0:T(8,128)S(1)}, f32[12,1,128]{2,1,0:T(1,128)S(1)}) custom-call(s32[3]{0:T(128)} %pad_add_fusion.spot, f32[10,10,8,128]{3,2,1,0:T(8,128)S(1)} %copy-done.6, f32[10,2,8,128]{3,2,1,0:T(8,128)S(1)} %collective-permute-done.14.below, f32[10,2,8,128]{3,2,1,0:T(8,128)S(1)} %collective-permute-done.15.above, ...), custom_call_target="tpu_custom_call" | custom-call | tf_op jit(solution)/shard_map/second_operator/pallas_call | solution.py:438
  107.0 23.3 %all_to_all.16.gathered = f32[12,1,128]{2,1,0:T(1,128)S(1)} all-to-all(f32[12,1,128]{2,1,0:T(1,128)S(1)} %get-tuple-element.81), channel_id=1, replica_groups=mesh['gx'=8,'gy'=8,'gz'=12] {'gz'}, dimensions={0} | all-to-all | bytes 12288 | tf_op jit(solution)/shard_map/all_to_all | solution.py:593
  131.4 18.8 %all_to_all.17 = f32[64,8,128]{2,1,0:T(8,128)S(1)} all-to-all(f32[64,8,128]{2,1,0:T(8,128)S(1)} %bitcast.23), channel_id=1, replica_groups=mesh['gx'=8,'gy'=8,'gz'=12] {'gx','gy'}, dimensions={0} | all-to-all | bytes 524288 | tf_op jit(solution)/shard_map/all_to_all | solution.py:593
  150.2 1.6 %finish.1 = (f32[64,128]{1,0:T(8,128)}, f32[64,128]{1,0:T(8,128)}) custom-call(s32[3]{0:T(128)} %pad_add_fusion.spot, f32[512,128]{1,0:T(8,128)S(1)} %bitcast.17, f32[64,128]{1,0:T(8,128)S(1)} %get-tuple-element.84.image, f32[128,128]{1,0:T(8,128)S(1)} %get-tuple-element.82.lines.second, f32[128,128]{1,0:T(8,128)S(1)} %as_lines.1.first, f32[64,128]{1,0:T(8,128)S(1)} %bitcast.22), custom_call_target="tpu_custom_call" | custom-call | tf_op jit(solution)/shard_map/finish/pallas_call | solution.py:582
  (79 shorter events, 19.2 us)
Async XLA Ops:
  2.4 6.4 %copy-start.4 = (f32[4,8,8,128]{3,2,1,0:T(8,128)S(1)}, f32[4,8,8,128]{3,2,1,0:T(8,128)}, u32[]{:S(2)}) copy-start(f32[4,8,8,128]{3,2,1,0:T(8,128)} %param.6) | copy-start | bytes 393220
  2.4 6.4 %copy-start.11 = (f32[8,8,128]{2,1,0:T(8,128)S(1)}, f32[8,8,128]{2,1,0:T(8,128)}, u32[]{:S(2)}) copy-start(f32[8,8,128]{2,1,0:T(8,128)} %param.5) | copy-start | bytes 98308
  2.4 7.2 %copy-start.18 = (f32[32,3,10]{0,1,2:T(4,128)S(1)}, f32[32,3,10]{0,1,2:T(4,128)}, u32[]{:S(2)}) copy-start(f32[32,3,10]{0,1,2:T(4,128)} %param.9) | copy-start | bytes 11524
  2.5 7.2 %copy-start.17 = (f32[32,3,10,10]{0,1,3,2:T(4,128)S(1)}, f32[32,3,10,10]{0,1,3,2:T(4,128)}, u32[]{:S(2)}) copy-start(f32[32,3,10,10]{0,1,3,2:T(4,128)} %param.8) | copy-start | bytes 115204
  2.5 7.3 %collective-permute-start = (f32[328,32]{1,0:T(8,128)S(1)}, f32[328,32]{1,0:T(8,128)S(1)}, u32[]{:S(2)}, u32[]{:S(2)}) collective-permute-start(f32[328,32]{1,0:T(8,128)S(1)} %get-tuple-element.88), channel_id=1, source_target_pairs={{0,1},{1,2},{2,3},{3,4},{4,5},{5,6},{6,7},{7,8},{8,9},{9,10},{10,1... | collective-permute-start | bytes 125960 | tf_op jit(solution)/shard_map/ppermute | solution.py:23
  7.5 6.7 %collective-permute-start.1 = (f32[328,32]{1,0:T(8,128)S(1)}, f32[328,32]{1,0:T(8,128)S(1)}, u32[]{:S(2)}, u32[]{:S(2)}) collective-permute-start(f32[328,32]{1,0:T(8,128)S(1)} %get-tuple-element.89), channel_id=1, source_target_pairs={{1,0},{2,1},{3,2},{4,3},{5,4},{6,5},{7,6},{8,7},{9,8},{10,9},{11,1... | collective-permute-start | bytes 125960 | tf_op jit(solution)/shard_map/ppermute | solution.py:23
  14.6 13.2 %collective-permute-start.2 = (f32[2,8,8,128]{3,2,1,0:T(8,128)S(1)}, f32[2,8,8,128]{3,2,1,0:T(8,128)S(1)}, u32[]{:S(2)}, u32[]{:S(2)}) collective-permute-start(f32[2,8,8,128]{3,2,1,0:T(8,128)S(1)} %get-tuple-element.47), channel_id=1, source_target_pairs={{0,96},{96,192},{192,288},{288,384},{384,480},{480,576},{576,672},... | collective-permute-start | bytes 196616 | tf_op jit(solution)/shard_map/ppermute | solution.py:23
  20.1 7.7 %collective-permute-start.3 = (f32[2,8,8,128]{3,2,1,0:T(8,128)S(1)}, f32[2,8,8,128]{3,2,1,0:T(8,128)S(1)}, u32[]{:S(2)}, u32[]{:S(2)}) collective-permute-start(f32[2,8,8,128]{3,2,1,0:T(8,128)S(1)} %get-tuple-element.48), channel_id=1, source_target_pairs={{96,0},{192,96},{288,192},{384,288},{480,384},{576,480},{672,576},... | collective-permute-start | bytes 196616 | tf_op jit(solution)/shard_map/ppermute | solution.py:23
  26.0 9.2 %copy-start.2 = (f32[330,128]{1,0:T(8,128)}, f32[330,128]{1,0:T(8,128)S(1)}, u32[]{:S(2)}) copy-start(f32[330,128]{1,0:T(8,128)S(1)} %fusion.table) | copy-start | bytes 506884
  26.8 1.0 copy-start
  27.8 3.1 %collective-permute-start.4 = (f32[10,2,8,128]{3,2,1,0:T(8,128)S(1)}, f32[10,2,8,128]{3,2,1,0:T(8,128)S(1)}, u32[]{:S(2)}, u32[]{:S(2)}) collective-permute-start(f32[10,2,8,128]{3,2,1,0:T(8,128)S(1)} %get-tuple-element.52), channel_id=1, source_target_pairs={{0,12},{12,24},{24,36},{36,48},{48,60},{60,72},{72,84},{1,13},{13,... | collective-permute-start | bytes 245768 | tf_op jit(solution)/shard_map/ppermute | solution.py:23
  29.1 6.0 %collective-permute-start.5 = (f32[10,2,8,128]{3,2,1,0:T(8,128)S(1)}, f32[10,2,8,128]{3,2,1,0:T(8,128)S(1)}, u32[]{:S(2)}, u32[]{:S(2)}) collective-permute-start(f32[10,2,8,128]{3,2,1,0:T(8,128)S(1)} %get-tuple-element.53), channel_id=1, source_target_pairs={{12,0},{24,12},{36,24},{48,36},{60,48},{72,60},{84,72},{13,1},{25,... | collective-permute-start | bytes 245768 | tf_op jit(solution)/shard_map/ppermute | solution.py:23
  38.3 4.3 %collective-permute-start.6 = (f32[10,2,8,128]{3,2,1,0:T(8,128)S(1)}, f32[10,2,8,128]{3,2,1,0:T(8,128)S(1)}, u32[]{:S(2)}, u32[]{:S(2)}) collective-permute-start(f32[10,2,8,128]{3,2,1,0:T(8,128)S(1)} %get-tuple-element.56), channel_id=1, source_target_pairs={{0,12},{12,24},{24,36},{36,48},{48,60},{60,72},{72,84},{1,13},{13,... | collective-permute-start | bytes 245768 | tf_op jit(solution)/shard_map/ppermute | solution.py:23
  40.5 6.2 %collective-permute-start.7 = (f32[10,2,8,128]{3,2,1,0:T(8,128)S(1)}, f32[10,2,8,128]{3,2,1,0:T(8,128)S(1)}, u32[]{:S(2)}, u32[]{:S(2)}) collective-permute-start(f32[10,2,8,128]{3,2,1,0:T(8,128)S(1)} %get-tuple-element.57), channel_id=1, source_target_pairs={{12,0},{24,12},{36,24},{48,36},{60,48},{72,60},{84,72},{13,1},{25,... | collective-permute-start | bytes 245768 | tf_op jit(solution)/shard_map/ppermute | solution.py:23
  47.3 7.4 %collective-permute-start.8 = (f32[2,8,8,128]{3,2,1,0:T(8,128)S(1)}, f32[2,8,8,128]{3,2,1,0:T(8,128)S(1)}, u32[]{:S(2)}, u32[]{:S(2)}) collective-permute-start(f32[2,8,8,128]{3,2,1,0:T(8,128)S(1)} %get-tuple-element.59), channel_id=1, source_target_pairs={{0,96},{96,192},{192,288},{288,384},{384,480},{480,576},{576,672},... | collective-permute-start | bytes 196616 | tf_op jit(solution)/shard_map/ppermute | solution.py:23
  52.8 5.6 %collective-permute-start.9 = (f32[2,8,8,128]{3,2,1,0:T(8,128)S(1)}, f32[2,8,8,128]{3,2,1,0:T(8,128)S(1)}, u32[]{:S(2)}, u32[]{:S(2)}) collective-permute-start(f32[2,8,8,128]{3,2,1,0:T(8,128)S(1)} %get-tuple-element.60), channel_id=1, source_target_pairs={{96,0},{192,96},{288,192},{384,288},{480,384},{576,480},{672,576},... | collective-permute-start | bytes 196616 | tf_op jit(solution)/shard_map/ppermute | solution.py:23
  58.3 1.2 copy-start.1
  59.6 1.0 copy-start.8
  63.1 4.3 %collective-permute-start.10 = (f32[2,8,8,128]{3,2,1,0:T(8,128)S(1)}, f32[2,8,8,128]{3,2,1,0:T(8,128)S(1)}, u32[]{:S(2)}, u32[]{:S(2)}) collective-permute-start(f32[2,8,8,128]{3,2,1,0:T(8,128)S(1)} %get-tuple-element.63), channel_id=1, source_target_pairs={{0,96},{96,192},{192,288},{288,384},{384,480},{480,576},{576,672},... | collective-permute-start | bytes 196616 | tf_op jit(solution)/shard_map/ppermute | solution.py:23
  65.1 5.6 %collective-permute-start.11 = (f32[2,8,8,128]{3,2,1,0:T(8,128)S(1)}, f32[2,8,8,128]{3,2,1,0:T(8,128)S(1)}, u32[]{:S(2)}, u32[]{:S(2)}) collective-permute-start(f32[2,8,8,128]{3,2,1,0:T(8,128)S(1)} %get-tuple-element.64), channel_id=1, source_target_pairs={{96,0},{192,96},{288,192},{384,288},{480,384},{576,480},{672,576},... | collective-permute-start | bytes 196616 | tf_op jit(solution)/shard_map/ppermute | solution.py:23
  70.7 10.3 %copy-start.3 = (f32[330,128]{1,0:T(8,128)S(1)}, f32[330,128]{1,0:T(8,128)}, u32[]{:S(2)}) copy-start(f32[330,128]{1,0:T(8,128)} %copy-done.2) | copy-start | bytes 506884
  70.7 6.3 %collective-permute-start.12 = (f32[10,2,8,128]{3,2,1,0:T(8,128)S(1)}, f32[10,2,8,128]{3,2,1,0:T(8,128)S(1)}, u32[]{:S(2)}, u32[]{:S(2)}) collective-permute-start(f32[10,2,8,128]{3,2,1,0:T(8,128)S(1)} %get-tuple-element.65), channel_id=1, source_target_pairs={{0,12},{12,24},{24,36},{36,48},{48,60},{60,72},{72,84},{1,13},{13,... | collective-permute-start | bytes 245768 | tf_op jit(solution)/shard_map/ppermute | solution.py:23
  75.5 5.5 %collective-permute-start.13 = (f32[10,2,8,128]{3,2,1,0:T(8,128)S(1)}, f32[10,2,8,128]{3,2,1,0:T(8,128)S(1)}, u32[]{:S(2)}, u32[]{:S(2)}) collective-permute-start(f32[10,2,8,128]{3,2,1,0:T(8,128)S(1)} %get-tuple-element.66), channel_id=1, source_target_pairs={{12,0},{24,12},{36,24},{48,36},{60,48},{72,60},{84,72},{13,1},{25,... | collective-permute-start | bytes 245768 | tf_op jit(solution)/shard_map/ppermute | solution.py:23
  84.3 9.5 %copy-start.5 = (f32[10,10,8,128]{3,2,1,0:T(8,128)}, f32[10,10,8,128]{3,2,1,0:T(8,128)S(1)}, u32[]{:S(2)}) copy-start(f32[10,10,8,128]{3,2,1,0:T(8,128)S(1)} %get-tuple-element.67.folded) | copy-start | bytes 1228804
  84.3 6.9 %collective-permute-start.14 = (f32[10,2,8,128]{3,2,1,0:T(8,128)S(1)}, f32[10,2,8,128]{3,2,1,0:T(8,128)S(1)}, u32[]{:S(2)}, u32[]{:S(2)}) collective-permute-start(f32[10,2,8,128]{3,2,1,0:T(8,128)S(1)} %get-tuple-element.68), channel_id=1, source_target_pairs={{0,12},{12,24},{24,36},{36,48},{48,60},{60,72},{72,84},{1,13},{13,... | collective-permute-start | bytes 245768 | tf_op jit(solution)/shard_map/ppermute | solution.py:23
  87.6 6.1 %collective-permute-start.15 = (f32[10,2,8,128]{3,2,1,0:T(8,128)S(1)}, f32[10,2,8,128]{3,2,1,0:T(8,128)S(1)}, u32[]{:S(2)}, u32[]{:S(2)}) collective-permute-start(f32[10,2,8,128]{3,2,1,0:T(8,128)S(1)} %get-tuple-element.69), channel_id=1, source_target_pairs={{12,0},{24,12},{36,24},{48,36},{60,48},{72,60},{84,72},{13,1},{25,... | collective-permute-start | bytes 245768 | tf_op jit(solution)/shard_map/ppermute | solution.py:23
  88.9 1.0 copy-start.14
  89.9 0.9 copy-start.16
  93.8 7.1 %collective-permute-start.16 = (f32[2,8,8,128]{3,2,1,0:T(8,128)S(1)}, f32[2,8,8,128]{3,2,1,0:T(8,128)S(1)}, u32[]{:S(2)}, u32[]{:S(2)}) collective-permute-start(f32[2,8,8,128]{3,2,1,0:T(8,128)S(1)} %get-tuple-element.75), channel_id=1, source_target_pairs={{0,96},{96,192},{192,288},{288,384},{384,480},{480,576},{576,672},... | collective-permute-start | bytes 196616 | tf_op jit(solution)/shard_map/ppermute | solution.py:23
  98.3 5.6 %collective-permute-start.17 = (f32[2,8,8,128]{3,2,1,0:T(8,128)S(1)}, f32[2,8,8,128]{3,2,1,0:T(8,128)S(1)}, u32[]{:S(2)}, u32[]{:S(2)}) collective-permute-start(f32[2,8,8,128]{3,2,1,0:T(8,128)S(1)} %get-tuple-element.76), channel_id=1, source_target_pairs={{96,0},{192,96},{288,192},{384,288},{480,384},{576,480},{672,576},... | collective-permute-start | bytes 196616 | tf_op jit(solution)/shard_map/ppermute | solution.py:23
  103.9 1.0 copy-start.6
  131.4 18.8 %copy-start.12 = (f32[8,8,128]{2,1,0:T(8,128)S(1)}, f32[8,8,128]{2,1,0:T(8,128)}, u32[]{:S(2)}) copy-start(f32[8,8,128]{2,1,0:T(8,128)} %param.5) | copy-start | bytes 98308
  (5 other events, 3.7 us)

commit v3 on v2

--- a/solution.py
+++ b/solution.py
@@ -13,6 +13,7 @@
 REACH = 4
 SMEM = pl.BlockSpec(memory_space=pltpu.SMEM)
 VMEM = pl.BlockSpec(memory_space=pltpu.VMEM)
+ROOM = pltpu.CompilerParams(vmem_limit_bytes=8 << 20)
 CHUNKS = ((0, 24), (24, 24), (48, 24), (72, 28))
 
 
@@ -98,6 +99,7 @@
         out_shape=[pltpu.VMEM((10, 2, 8, LANES), jnp.float32)] * 2,
         in_specs=[VMEM] * 3,
         out_specs=[VMEM] * 2,
+        compiler_params=ROOM,
         name="second_edges",
     )(*near(field, low, high))
 
@@ -195,6 +197,7 @@
         + [pltpu.VMEM((104, LANES), jnp.float32)],
         in_specs=[VMEM] * 7,
         out_specs=[VMEM] * len(outs),
+        compiler_params=ROOM,
         name="block_solve_shared" if shared else "block_solve_first",
     )(*near(field, low, high, below, above, table, valid))
 
@@ -221,6 +224,7 @@
         out_shape=[pltpu.VMEM((2, 8, 8, LANES), jnp.float32)] * 2,
         in_specs=[VMEM] * 3,
         out_specs=[VMEM] * 2,
+        compiler_params=ROOM,
         name="first_edges",
     )(*near(rims, below, above))
 
@@ -303,6 +307,7 @@
         ],
         in_specs=[VMEM] * 2,
         out_specs=[VMEM] * 2,
+        compiler_params=ROOM,
         name="own_lines",
     )(*near(right_side, geometry))
 
@@ -326,6 +331,7 @@
         out_shape=outs,
         in_specs=[VMEM] * 2,
         out_specs=[VMEM] * len(outs),
+        compiler_params=ROOM,
         name="end_lines_field" if with_edges else "end_lines_metric",
     )(*near(ends, own))
 
@@ -385,6 +391,7 @@
         out_shape=[full, full, edge, edge, pltpu.VMEM((1, LANES), jnp.float32)],
         in_specs=[VMEM] * 6,
         out_specs=[VMEM] * 5,
+        compiler_params=ROOM,
         name="first_operator",
     )(*near(folded, below, above, low, high, geometry))
 
@@ -444,6 +451,7 @@
         in_specs=[SMEM] + [VMEM] * 10,
         out_specs=[VMEM, VMEM],
         scratch_shapes=[pltpu.VMEM((512, LANES), jnp.float32)] * 2,
+        compiler_params=ROOM,
         name="second_operator",
     )(spot, *near(folded, below, above, low, high, geometry, *sums))
 
@@ -458,6 +466,7 @@
         out_shape=pltpu.VMEM((128, LANES), jnp.float32),
         in_specs=[VMEM] * 2,
         out_specs=VMEM,
+        compiler_params=ROOM,
         name="as_lines",
     )(*near(one, two))
 
@@ -532,6 +541,7 @@
         in_specs=[SMEM, VMEM, VMEM],
         out_specs=[VMEM, VMEM],
         scratch_shapes=[pltpu.VMEM((gathered.shape[0], LANES), jnp.float32)],
+        compiler_params=ROOM,
         name="middle",
     )(spot, *near(gathered, lines))
 
@@ -585,6 +595,7 @@
         in_specs=[SMEM] + [VMEM] * 5,
         out_specs=[VMEM, VMEM],
         scratch_shapes=[pltpu.VMEM((64, LANES), jnp.float32)],
+        compiler_params=ROOM,
         name="finish",
     )(spot, *near(gathered, image, second, first, right_side))
 

time: 153 us -> 145 us (0.948)
  local copies, waits for them, and re-layouts: 10.5 us -> 0.7 us
  waiting for transfers between devices: 30.6 us -> 32.4 us
    unnamed x40 -> x10, local copies, waits for them, and re-layouts: 9.85 us -> 0.05 us
    ppermute x9, waiting for transfers between devices: 29 us -> 31.2 us  [swap(): lax.ppermute(backward_part, axis, backward)]
  transfers between devices with their start and end apart: 18 -> 18, of which waited for: 11 -> 12; matrix products, arithmetic and copies ran while one was open for 1% -> 1% of each run, Pallas kernels for 1% -> 1%
where the time goes in v3:
time: 145 us; the launch traced here: 144 us
  starting transfers between devices  52.4 us (36%)
  blocking collectives  42.4 us (29%)
  waiting for transfers between devices  32.4 us (22%)
  Pallas kernels  12.7 us (9%)
  other arithmetic  1.93 us (1%)
    all_to_all x2, blocking collectives, exchange(): return lax.all_to_all(rows, axes, 0, 0, tiled=True)  42.4 us
    ppermute x9, starting transfers between devices, swap(): lax.ppermute(forward_part, axis, forward)  34.5 us
    ppermute x9, waiting for transfers between devices, swap(): lax.ppermute(backward_part, axis, backward)  31.2 us
    ppermute x9, starting transfers between devices, swap(): lax.ppermute(backward_part, axis, backward)  17.9 us
    pallas_call x2, Pallas kernels, block_solve(): pl.pallas_call(functools.partial(solve_kernel, count, shared), out_shape=...  5.01 us
  transfers between devices with their start and end apart: 18, of which 12 were waited for; matrix products, arithmetic and copies ran while one was open for 1% of the time, Pallas kernels for 1%

profile of v3, /device:TPU:1, one launch (start us, length us, event | category | flops | bytes accessed | tf_op | source)
XLA Modules:
  0.0 143.9 jit_solution(7475380696537670941)
XLA Ops:
  2.5 5.0 %collective-permute-start = (f32[328,32]{1,0:T(8,128)S(1)}, f32[328,32]{1,0:T(8,128)S(1)}, u32[]{:S(2)}, u32[]{:S(2)}) collective-permute-start(f32[328,32]{1,0:T(8,128)S(1)} %get-tuple-element.88), channel_id=1, source_target_pairs={{0,1},{1,2},{2,3},{3,4},{4,5},{5,6},{6,7},{7,8},{8,9},{9,10},{10,1... | collective-permute-start | bytes 125960 | tf_op jit(solution)/shard_map/ppermute | solution.py:24
  7.5 1.3 collective-permute-start.1
  9.9 4.4 %collective-permute-done.1 = f32[328,32]{1,0:T(8,128)S(1)} collective-permute-done((f32[328,32]{1,0:T(8,128)S(1)}, f32[328,32]{1,0:T(8,128)S(1)}, u32[]{:S(2)}, u32[]{:S(2)}) %collective-permute-start.1) | collective-permute-done | bytes 42016 | tf_op jit(solution)/shard_map/ppermute | solution.py:24
  14.6 5.5 %collective-permute-start.2 = (f32[2,8,8,128]{3,2,1,0:T(8,128)S(1)}, f32[2,8,8,128]{3,2,1,0:T(8,128)S(1)}, u32[]{:S(2)}, u32[]{:S(2)}) collective-permute-start(f32[2,8,8,128]{3,2,1,0:T(8,128)S(1)} %get-tuple-element.47), channel_id=1, source_target_pairs={{0,96},{96,192},{192,288},{288,384},{384,480},{480,576},{576,672},... | collective-permute-start | bytes 196616 | tf_op jit(solution)/shard_map/ppermute | solution.py:24
  20.1 5.2 %collective-permute-start.3 = (f32[2,8,8,128]{3,2,1,0:T(8,128)S(1)}, f32[2,8,8,128]{3,2,1,0:T(8,128)S(1)}, u32[]{:S(2)}, u32[]{:S(2)}) collective-permute-start(f32[2,8,8,128]{3,2,1,0:T(8,128)S(1)} %get-tuple-element.48), channel_id=1, source_target_pairs={{96,0},{192,96},{288,192},{384,288},{480,384},{576,480},{672,576},... | collective-permute-start | bytes 196616 | tf_op jit(solution)/shard_map/ppermute | solution.py:24
  26.9 2.1 %collective-permute-start.4 = (f32[10,2,8,128]{3,2,1,0:T(8,128)S(1)}, f32[10,2,8,128]{3,2,1,0:T(8,128)S(1)}, u32[]{:S(2)}, u32[]{:S(2)}) collective-permute-start(f32[10,2,8,128]{3,2,1,0:T(8,128)S(1)} %get-tuple-element.52), channel_id=1, source_target_pairs={{0,12},{12,24},{24,36},{36,48},{48,60},{60,72},{72,84},{1,13},{13,... | collective-permute-start | bytes 245768 | tf_op jit(solution)/shard_map/ppermute | solution.py:24
  28.9 1.3 collective-permute-start.5
  30.4 4.0 %collective-permute-done.5.above = f32[10,2,8,128]{3,2,1,0:T(8,128)S(1)} collective-permute-done((f32[10,2,8,128]{3,2,1,0:T(8,128)S(1)}, f32[10,2,8,128]{3,2,1,0:T(8,128)S(1)}, u32[]{:S(2)}, u32[]{:S(2)}) %collective-permute-start.5) | collective-permute-done | bytes 81952 | tf_op jit(solution)/shard_map/ppermute | solution.py:24
  34.4 2.4 %block_solve_first.1 = (f32[10,10,8,128]{3,2,1,0:T(8,128)S(1)}, f32[4,10,8,128]{3,2,1,0:T(8,128)S(1)}, f32[10,2,8,128]{3,2,1,0:T(8,128)S(1)}, f32[10,2,8,128]{3,2,1,0:T(8,128)S(1)}, f32[1,128]{1,0:T(1,128)S(1)}) custom-call(f32[512,128]{1,0:T(8,128)S(1)} %get-tuple-element.46.field, f32[2,8,8,128]{3,2,1,0:T(8,128)S(1)} %collective-permute-done.2.low, ...), custom_call_target="tpu_custom_call" | custom-call | tf_op jit(solution)/shard_map/block_solve_first/pallas_call | solution.py:193
  36.9 2.9 %collective-permute-start.6 = (f32[10,2,8,128]{3,2,1,0:T(8,128)S(1)}, f32[10,2,8,128]{3,2,1,0:T(8,128)S(1)}, u32[]{:S(2)}, u32[]{:S(2)}) collective-permute-start(f32[10,2,8,128]{3,2,1,0:T(8,128)S(1)} %get-tuple-element.56), channel_id=1, source_target_pairs={{0,12},{12,24},{24,36},{36,48},{48,60},{60,72},{72,84},{1,13},{13,... | collective-permute-start | bytes 245768 | tf_op jit(solution)/shard_map/ppermute | solution.py:24
  39.8 1.3 collective-permute-start.7
  41.5 4.4 %collective-permute-done.7.above = f32[10,2,8,128]{3,2,1,0:T(8,128)S(1)} collective-permute-done((f32[10,2,8,128]{3,2,1,0:T(8,128)S(1)}, f32[10,2,8,128]{3,2,1,0:T(8,128)S(1)}, u32[]{:S(2)}, u32[]{:S(2)}) %collective-permute-start.7) | collective-permute-done | bytes 81952 | tf_op jit(solution)/shard_map/ppermute | solution.py:24
  45.9 4.7 %collective-permute-start.8 = (f32[2,8,8,128]{3,2,1,0:T(8,128)S(1)}, f32[2,8,8,128]{3,2,1,0:T(8,128)S(1)}, u32[]{:S(2)}, u32[]{:S(2)}) collective-permute-start(f32[2,8,8,128]{3,2,1,0:T(8,128)S(1)} %get-tuple-element.59), channel_id=1, source_target_pairs={{0,96},{96,192},{192,288},{288,384},{384,480},{480,576},{576,672},... | collective-permute-start | bytes 196616 | tf_op jit(solution)/shard_map/ppermute | solution.py:24
  50.7 1.9 %collective-permute-start.9 = (f32[2,8,8,128]{3,2,1,0:T(8,128)S(1)}, f32[2,8,8,128]{3,2,1,0:T(8,128)S(1)}, u32[]{:S(2)}, u32[]{:S(2)}) collective-permute-start(f32[2,8,8,128]{3,2,1,0:T(8,128)S(1)} %get-tuple-element.60), channel_id=1, source_target_pairs={{96,0},{192,96},{288,192},{384,288},{480,384},{576,480},{672,576},... | collective-permute-start | bytes 196616 | tf_op jit(solution)/shard_map/ppermute | solution.py:24
  52.6 3.6 %collective-permute-done.9.high = f32[2,8,8,128]{3,2,1,0:T(8,128)S(1)} collective-permute-done((f32[2,8,8,128]{3,2,1,0:T(8,128)S(1)}, f32[2,8,8,128]{3,2,1,0:T(8,128)S(1)}, u32[]{:S(2)}, u32[]{:S(2)}) %collective-permute-start.9) | collective-permute-done | bytes 65568 | tf_op jit(solution)/shard_map/ppermute | solution.py:24
  57.2 1.9 %collective-permute-start.10 = (f32[2,8,8,128]{3,2,1,0:T(8,128)S(1)}, f32[2,8,8,128]{3,2,1,0:T(8,128)S(1)}, u32[]{:S(2)}, u32[]{:S(2)}) collective-permute-start(f32[2,8,8,128]{3,2,1,0:T(8,128)S(1)} %get-tuple-element.63), channel_id=1, source_target_pairs={{0,96},{96,192},{192,288},{288,384},{384,480},{480,576},{576,672},... | collective-permute-start | bytes 196616 | tf_op jit(solution)/shard_map/ppermute | solution.py:24
  59.2 2.4 %collective-permute-start.11 = (f32[2,8,8,128]{3,2,1,0:T(8,128)S(1)}, f32[2,8,8,128]{3,2,1,0:T(8,128)S(1)}, u32[]{:S(2)}, u32[]{:S(2)}) collective-permute-start(f32[2,8,8,128]{3,2,1,0:T(8,128)S(1)} %get-tuple-element.64), channel_id=1, source_target_pairs={{96,0},{192,96},{288,192},{384,288},{480,384},{576,480},{672,576},... | collective-permute-start | bytes 196616 | tf_op jit(solution)/shard_map/ppermute | solution.py:24
  61.6 3.2 %collective-permute-done.11.high = f32[2,8,8,128]{3,2,1,0:T(8,128)S(1)} collective-permute-done((f32[2,8,8,128]{3,2,1,0:T(8,128)S(1)}, f32[2,8,8,128]{3,2,1,0:T(8,128)S(1)}, u32[]{:S(2)}, u32[]{:S(2)}) %collective-permute-start.11) | collective-permute-done | bytes 65568 | tf_op jit(solution)/shard_map/ppermute | solution.py:24
  64.8 4.9 %collective-permute-start.12 = (f32[10,2,8,128]{3,2,1,0:T(8,128)S(1)}, f32[10,2,8,128]{3,2,1,0:T(8,128)S(1)}, u32[]{:S(2)}, u32[]{:S(2)}) collective-permute-start(f32[10,2,8,128]{3,2,1,0:T(8,128)S(1)} %get-tuple-element.65), channel_id=1, source_target_pairs={{0,12},{12,24},{24,36},{36,48},{48,60},{60,72},{72,84},{1,13},{13,... | collective-permute-start | bytes 245768 | tf_op jit(solution)/shard_map/ppermute | solution.py:24
  69.7 1.3 collective-permute-start.13
  71.1 4.0 %collective-permute-done.13.above = f32[10,2,8,128]{3,2,1,0:T(8,128)S(1)} collective-permute-done((f32[10,2,8,128]{3,2,1,0:T(8,128)S(1)}, f32[10,2,8,128]{3,2,1,0:T(8,128)S(1)}, u32[]{:S(2)}, u32[]{:S(2)}) %collective-permute-start.13) | collective-permute-done | bytes 81952 | tf_op jit(solution)/shard_map/ppermute | solution.py:24
  75.1 2.6 %block_solve_shared.1 = (f32[10,10,8,128]{3,2,1,0:T(8,128)S(1)}, f32[4,10,8,128]{3,2,1,0:T(8,128)S(1)}, f32[10,2,8,128]{3,2,1,0:T(8,128)S(1)}, f32[10,2,8,128]{3...) custom-call(f32[512,128]{1,0:T(8,128)S(1)} %get-tuple-element.62.field, ...), custom_call_target="tpu_custom_call" | custom-call | tf_op jit(solution)/shard_map/block_solve_shared/pallas_call | solution.py:193
  77.7 3.4 %collective-permute-start.14 = (f32[10,2,8,128]{3,2,1,0:T(8,128)S(1)}, f32[10,2,8,128]{3,2,1,0:T(8,128)S(1)}, u32[]{:S(2)}, u32[]{:S(2)}) collective-permute-start(f32[10,2,8,128]{3,2,1,0:T(8,128)S(1)} %get-tuple-element.68), channel_id=1, source_target_pairs={{0,12},{12,24},{24,36},{36,48},{48,60},{60,72},{72,84},{1,13},{13,... | collective-permute-start | bytes 245768 | tf_op jit(solution)/shard_map/ppermute | solution.py:24
  81.1 1.3 collective-permute-start.15
  83.3 4.0 %collective-permute-done.15.above = f32[10,2,8,128]{3,2,1,0:T(8,128)S(1)} collective-permute-done((f32[10,2,8,128]{3,2,1,0:T(8,128)S(1)}, f32[10,2,8,128]{3,2,1,0:T(8,128)S(1)}, u32[]{:S(2)}, u32[]{:S(2)}) %collective-permute-start.15) | collective-permute-done | bytes 81952 | tf_op jit(solution)/shard_map/ppermute | solution.py:24
  87.3 4.1 %collective-permute-start.16 = (f32[2,8,8,128]{3,2,1,0:T(8,128)S(1)}, f32[2,8,8,128]{3,2,1,0:T(8,128)S(1)}, u32[]{:S(2)}, u32[]{:S(2)}) collective-permute-start(f32[2,8,8,128]{3,2,1,0:T(8,128)S(1)} %get-tuple-element.75), channel_id=1, source_target_pairs={{0,96},{96,192},{192,288},{288,384},{384,480},{480,576},{576,672},... | collective-permute-start | bytes 196616 | tf_op jit(solution)/shard_map/ppermute | solution.py:24
  91.4 1.9 %collective-permute-start.17 = (f32[2,8,8,128]{3,2,1,0:T(8,128)S(1)}, f32[2,8,8,128]{3,2,1,0:T(8,128)S(1)}, u32[]{:S(2)}, u32[]{:S(2)}) collective-permute-start(f32[2,8,8,128]{3,2,1,0:T(8,128)S(1)} %get-tuple-element.76), channel_id=1, source_target_pairs={{96,0},{192,96},{288,192},{384,288},{480,384},{576,480},{672,576},... | collective-permute-start | bytes 196616 | tf_op jit(solution)/shard_map/ppermute | solution.py:24
  93.4 3.6 %collective-permute-done.17.high = f32[2,8,8,128]{3,2,1,0:T(8,128)S(1)} collective-permute-done((f32[2,8,8,128]{3,2,1,0:T(8,128)S(1)}, f32[2,8,8,128]{3,2,1,0:T(8,128)S(1)}, u32[]{:S(2)}, u32[]{:S(2)}) %collective-permute-start.17) | collective-permute-done | bytes 65568 | tf_op jit(solution)/shard_map/ppermute | solution.py:24
  97.0 1.9 %second_operator.1 = (f32[128,128]{1,0:T(8,128)S(1)}, f32[12,1,128]{2,1,0:T(1,128)S(1)}) custom-call(s32[3]{0:T(128)S(1)} %pad_add_fusion.spot, f32[10,10,8,128]{3,2,1,0:T(8,128)S(1)} %get-tuple-element.67.folded, f32[10,2,8,128]{3,2,1,0:T(8,128)S(1)} %collective-permute-done.14.below, f32[10,2,8,128]{3,2,1,0:T(8,128)S(1)} %collective-permute-done.15.above, ...), custom_call_target="tpu_custom_call" | custom-call | tf_op jit(solution)/shard_map/second_operator/pallas_call | solution.py:445
  98.9 23.3 %all_to_all.16.gathered = f32[12,1,128]{2,1,0:T(1,128)S(1)} all-to-all(f32[12,1,128]{2,1,0:T(1,128)S(1)} %get-tuple-element.81), channel_id=1, replica_groups=mesh['gx'=8,'gy'=8,'gz'=12] {'gz'}, dimensions={0} | all-to-all | bytes 12288 | tf_op jit(solution)/shard_map/all_to_all | solution.py:604
  123.2 19.2 %all_to_all.17 = f32[64,8,128]{2,1,0:T(8,128)S(1)} all-to-all(f32[64,8,128]{2,1,0:T(8,128)S(1)} %bitcast.23), channel_id=1, replica_groups=mesh['gx'=8,'gy'=8,'gz'=12] {'gx','gy'}, dimensions={0} | all-to-all | bytes 524288 | tf_op jit(solution)/shard_map/all_to_all | solution.py:604
  142.4 1.5 %finish.1 = (f32[64,128]{1,0:T(8,128)}, f32[64,128]{1,0:T(8,128)}) custom-call(s32[3]{0:T(128)S(1)} %pad_add_fusion.spot, f32[512,128]{1,0:T(8,128)S(1)} %bitcast.17, f32[64,128]{1,0:T(8,128)S(1)} %get-tuple-element.84.image, f32[128,128]{1,0:T(8,128)S(1)} %get-tuple-element.82.lines.second, f32[128,128]{1,0:T(8,128)S(1)} %as_lines.1.first, ...), custom_call_target="tpu_custom_call" | custom-call | tf_op jit(solution)/shard_map/finish/pallas_call | solution.py:592
  (49 shorter events, 8.4 us)
Async XLA Ops:
  2.4 6.4 %copy-start = (f32[4,8,8,128]{3,2,1,0:T(8,128)S(1)}, f32[4,8,8,128]{3,2,1,0:T(8,128)}, u32[]{:S(2)}) copy-start(f32[4,8,8,128]{3,2,1,0:T(8,128)} %param.6) | copy-start | bytes 393220
  2.4 6.4 %copy-start.1 = (f32[8,8,128]{2,1,0:T(8,128)S(1)}, f32[8,8,128]{2,1,0:T(8,128)}, u32[]{:S(2)}) copy-start(f32[8,8,128]{2,1,0:T(8,128)} %param.5) | copy-start | bytes 98308
  2.4 7.2 %copy-start.3 = (f32[32,3,10]{0,1,2:T(4,128)S(1)}, f32[32,3,10]{0,1,2:T(4,128)}, u32[]{:S(2)}) copy-start(f32[32,3,10]{0,1,2:T(4,128)} %param.9) | copy-start | bytes 11524
  2.5 7.2 %copy-start.2 = (f32[32,3,10,10]{0,1,3,2:T(4,128)S(1)}, f32[32,3,10,10]{0,1,3,2:T(4,128)}, u32[]{:S(2)}) copy-start(f32[32,3,10,10]{0,1,3,2:T(4,128)} %param.8) | copy-start | bytes 115204
  2.5 7.3 %collective-permute-start = (f32[328,32]{1,0:T(8,128)S(1)}, f32[328,32]{1,0:T(8,128)S(1)}, u32[]{:S(2)}, u32[]{:S(2)}) collective-permute-start(f32[328,32]{1,0:T(8,128)S(1)} %get-tuple-element.88), channel_id=1, source_target_pairs={{0,1},{1,2},{2,3},{3,4},{4,5},{5,6},{6,7},{7,8},{8,9},{9,10},{10,1... | collective-permute-start | bytes 125960 | tf_op jit(solution)/shard_map/ppermute | solution.py:24
  7.5 6.7 %collective-permute-start.1 = (f32[328,32]{1,0:T(8,128)S(1)}, f32[328,32]{1,0:T(8,128)S(1)}, u32[]{:S(2)}, u32[]{:S(2)}) collective-permute-start(f32[328,32]{1,0:T(8,128)S(1)} %get-tuple-element.89), channel_id=1, source_target_pairs={{1,0},{2,1},{3,2},{4,3},{5,4},{6,5},{7,6},{8,7},{9,8},{10,9},{11,1... | collective-permute-start | bytes 125960 | tf_op jit(solution)/shard_map/ppermute | solution.py:24
  14.6 12.2 %collective-permute-start.2 = (f32[2,8,8,128]{3,2,1,0:T(8,128)S(1)}, f32[2,8,8,128]{3,2,1,0:T(8,128)S(1)}, u32[]{:S(2)}, u32[]{:S(2)}) collective-permute-start(f32[2,8,8,128]{3,2,1,0:T(8,128)S(1)} %get-tuple-element.47), channel_id=1, source_target_pairs={{0,96},{96,192},{192,288},{288,384},{384,480},{480,576},{576,672},... | collective-permute-start | bytes 196616 | tf_op jit(solution)/shard_map/ppermute | solution.py:24
  20.1 6.7 %collective-permute-start.3 = (f32[2,8,8,128]{3,2,1,0:T(8,128)S(1)}, f32[2,8,8,128]{3,2,1,0:T(8,128)S(1)}, u32[]{:S(2)}, u32[]{:S(2)}) collective-permute-start(f32[2,8,8,128]{3,2,1,0:T(8,128)S(1)} %get-tuple-element.48), channel_id=1, source_target_pairs={{96,0},{192,96},{288,192},{384,288},{480,384},{576,480},{672,576},... | collective-permute-start | bytes 196616 | tf_op jit(solution)/shard_map/ppermute | solution.py:24
  26.9 3.6 %collective-permute-start.4 = (f32[10,2,8,128]{3,2,1,0:T(8,128)S(1)}, f32[10,2,8,128]{3,2,1,0:T(8,128)S(1)}, u32[]{:S(2)}, u32[]{:S(2)}) collective-permute-start(f32[10,2,8,128]{3,2,1,0:T(8,128)S(1)} %get-tuple-element.52), channel_id=1, source_target_pairs={{0,12},{12,24},{24,36},{36,48},{48,60},{60,72},{72,84},{1,13},{13,... | collective-permute-start | bytes 245768 | tf_op jit(solution)/shard_map/ppermute | solution.py:24
  28.9 5.5 %collective-permute-start.5 = (f32[10,2,8,128]{3,2,1,0:T(8,128)S(1)}, f32[10,2,8,128]{3,2,1,0:T(8,128)S(1)}, u32[]{:S(2)}, u32[]{:S(2)}) collective-permute-start(f32[10,2,8,128]{3,2,1,0:T(8,128)S(1)} %get-tuple-element.53), channel_id=1, source_target_pairs={{12,0},{24,12},{36,24},{48,36},{60,48},{72,60},{84,72},{13,1},{25,... | collective-permute-start | bytes 245768 | tf_op jit(solution)/shard_map/ppermute | solution.py:24
  36.9 4.6 %collective-permute-start.6 = (f32[10,2,8,128]{3,2,1,0:T(8,128)S(1)}, f32[10,2,8,128]{3,2,1,0:T(8,128)S(1)}, u32[]{:S(2)}, u32[]{:S(2)}) collective-permute-start(f32[10,2,8,128]{3,2,1,0:T(8,128)S(1)} %get-tuple-element.56), channel_id=1, source_target_pairs={{0,12},{12,24},{24,36},{36,48},{48,60},{60,72},{72,84},{1,13},{13,... | collective-permute-start | bytes 245768 | tf_op jit(solution)/shard_map/ppermute | solution.py:24
  39.8 6.1 %collective-permute-start.7 = (f32[10,2,8,128]{3,2,1,0:T(8,128)S(1)}, f32[10,2,8,128]{3,2,1,0:T(8,128)S(1)}, u32[]{:S(2)}, u32[]{:S(2)}) collective-permute-start(f32[10,2,8,128]{3,2,1,0:T(8,128)S(1)} %get-tuple-element.57), channel_id=1, source_target_pairs={{12,0},{24,12},{36,24},{48,36},{60,48},{72,60},{84,72},{13,1},{25,... | collective-permute-start | bytes 245768 | tf_op jit(solution)/shard_map/ppermute | solution.py:24
  45.9 6.7 %collective-permute-start.8 = (f32[2,8,8,128]{3,2,1,0:T(8,128)S(1)}, f32[2,8,8,128]{3,2,1,0:T(8,128)S(1)}, u32[]{:S(2)}, u32[]{:S(2)}) collective-permute-start(f32[2,8,8,128]{3,2,1,0:T(8,128)S(1)} %get-tuple-element.59), channel_id=1, source_target_pairs={{0,96},{96,192},{192,288},{288,384},{384,480},{480,576},{576,672},... | collective-permute-start | bytes 196616 | tf_op jit(solution)/shard_map/ppermute | solution.py:24
  50.7 5.6 %collective-permute-start.9 = (f32[2,8,8,128]{3,2,1,0:T(8,128)S(1)}, f32[2,8,8,128]{3,2,1,0:T(8,128)S(1)}, u32[]{:S(2)}, u32[]{:S(2)}) collective-permute-start(f32[2,8,8,128]{3,2,1,0:T(8,128)S(1)} %get-tuple-element.60), channel_id=1, source_target_pairs={{96,0},{192,96},{288,192},{384,288},{480,384},{576,480},{672,576},... | collective-permute-start | bytes 196616 | tf_op jit(solution)/shard_map/ppermute | solution.py:24
  57.2 4.3 %collective-permute-start.10 = (f32[2,8,8,128]{3,2,1,0:T(8,128)S(1)}, f32[2,8,8,128]{3,2,1,0:T(8,128)S(1)}, u32[]{:S(2)}, u32[]{:S(2)}) collective-permute-start(f32[2,8,8,128]{3,2,1,0:T(8,128)S(1)} %get-tuple-element.63), channel_id=1, source_target_pairs={{0,96},{96,192},{192,288},{288,384},{384,480},{480,576},{576,672},... | collective-permute-start | bytes 196616 | tf_op jit(solution)/shard_map/ppermute | solution.py:24
  59.2 5.6 %collective-permute-start.11 = (f32[2,8,8,128]{3,2,1,0:T(8,128)S(1)}, f32[2,8,8,128]{3,2,1,0:T(8,128)S(1)}, u32[]{:S(2)}, u32[]{:S(2)}) collective-permute-start(f32[2,8,8,128]{3,2,1,0:T(8,128)S(1)} %get-tuple-element.64), channel_id=1, source_target_pairs={{96,0},{192,96},{288,192},{384,288},{480,384},{576,480},{672,576},... | collective-permute-start | bytes 196616 | tf_op jit(solution)/shard_map/ppermute | solution.py:24
  64.8 6.4 %collective-permute-start.12 = (f32[10,2,8,128]{3,2,1,0:T(8,128)S(1)}, f32[10,2,8,128]{3,2,1,0:T(8,128)S(1)}, u32[]{:S(2)}, u32[]{:S(2)}) collective-permute-start(f32[10,2,8,128]{3,2,1,0:T(8,128)S(1)} %get-tuple-element.65), channel_id=1, source_target_pairs={{0,12},{12,24},{24,36},{36,48},{48,60},{60,72},{72,84},{1,13},{13,... | collective-permute-start | bytes 245768 | tf_op jit(solution)/shard_map/ppermute | solution.py:24
  69.7 5.4 %collective-permute-start.13 = (f32[10,2,8,128]{3,2,1,0:T(8,128)S(1)}, f32[10,2,8,128]{3,2,1,0:T(8,128)S(1)}, u32[]{:S(2)}, u32[]{:S(2)}) collective-permute-start(f32[10,2,8,128]{3,2,1,0:T(8,128)S(1)} %get-tuple-element.66), channel_id=1, source_target_pairs={{12,0},{24,12},{36,24},{48,36},{60,48},{72,60},{84,72},{13,1},{25,... | collective-permute-start | bytes 245768 | tf_op jit(solution)/shard_map/ppermute | solution.py:24
  77.7 5.6 %collective-permute-start.14 = (f32[10,2,8,128]{3,2,1,0:T(8,128)S(1)}, f32[10,2,8,128]{3,2,1,0:T(8,128)S(1)}, u32[]{:S(2)}, u32[]{:S(2)}) collective-permute-start(f32[10,2,8,128]{3,2,1,0:T(8,128)S(1)} %get-tuple-element.68), channel_id=1, source_target_pairs={{0,12},{12,24},{24,36},{36,48},{48,60},{60,72},{72,84},{1,13},{13,... | collective-permute-start | bytes 245768 | tf_op jit(solution)/shard_map/ppermute | solution.py:24
  81.1 6.2 %collective-permute-start.15 = (f32[10,2,8,128]{3,2,1,0:T(8,128)S(1)}, f32[10,2,8,128]{3,2,1,0:T(8,128)S(1)}, u32[]{:S(2)}, u32[]{:S(2)}) collective-permute-start(f32[10,2,8,128]{3,2,1,0:T(8,128)S(1)} %get-tuple-element.69), channel_id=1, source_target_pairs={{12,0},{24,12},{36,24},{48,36},{60,48},{72,60},{84,72},{13,1},{25,... | collective-permute-start | bytes 245768 | tf_op jit(solution)/shard_map/ppermute | solution.py:24
  87.3 6.1 %collective-permute-start.16 = (f32[2,8,8,128]{3,2,1,0:T(8,128)S(1)}, f32[2,8,8,128]{3,2,1,0:T(8,128)S(1)}, u32[]{:S(2)}, u32[]{:S(2)}) collective-permute-start(f32[2,8,8,128]{3,2,1,0:T(8,128)S(1)} %get-tuple-element.75), channel_id=1, source_target_pairs={{0,96},{96,192},{192,288},{288,384},{384,480},{480,576},{576,672},... | collective-permute-start | bytes 196616 | tf_op jit(solution)/shard_map/ppermute | solution.py:24
  91.4 5.6 %collective-permute-start.17 = (f32[2,8,8,128]{3,2,1,0:T(8,128)S(1)}, f32[2,8,8,128]{3,2,1,0:T(8,128)S(1)}, u32[]{:S(2)}, u32[]{:S(2)}) collective-permute-start(f32[2,8,8,128]{3,2,1,0:T(8,128)S(1)} %get-tuple-element.76), channel_id=1, source_target_pairs={{96,0},{192,96},{288,192},{384,288},{480,384},{576,480},{672,576},... | collective-permute-start | bytes 196616 | tf_op jit(solution)/shard_map/ppermute | solution.py:24

commit v4 on v3

--- a/solution.py
+++ b/solution.py
@@ -11,6 +11,7 @@
 HIGHEST = lax.Precision.HIGHEST
 LANES = 128
 REACH = 4
+GROUP = 32
 SMEM = pl.BlockSpec(memory_space=pltpu.SMEM)
 VMEM = pl.BlockSpec(memory_space=pltpu.VMEM)
 ROOM = pltpu.CompilerParams(vmem_limit_bytes=8 << 20)
@@ -73,6 +74,27 @@
             target[pl.ds(100 * out + start, size), :] = total
 
 
+def pack(out, pieces):
+    lane = lax.broadcasted_iota(jnp.int32, (8, LANES), 1)
+    for place in range(len(pieces) // 4):
+        total = pieces[4 * place]
+        for slot in range(1, 4):
+            moved = pltpu.roll(pieces[4 * place + slot], GROUP * slot, 1)
+            total = jnp.where(lane >= GROUP * slot, moved, total)
+        out[place] = total
+
+
+class Unpacked:
+    def __init__(self, ref, width):
+        self.ref, self.width = ref, width
+
+    def __getitem__(self, index):
+        place = self.width * index[0] + index[1]
+        piece = self.ref[place // 4]
+        slot = place % 4
+        return piece if slot == 0 else pltpu.roll(piece, LANES - GROUP * slot, 1)
+
+
 def extended_first(a, y, field, low, high, shared):
     if a == 0:
         return low[0, y]
@@ -87,16 +109,16 @@
 
 
 def second_edges_kernel(shared, field, low, high, backward, forward):
-    for a in range(10):
-        for y in range(2):
-            backward[a, y] = extended_first(a, y, field, low, high, shared)
-            forward[a, y] = extended_first(a, 6 + y, field, low, high, shared)
+    low, high = Unpacked(low, 8), Unpacked(high, 8)
+    pairs = [(a, y) for a in range(10) for y in range(2)]
+    pack(backward, [extended_first(a, y, field, low, high, shared) for a, y in pairs])
+    pack(forward, [extended_first(a, 6 + y, field, low, high, shared) for a, y in pairs])
 
 
 def second_edges(field, low, high, shared):
     return pl.pallas_call(
         functools.partial(second_edges_kernel, shared),
-        out_shape=[pltpu.VMEM((10, 2, 8, LANES), jnp.float32)] * 2,
+        out_shape=[pltpu.VMEM((5, 8, LANES), jnp.float32)] * 2,
         in_specs=[VMEM] * 3,
         out_specs=[VMEM] * 2,
         compiler_params=ROOM,
@@ -109,6 +131,8 @@
         folded, rims, backward, forward, inner, size_row, assembled, blocks, left, right, pair = refs
     else:
         folded, rims, backward, forward, inner, blocks, left, right, pair = refs
+    low, high = Unpacked(low, 8), Unpacked(high, 8)
+    below, above = Unpacked(below, 2), Unpacked(above, 2)
     blocks[pl.ds(1000, 40), :] = jnp.zeros((40, LANES), jnp.float32)
     left[pl.ds(1000, 40), :] = jnp.zeros((40, LANES), jnp.float32)
     right[pl.ds(1000, 40), :] = jnp.zeros((40, LANES), jnp.float32)
@@ -168,19 +192,18 @@
         for b in range(10):
             nodes = right[pl.ds(100 * a + 10 * b + 1, 8), :]
             folded[a, b] = nodes
-            if b < 2:
-                backward[a, b] = nodes
-            if b > 7:
-                forward[a, b - 8] = nodes
             if a < 2:
                 rims[a, b] = nodes
             if a > 7:
                 rims[a - 6, b] = nodes
+    pairs = [(a, b) for a in range(10) for b in range(2)]
+    pack(backward, [folded[a, b] for a, b in pairs])
+    pack(forward, [folded[a, b + 8] for a, b in pairs])
 
 
 def block_solve(field, low, high, below, above, table, valid, count, shared):
     row = pltpu.VMEM((1, LANES), jnp.float32)
-    edge = pltpu.VMEM((10, 2, 8, LANES), jnp.float32)
+    edge = pltpu.VMEM((5, 8, LANES), jnp.float32)
     outs = [
         pltpu.VMEM((10, 10, 8, LANES), jnp.float32),
         pltpu.VMEM((4, 10, 8, LANES), jnp.float32),
@@ -212,16 +235,16 @@
 
 
 def first_edges_kernel(rims, below, above, backward, forward):
-    for a in range(2):
-        for y in range(8):
-            backward[a, y] = folded_second(rims, a, y, a, below, above)
-            forward[a, y] = folded_second(rims, a + 2, y, a + 8, below, above)
+    below, above = Unpacked(below, 2), Unpacked(above, 2)
+    pairs = [(a, y) for a in range(2) for y in range(8)]
+    pack(backward, [folded_second(rims, a, y, a, below, above) for a, y in pairs])
+    pack(forward, [folded_second(rims, a + 2, y, a + 8, below, above) for a, y in pairs])
 
 
 def first_edges(rims, below, above):
     return pl.pallas_call(
         first_edges_kernel,
-        out_shape=[pltpu.VMEM((2, 8, 8, LANES), jnp.float32)] * 2,
+        out_shape=[pltpu.VMEM((4, 8, LANES), jnp.float32)] * 2,
         in_specs=[VMEM] * 3,
         out_specs=[VMEM] * 2,
         compiler_params=ROOM,
@@ -312,20 +335,21 @@
     )(*near(right_side, geometry))
 
 
+def pack_ends(field, backward, forward):
+    pack(backward, [field[pl.ds(8 * i, 8), :] for i in range(16)])
+    pack(forward, [field[pl.ds(384 + 8 * i, 8), :] for i in range(16)])
+
+
 def end_lines_kernel(count, with_edges, ends, own, out, *edges):
     spread_lines(ends[...], lambda e: jnp.where(e < REACH, e, e + count), out, own)
     if with_edges:
-        backward, forward = edges
-        for x in range(2):
-            for y in range(8):
-                backward[x, y] = out[pl.ds(64 * x + 8 * y, 8), :]
-                forward[x, y] = out[pl.ds(64 * (6 + x) + 8 * y, 8), :]
+        pack_ends(out, *edges)
 
 
 def end_lines(ends, own, count, with_edges):
     outs = [pltpu.VMEM(own.shape, jnp.float32)]
     if with_edges:
-        outs += [pltpu.VMEM((2, 8, 8, LANES), jnp.float32)] * 2
+        outs += [pltpu.VMEM((4, 8, LANES), jnp.float32)] * 2
     return pl.pallas_call(
         functools.partial(end_lines_kernel, count, with_edges),
         out_shape=outs,
@@ -337,6 +361,8 @@
 
 
 def apply_local(derivative, folded, below, above, low, high, geometry, field, image):
+    below, above = Unpacked(below, 2), Unpacked(above, 2)
+    low, high = Unpacked(low, 8), Unpacked(high, 8)
     for x in range(8):
         for y in range(8):
             nodes = folded_second(folded, x + 1, y, x + 1, below, above)
@@ -377,15 +403,12 @@
     last = image[pl.ds(7, 64, stride=8), :]
     image[pl.ds(0, 64, stride=8), :] = first + pltpu.roll(last, 1, 1)
     image[pl.ds(7, 64, stride=8), :] = last + pltpu.roll(first, LANES - 1, 1)
-    for x in range(2):
-        for y in range(8):
-            backward[x, y] = image[pl.ds(64 * x + 8 * y, 8), :]
-            forward[x, y] = image[pl.ds(64 * (6 + x) + 8 * y, 8), :]
+    pack_ends(image, backward, forward)
 
 
 def first_operator(folded, below, above, low, high, geometry, count):
     full = pltpu.VMEM((512, LANES), jnp.float32)
-    edge = pltpu.VMEM((2, 8, 8, LANES), jnp.float32)
+    edge = pltpu.VMEM((4, 8, LANES), jnp.float32)
     return pl.pallas_call(
         functools.partial(first_operator_kernel, count, derivative_table()),
         out_shape=[full, full, edge, edge, pltpu.VMEM((1, LANES), jnp.float32)],

time: 145 us -> 140 us (0.966)
  waiting for transfers between devices: 32.4 us -> 27.1 us
    ppermute x9, waiting for transfers between devices: 31.2 us -> 27.1 us  [swap(): lax.ppermute(backward_part, axis, backward)]
  transfers between devices with their start and end apart: 18 -> 18, of which waited for: 12 -> 8; matrix products, arithmetic and copies ran while one was open for 1% -> 1% of each run, Pallas kernels for 1% -> 1%
where the time goes in v4:
time: 140 us
  starting transfers between devices  52.2 us (37%)
  blocking collectives  42.6 us (30%)
  waiting for transfers between devices  27.1 us (19%)
  Pallas kernels  13.6 us (10%)
  other arithmetic  1.93 us (1%)
    all_to_all x2, blocking collectives, exchange(): return lax.all_to_all(rows, axes, 0, 0, tiled=True)  42.6 us
    ppermute x9, starting transfers between devices, swap(): lax.ppermute(forward_part, axis, forward)  34.3 us
    ppermute x9, waiting for transfers between devices, swap(): lax.ppermute(backward_part, axis, backward)  27.1 us
    ppermute x9, starting transfers between devices, swap(): lax.ppermute(backward_part, axis, backward)  17.9 us
    pallas_call x2, Pallas kernels, block_solve(): pl.pallas_call(functools.partial(solve_kernel, count, shared), out_shape=...  5.22 us
  transfers between devices with their start and end apart: 18, of which 8 were waited for; matrix products, arithmetic and copies ran while one was open for 1% of the time, Pallas kernels for 1%

profile of v4, /device:TPU:1, one launch (start us, length us, event | category | flops | bytes accessed | tf_op | source)
XLA Modules:
  0.0 139.5 jit_solution(13481684955999482350)
XLA Ops:
  2.5 5.0 %collective-permute-start = (f32[328,32]{1,0:T(8,128)S(1)}, f32[328,32]{1,0:T(8,128)S(1)}, u32[]{:S(2)}, u32[]{:S(2)}) collective-permute-start(f32[328,32]{1,0:T(8,128)S(1)} %get-tuple-element.88), channel_id=1, source_target_pairs={{0,1},{1,2},{2,3},{3,4},{4,5},{5,6},{6,7},{7,8},{8,9},{9,10},{10,1... | collective-permute-start | bytes 125960 | tf_op jit(solution)/shard_map/ppermute | solution.py:25
  7.5 1.3 collective-permute-start.1
  9.9 4.4 %collective-permute-done.1 = f32[328,32]{1,0:T(8,128)S(1)} collective-permute-done((f32[328,32]{1,0:T(8,128)S(1)}, f32[328,32]{1,0:T(8,128)S(1)}, u32[]{:S(2)}, u32[]{:S(2)}) %collective-permute-start.1) | collective-permute-done | bytes 42016 | tf_op jit(solution)/shard_map/ppermute | solution.py:25
  14.7 5.5 %collective-permute-start.2 = (f32[4,8,128]{2,1,0:T(8,128)S(1)}, f32[4,8,128]{2,1,0:T(8,128)S(1)}, u32[]{:S(2)}, u32[]{:S(2)}) collective-permute-start(f32[4,8,128]{2,1,0:T(8,128)S(1)} %get-tuple-element.47), channel_id=1, source_target_pairs={{0,96},{96,192},{192,288},{288,384},{384,480},{480,576},{576,672},... | collective-permute-start | bytes 49160 | tf_op jit(solution)/shard_map/ppermute | solution.py:25
  20.2 5.2 %collective-permute-start.3 = (f32[4,8,128]{2,1,0:T(8,128)S(1)}, f32[4,8,128]{2,1,0:T(8,128)S(1)}, u32[]{:S(2)}, u32[]{:S(2)}) collective-permute-start(f32[4,8,128]{2,1,0:T(8,128)S(1)} %get-tuple-element.48), channel_id=1, source_target_pairs={{96,0},{192,96},{288,192},{384,288},{480,384},{576,480},{672,576},... | collective-permute-start | bytes 49160 | tf_op jit(solution)/shard_map/ppermute | solution.py:25
  27.0 1.6 %collective-permute-start.4 = (f32[5,8,128]{2,1,0:T(8,128)S(1)}, f32[5,8,128]{2,1,0:T(8,128)S(1)}, u32[]{:S(2)}, u32[]{:S(2)}) collective-permute-start(f32[5,8,128]{2,1,0:T(8,128)S(1)} %get-tuple-element.52), channel_id=1, source_target_pairs={{0,12},{12,24},{24,36},{36,48},{48,60},{60,72},{72,84},{1,13},{13,... | collective-permute-start | bytes 61448 | tf_op jit(solution)/shard_map/ppermute | solution.py:25
  28.6 1.3 collective-permute-start.5
  29.9 3.4 %collective-permute-done.5.above = f32[5,8,128]{2,1,0:T(8,128)S(1)} collective-permute-done((f32[5,8,128]{2,1,0:T(8,128)S(1)}, f32[5,8,128]{2,1,0:T(8,128)S(1)}, u32[]{:S(2)}, u32[]{:S(2)}) %collective-permute-start.5) | collective-permute-done | bytes 20512 | tf_op jit(solution)/shard_map/ppermute | solution.py:25
  33.4 2.5 %block_solve_first.1 = (f32[10,10,8,128]{3,2,1,0:T(8,128)S(1)}, f32[4,10,8,128]{3,2,1,0:T(8,128)S(1)}, f32[5,8,128]{2,1,0:T(8,128)S(1)}, f32[5,8,128]{2,1,0:T(8,128)S(1)}, f32[1,128]{1,0:T(1,128)S(1)}) custom-call(f32[512,128]{1,0:T(8,128)S(1)} %get-tuple-element.46.field, f32[4,8,128]{2,1,0:T(8,128)S(1)} %collective-permute-done.2.low, ...), custom_call_target="tpu_custom_call" | custom-call | tf_op jit(solution)/shard_map/block_solve_first/pallas_call | solution.py:216
  35.9 3.0 %collective-permute-start.6 = (f32[5,8,128]{2,1,0:T(8,128)S(1)}, f32[5,8,128]{2,1,0:T(8,128)S(1)}, u32[]{:S(2)}, u32[]{:S(2)}) collective-permute-start(f32[5,8,128]{2,1,0:T(8,128)S(1)} %get-tuple-element.56), channel_id=1, source_target_pairs={{0,12},{12,24},{24,36},{36,48},{48,60},{60,72},{72,84},{1,13},{13,... | collective-permute-start | bytes 61448 | tf_op jit(solution)/shard_map/ppermute | solution.py:25
  38.9 1.3 collective-permute-start.7
  40.2 4.1 %collective-permute-done.7.above = f32[5,8,128]{2,1,0:T(8,128)S(1)} collective-permute-done((f32[5,8,128]{2,1,0:T(8,128)S(1)}, f32[5,8,128]{2,1,0:T(8,128)S(1)}, u32[]{:S(2)}, u32[]{:S(2)}) %collective-permute-start.7) | collective-permute-done | bytes 20512 | tf_op jit(solution)/shard_map/ppermute | solution.py:25
  44.5 4.3 %collective-permute-start.8 = (f32[4,8,128]{2,1,0:T(8,128)S(1)}, f32[4,8,128]{2,1,0:T(8,128)S(1)}, u32[]{:S(2)}, u32[]{:S(2)}) collective-permute-start(f32[4,8,128]{2,1,0:T(8,128)S(1)} %get-tuple-element.59), channel_id=1, source_target_pairs={{0,96},{96,192},{192,288},{288,384},{384,480},{480,576},{576,672},... | collective-permute-start | bytes 49160 | tf_op jit(solution)/shard_map/ppermute | solution.py:25
  48.8 1.9 %collective-permute-start.9 = (f32[4,8,128]{2,1,0:T(8,128)S(1)}, f32[4,8,128]{2,1,0:T(8,128)S(1)}, u32[]{:S(2)}, u32[]{:S(2)}) collective-permute-start(f32[4,8,128]{2,1,0:T(8,128)S(1)} %get-tuple-element.60), channel_id=1, source_target_pairs={{96,0},{192,96},{288,192},{384,288},{480,384},{576,480},{672,576},... | collective-permute-start | bytes 49160 | tf_op jit(solution)/shard_map/ppermute | solution.py:25
  50.7 3.1 %collective-permute-done.9.high = f32[4,8,128]{2,1,0:T(8,128)S(1)} collective-permute-done((f32[4,8,128]{2,1,0:T(8,128)S(1)}, f32[4,8,128]{2,1,0:T(8,128)S(1)}, u32[]{:S(2)}, u32[]{:S(2)}) %collective-permute-start.9) | collective-permute-done | bytes 16416 | tf_op jit(solution)/shard_map/ppermute | solution.py:25
  55.0 1.9 %collective-permute-start.10 = (f32[4,8,128]{2,1,0:T(8,128)S(1)}, f32[4,8,128]{2,1,0:T(8,128)S(1)}, u32[]{:S(2)}, u32[]{:S(2)}) collective-permute-start(f32[4,8,128]{2,1,0:T(8,128)S(1)} %get-tuple-element.63), channel_id=1, source_target_pairs={{0,96},{96,192},{192,288},{288,384},{384,480},{480,576},{576,672},... | collective-permute-start | bytes 49160 | tf_op jit(solution)/shard_map/ppermute | solution.py:25
  56.9 2.4 %collective-permute-start.11 = (f32[4,8,128]{2,1,0:T(8,128)S(1)}, f32[4,8,128]{2,1,0:T(8,128)S(1)}, u32[]{:S(2)}, u32[]{:S(2)}) collective-permute-start(f32[4,8,128]{2,1,0:T(8,128)S(1)} %get-tuple-element.64), channel_id=1, source_target_pairs={{96,0},{192,96},{288,192},{384,288},{480,384},{576,480},{672,576},... | collective-permute-start | bytes 49160 | tf_op jit(solution)/shard_map/ppermute | solution.py:25
  59.3 2.6 %collective-permute-done.11.high = f32[4,8,128]{2,1,0:T(8,128)S(1)} collective-permute-done((f32[4,8,128]{2,1,0:T(8,128)S(1)}, f32[4,8,128]{2,1,0:T(8,128)S(1)}, u32[]{:S(2)}, u32[]{:S(2)}) %collective-permute-start.11) | collective-permute-done | bytes 16416 | tf_op jit(solution)/shard_map/ppermute | solution.py:25
  62.1 4.9 %collective-permute-start.12 = (f32[5,8,128]{2,1,0:T(8,128)S(1)}, f32[5,8,128]{2,1,0:T(8,128)S(1)}, u32[]{:S(2)}, u32[]{:S(2)}) collective-permute-start(f32[5,8,128]{2,1,0:T(8,128)S(1)} %get-tuple-element.65), channel_id=1, source_target_pairs={{0,12},{12,24},{24,36},{36,48},{48,60},{60,72},{72,84},{1,13},{13,... | collective-permute-start | bytes 61448 | tf_op jit(solution)/shard_map/ppermute | solution.py:25
  67.0 1.3 collective-permute-start.13
  68.3 3.5 %collective-permute-done.13.above = f32[5,8,128]{2,1,0:T(8,128)S(1)} collective-permute-done((f32[5,8,128]{2,1,0:T(8,128)S(1)}, f32[5,8,128]{2,1,0:T(8,128)S(1)}, u32[]{:S(2)}, u32[]{:S(2)}) %collective-permute-start.13) | collective-permute-done | bytes 20512 | tf_op jit(solution)/shard_map/ppermute | solution.py:25
  71.8 2.7 %block_solve_shared.1 = (f32[10,10,8,128]{3,2,1,0:T(8,128)S(1)}, f32[4,10,8,128]{3,2,1,0:T(8,128)S(1)}, f32[5,8,128]{2,1,0:T(8,128)S(1)}, f32[5,8,128]{2,1,0:T(8...) custom-call(f32[512,128]{1,0:T(8,128)S(1)} %get-tuple-element.62.field, ...), custom_call_target="tpu_custom_call" | custom-call | tf_op jit(solution)/shard_map/block_solve_shared/pallas_call | solution.py:216
  74.5 3.4 %collective-permute-start.14 = (f32[5,8,128]{2,1,0:T(8,128)S(1)}, f32[5,8,128]{2,1,0:T(8,128)S(1)}, u32[]{:S(2)}, u32[]{:S(2)}) collective-permute-start(f32[5,8,128]{2,1,0:T(8,128)S(1)} %get-tuple-element.68), channel_id=1, source_target_pairs={{0,12},{12,24},{24,36},{36,48},{48,60},{60,72},{72,84},{1,13},{13,... | collective-permute-start | bytes 61448 | tf_op jit(solution)/shard_map/ppermute | solution.py:25
  77.9 1.3 collective-permute-start.15
  79.6 2.8 %collective-permute-done.15.above = f32[5,8,128]{2,1,0:T(8,128)S(1)} collective-permute-done((f32[5,8,128]{2,1,0:T(8,128)S(1)}, f32[5,8,128]{2,1,0:T(8,128)S(1)}, u32[]{:S(2)}, u32[]{:S(2)}) %collective-permute-start.15) | collective-permute-done | bytes 20512 | tf_op jit(solution)/shard_map/ppermute | solution.py:25
  82.6 4.8 %collective-permute-start.16 = (f32[4,8,128]{2,1,0:T(8,128)S(1)}, f32[4,8,128]{2,1,0:T(8,128)S(1)}, u32[]{:S(2)}, u32[]{:S(2)}) collective-permute-start(f32[4,8,128]{2,1,0:T(8,128)S(1)} %get-tuple-element.75), channel_id=1, source_target_pairs={{0,96},{96,192},{192,288},{288,384},{384,480},{480,576},{576,672},... | collective-permute-start | bytes 49160 | tf_op jit(solution)/shard_map/ppermute | solution.py:25
  87.4 1.9 %collective-permute-start.17 = (f32[4,8,128]{2,1,0:T(8,128)S(1)}, f32[4,8,128]{2,1,0:T(8,128)S(1)}, u32[]{:S(2)}, u32[]{:S(2)}) collective-permute-start(f32[4,8,128]{2,1,0:T(8,128)S(1)} %get-tuple-element.76), channel_id=1, source_target_pairs={{96,0},{192,96},{288,192},{384,288},{480,384},{576,480},{672,576},... | collective-permute-start | bytes 49160 | tf_op jit(solution)/shard_map/ppermute | solution.py:25
  89.4 3.0 %collective-permute-done.17.high = f32[4,8,128]{2,1,0:T(8,128)S(1)} collective-permute-done((f32[4,8,128]{2,1,0:T(8,128)S(1)}, f32[4,8,128]{2,1,0:T(8,128)S(1)}, u32[]{:S(2)}, u32[]{:S(2)}) %collective-permute-start.17) | collective-permute-done | bytes 16416 | tf_op jit(solution)/shard_map/ppermute | solution.py:25
  92.4 2.0 %second_operator.1 = (f32[128,128]{1,0:T(8,128)S(1)}, f32[12,1,128]{2,1,0:T(1,128)S(1)}) custom-call(s32[3]{0:T(128)S(1)} %pad_add_fusion.spot, f32[10,10,8,128]{3,2,1,0:T(8,128)S(1)} %get-tuple-element.67.folded, f32[5,8,128]{2,1,0:T(8,128)S(1)} %collective-permute-done.14.below, f32[5,8,128]{2,1,0:T(8,128)S(1)} %collective-permute-done.15.above, ...), custom_call_target="tpu_custom_call" | custom-call | tf_op jit(solution)/shard_map/second_operator/pallas_call | solution.py:468
  94.4 23.3 %all_to_all.16.gathered = f32[12,1,128]{2,1,0:T(1,128)S(1)} all-to-all(f32[12,1,128]{2,1,0:T(1,128)S(1)} %get-tuple-element.81), channel_id=1, replica_groups=mesh['gx'=8,'gy'=8,'gz'=12] {'gz'}, dimensions={0} | all-to-all | bytes 12288 | tf_op jit(solution)/shard_map/all_to_all | solution.py:627
  118.7 19.3 %all_to_all.17 = f32[64,8,128]{2,1,0:T(8,128)S(1)} all-to-all(f32[64,8,128]{2,1,0:T(8,128)S(1)} %bitcast.23), channel_id=1, replica_groups=mesh['gx'=8,'gy'=8,'gz'=12] {'gx','gy'}, dimensions={0} | all-to-all | bytes 524288 | tf_op jit(solution)/shard_map/all_to_all | solution.py:627
  138.0 1.5 %finish.1 = (f32[64,128]{1,0:T(8,128)}, f32[64,128]{1,0:T(8,128)}) custom-call(s32[3]{0:T(128)S(1)} %pad_add_fusion.spot, f32[512,128]{1,0:T(8,128)S(1)} %bitcast.17, f32[64,128]{1,0:T(8,128)S(1)} %get-tuple-element.84.image, f32[128,128]{1,0:T(8,128)S(1)} %get-tuple-element.82.lines.second, f32[128,128]{1,0:T(8,128)S(1)} %as_lines.1.first, ...), custom_call_target="tpu_custom_call" | custom-call | tf_op jit(solution)/shard_map/finish/pallas_call | solution.py:615
  (49 shorter events, 7.9 us)
Async XLA Ops:
  2.4 6.4 %copy-start = (f32[4,8,8,128]{3,2,1,0:T(8,128)S(1)}, f32[4,8,8,128]{3,2,1,0:T(8,128)}, u32[]{:S(2)}) copy-start(f32[4,8,8,128]{3,2,1,0:T(8,128)} %param.6) | copy-start | bytes 393220
  2.4 6.4 %copy-start.1 = (f32[8,8,128]{2,1,0:T(8,128)S(1)}, f32[8,8,128]{2,1,0:T(8,128)}, u32[]{:S(2)}) copy-start(f32[8,8,128]{2,1,0:T(8,128)} %param.5) | copy-start | bytes 98308
  2.4 7.2 %copy-start.3 = (f32[32,3,10]{0,1,2:T(4,128)S(1)}, f32[32,3,10]{0,1,2:T(4,128)}, u32[]{:S(2)}) copy-start(f32[32,3,10]{0,1,2:T(4,128)} %param.9) | copy-start | bytes 11524
  2.5 7.2 %copy-start.2 = (f32[32,3,10,10]{0,1,3,2:T(4,128)S(1)}, f32[32,3,10,10]{0,1,3,2:T(4,128)}, u32[]{:S(2)}) copy-start(f32[32,3,10,10]{0,1,3,2:T(4,128)} %param.8) | copy-start | bytes 115204
  2.5 7.3 %collective-permute-start = (f32[328,32]{1,0:T(8,128)S(1)}, f32[328,32]{1,0:T(8,128)S(1)}, u32[]{:S(2)}, u32[]{:S(2)}) collective-permute-start(f32[328,32]{1,0:T(8,128)S(1)} %get-tuple-element.88), channel_id=1, source_target_pairs={{0,1},{1,2},{2,3},{3,4},{4,5},{5,6},{6,7},{7,8},{8,9},{9,10},{10,1... | collective-permute-start | bytes 125960 | tf_op jit(solution)/shard_map/ppermute | solution.py:25
  7.5 6.7 %collective-permute-start.1 = (f32[328,32]{1,0:T(8,128)S(1)}, f32[328,32]{1,0:T(8,128)S(1)}, u32[]{:S(2)}, u32[]{:S(2)}) collective-permute-start(f32[328,32]{1,0:T(8,128)S(1)} %get-tuple-element.89), channel_id=1, source_target_pairs={{1,0},{2,1},{3,2},{4,3},{5,4},{6,5},{7,6},{8,7},{9,8},{10,9},{11,1... | collective-permute-start | bytes 125960 | tf_op jit(solution)/shard_map/ppermute | solution.py:25
  14.7 12.2 %collective-permute-start.2 = (f32[4,8,128]{2,1,0:T(8,128)S(1)}, f32[4,8,128]{2,1,0:T(8,128)S(1)}, u32[]{:S(2)}, u32[]{:S(2)}) collective-permute-start(f32[4,8,128]{2,1,0:T(8,128)S(1)} %get-tuple-element.47), channel_id=1, source_target_pairs={{0,96},{96,192},{192,288},{288,384},{384,480},{480,576},{576,672},... | collective-permute-start | bytes 49160 | tf_op jit(solution)/shard_map/ppermute | solution.py:25
  20.2 6.7 %collective-permute-start.3 = (f32[4,8,128]{2,1,0:T(8,128)S(1)}, f32[4,8,128]{2,1,0:T(8,128)S(1)}, u32[]{:S(2)}, u32[]{:S(2)}) collective-permute-start(f32[4,8,128]{2,1,0:T(8,128)S(1)} %get-tuple-element.48), channel_id=1, source_target_pairs={{96,0},{192,96},{288,192},{384,288},{480,384},{576,480},{672,576},... | collective-permute-start | bytes 49160 | tf_op jit(solution)/shard_map/ppermute | solution.py:25
  27.0 2.9 %collective-permute-start.4 = (f32[5,8,128]{2,1,0:T(8,128)S(1)}, f32[5,8,128]{2,1,0:T(8,128)S(1)}, u32[]{:S(2)}, u32[]{:S(2)}) collective-permute-start(f32[5,8,128]{2,1,0:T(8,128)S(1)} %get-tuple-element.52), channel_id=1, source_target_pairs={{0,12},{12,24},{24,36},{36,48},{48,60},{60,72},{72,84},{1,13},{13,... | collective-permute-start | bytes 61448 | tf_op jit(solution)/shard_map/ppermute | solution.py:25
  28.6 4.8 %collective-permute-start.5 = (f32[5,8,128]{2,1,0:T(8,128)S(1)}, f32[5,8,128]{2,1,0:T(8,128)S(1)}, u32[]{:S(2)}, u32[]{:S(2)}) collective-permute-start(f32[5,8,128]{2,1,0:T(8,128)S(1)} %get-tuple-element.53), channel_id=1, source_target_pairs={{12,0},{24,12},{36,24},{48,36},{60,48},{72,60},{84,72},{13,1},{25,... | collective-permute-start | bytes 61448 | tf_op jit(solution)/shard_map/ppermute | solution.py:25
  35.9 4.3 %collective-permute-start.6 = (f32[5,8,128]{2,1,0:T(8,128)S(1)}, f32[5,8,128]{2,1,0:T(8,128)S(1)}, u32[]{:S(2)}, u32[]{:S(2)}) collective-permute-start(f32[5,8,128]{2,1,0:T(8,128)S(1)} %get-tuple-element.56), channel_id=1, source_target_pairs={{0,12},{12,24},{24,36},{36,48},{48,60},{60,72},{72,84},{1,13},{13,... | collective-permute-start | bytes 61448 | tf_op jit(solution)/shard_map/ppermute | solution.py:25
  38.9 5.4 %collective-permute-start.7 = (f32[5,8,128]{2,1,0:T(8,128)S(1)}, f32[5,8,128]{2,1,0:T(8,128)S(1)}, u32[]{:S(2)}, u32[]{:S(2)}) collective-permute-start(f32[5,8,128]{2,1,0:T(8,128)S(1)} %get-tuple-element.57), channel_id=1, source_target_pairs={{12,0},{24,12},{36,24},{48,36},{60,48},{72,60},{84,72},{13,1},{25,... | collective-permute-start | bytes 61448 | tf_op jit(solution)/shard_map/ppermute | solution.py:25
  44.5 6.3 %collective-permute-start.8 = (f32[4,8,128]{2,1,0:T(8,128)S(1)}, f32[4,8,128]{2,1,0:T(8,128)S(1)}, u32[]{:S(2)}, u32[]{:S(2)}) collective-permute-start(f32[4,8,128]{2,1,0:T(8,128)S(1)} %get-tuple-element.59), channel_id=1, source_target_pairs={{0,96},{96,192},{192,288},{288,384},{384,480},{480,576},{576,672},... | collective-permute-start | bytes 49160 | tf_op jit(solution)/shard_map/ppermute | solution.py:25
  48.8 5.1 %collective-permute-start.9 = (f32[4,8,128]{2,1,0:T(8,128)S(1)}, f32[4,8,128]{2,1,0:T(8,128)S(1)}, u32[]{:S(2)}, u32[]{:S(2)}) collective-permute-start(f32[4,8,128]{2,1,0:T(8,128)S(1)} %get-tuple-element.60), channel_id=1, source_target_pairs={{96,0},{192,96},{288,192},{384,288},{480,384},{576,480},{672,576},... | collective-permute-start | bytes 49160 | tf_op jit(solution)/shard_map/ppermute | solution.py:25
  55.0 4.3 %collective-permute-start.10 = (f32[4,8,128]{2,1,0:T(8,128)S(1)}, f32[4,8,128]{2,1,0:T(8,128)S(1)}, u32[]{:S(2)}, u32[]{:S(2)}) collective-permute-start(f32[4,8,128]{2,1,0:T(8,128)S(1)} %get-tuple-element.63), channel_id=1, source_target_pairs={{0,96},{96,192},{192,288},{288,384},{384,480},{480,576},{576,672},... | collective-permute-start | bytes 49160 | tf_op jit(solution)/shard_map/ppermute | solution.py:25
  56.9 5.1 %collective-permute-start.11 = (f32[4,8,128]{2,1,0:T(8,128)S(1)}, f32[4,8,128]{2,1,0:T(8,128)S(1)}, u32[]{:S(2)}, u32[]{:S(2)}) collective-permute-start(f32[4,8,128]{2,1,0:T(8,128)S(1)} %get-tuple-element.64), channel_id=1, source_target_pairs={{96,0},{192,96},{288,192},{384,288},{480,384},{576,480},{672,576},... | collective-permute-start | bytes 49160 | tf_op jit(solution)/shard_map/ppermute | solution.py:25
  62.1 6.2 %collective-permute-start.12 = (f32[5,8,128]{2,1,0:T(8,128)S(1)}, f32[5,8,128]{2,1,0:T(8,128)S(1)}, u32[]{:S(2)}, u32[]{:S(2)}) collective-permute-start(f32[5,8,128]{2,1,0:T(8,128)S(1)} %get-tuple-element.65), channel_id=1, source_target_pairs={{0,12},{12,24},{24,36},{36,48},{48,60},{60,72},{72,84},{1,13},{13,... | collective-permute-start | bytes 61448 | tf_op jit(solution)/shard_map/ppermute | solution.py:25
  67.0 4.8 %collective-permute-start.13 = (f32[5,8,128]{2,1,0:T(8,128)S(1)}, f32[5,8,128]{2,1,0:T(8,128)S(1)}, u32[]{:S(2)}, u32[]{:S(2)}) collective-permute-start(f32[5,8,128]{2,1,0:T(8,128)S(1)} %get-tuple-element.66), channel_id=1, source_target_pairs={{12,0},{24,12},{36,24},{48,36},{60,48},{72,60},{84,72},{13,1},{25,... | collective-permute-start | bytes 61448 | tf_op jit(solution)/shard_map/ppermute | solution.py:25
  74.5 5.0 %collective-permute-start.14 = (f32[5,8,128]{2,1,0:T(8,128)S(1)}, f32[5,8,128]{2,1,0:T(8,128)S(1)}, u32[]{:S(2)}, u32[]{:S(2)}) collective-permute-start(f32[5,8,128]{2,1,0:T(8,128)S(1)} %get-tuple-element.68), channel_id=1, source_target_pairs={{0,12},{12,24},{24,36},{36,48},{48,60},{60,72},{72,84},{1,13},{13,... | collective-permute-start | bytes 61448 | tf_op jit(solution)/shard_map/ppermute | solution.py:25
  77.9 4.5 %collective-permute-start.15 = (f32[5,8,128]{2,1,0:T(8,128)S(1)}, f32[5,8,128]{2,1,0:T(8,128)S(1)}, u32[]{:S(2)}, u32[]{:S(2)}) collective-permute-start(f32[5,8,128]{2,1,0:T(8,128)S(1)} %get-tuple-element.69), channel_id=1, source_target_pairs={{12,0},{24,12},{36,24},{48,36},{60,48},{72,60},{84,72},{13,1},{25,... | collective-permute-start | bytes 61448 | tf_op jit(solution)/shard_map/ppermute | solution.py:25
  82.6 6.8 %collective-permute-start.16 = (f32[4,8,128]{2,1,0:T(8,128)S(1)}, f32[4,8,128]{2,1,0:T(8,128)S(1)}, u32[]{:S(2)}, u32[]{:S(2)}) collective-permute-start(f32[4,8,128]{2,1,0:T(8,128)S(1)} %get-tuple-element.75), channel_id=1, source_target_pairs={{0,96},{96,192},{192,288},{288,384},{384,480},{480,576},{576,672},... | collective-permute-start | bytes 49160 | tf_op jit(solution)/shard_map/ppermute | solution.py:25
  87.4 5.1 %collective-permute-start.17 = (f32[4,8,128]{2,1,0:T(8,128)S(1)}, f32[4,8,128]{2,1,0:T(8,128)S(1)}, u32[]{:S(2)}, u32[]{:S(2)}) collective-permute-start(f32[4,8,128]{2,1,0:T(8,128)S(1)} %get-tuple-element.76), channel_id=1, source_target_pairs={{96,0},{192,96},{288,192},{384,288},{480,384},{576,480},{672,576},... | collective-permute-start | bytes 49160 | tf_op jit(solution)/shard_map/ppermute | solution.py:25

commit v5 on v4

--- a/solution.py
+++ b/solution.py
@@ -217,7 +217,7 @@
         functools.partial(solve_kernel, count, shared),
         out_shape=outs,
         scratch_shapes=[pltpu.VMEM((1040, LANES), jnp.float32)] * 3
-        + [pltpu.VMEM((104, LANES), jnp.float32)],
+        + [pltpu.VMEM((112, LANES), jnp.float32)],
         in_specs=[VMEM] * 7,
         out_specs=[VMEM] * len(outs),
         compiler_params=ROOM,
@@ -316,6 +316,48 @@
             out[spot, :] = value if base is None else value + base[spot, :]
 
 
+def lane_groups(width, pieces, start):
+    lane = lax.broadcasted_iota(jnp.int32, pieces[0].shape, 1)
+    total = jnp.zeros(pieces[0].shape, jnp.float32)
+    for slot, piece in enumerate(pieces):
+        shift = (width * slot - start) % LANES
+        moved = pltpu.roll(piece, shift, 1) if shift else piece
+        total = jnp.where(lane // width == slot, moved, total)
+    return total
+
+
+def ends_kernel(right_side, geometry, classes, backward, forward):
+    field = [right_side[pl.ds(16 * i, 16), :] for i in range(4)]
+    metric = [geometry[pl.ds(32 * i, 32), :] for i in range(8)]
+    for out, from_end in ((backward, False), (forward, True)):
+        out[pl.ds(0, 16), :] = lane_groups(32, field, LANES - 32 if from_end else 0)
+        out[pl.ds(16, 32), :] = lane_groups(16, metric, LANES - 16 if from_end else 0)
+        out[pl.ds(48, 8), :] = jnp.zeros((8, LANES), jnp.float32)
+        out[pl.ds(48, 1), 0 : classes.shape[1]] = classes[...].astype(jnp.float32)
+
+
+def end_messages(right_side, geometry, classes):
+    return pl.pallas_call(
+        ends_kernel,
+        out_shape=[pltpu.VMEM((56, LANES), jnp.float32)] * 2,
+        in_specs=[VMEM] * 3,
+        out_specs=[VMEM] * 2,
+        compiler_params=ROOM,
+        name="end_messages",
+    )(*near(right_side, geometry, classes))
+
+
+def received_lines(low, high, first, rows, width):
+    low, high = low[pl.ds(first, rows), :], high[pl.ds(first, rows), :]
+    lane = lax.broadcasted_iota(jnp.int32, (rows, LANES), 1)
+    lines = []
+    for slot in range(LANES // width):
+        before = pltpu.roll(low, (-width * slot) % LANES, 1) if slot else low
+        after = pltpu.roll(high, (width - width * slot) % LANES, 1) if slot != 1 else high
+        lines.append(jnp.where(lane < width, before, jnp.where(lane < 2 * width, after, 0.0)))
+    return jnp.concatenate(lines, axis=0)
+
+
 def own_lines_kernel(right_side, geometry, field, metric):
     spread_lines(right_side[...], lambda e: e + REACH, field)
     spread_lines(geometry[...], lambda e: e + REACH, metric)
@@ -340,24 +382,28 @@
     pack(forward, [field[pl.ds(384 + 8 * i, 8), :] for i in range(16)])
 
 
-def end_lines_kernel(count, with_edges, ends, own, out, *edges):
-    spread_lines(ends[...], lambda e: jnp.where(e < REACH, e, e + count), out, own)
-    if with_edges:
+def end_lines_kernel(count, field_too, low, high, own, out, *edges):
+    if field_too:
+        lines = received_lines(low, high, 0, 16, 32)
+        spread_lines(lines, lambda e: jnp.where(e < REACH, e, e + count), out, own)
         pack_ends(out, *edges)
-
-
-def end_lines(ends, own, count, with_edges):
+    else:
+        lines = received_lines(low, high, 16, 32, 16)
+        spread_lines(lines, lambda e: e + REACH - 2 + jnp.where(e < 2, 0, count), out, own)
+
+
+def end_lines(low, high, own, count, field_too):
     outs = [pltpu.VMEM(own.shape, jnp.float32)]
-    if with_edges:
+    if field_too:
         outs += [pltpu.VMEM((4, 8, LANES), jnp.float32)] * 2
     return pl.pallas_call(
-        functools.partial(end_lines_kernel, count, with_edges),
+        functools.partial(end_lines_kernel, count, field_too),
         out_shape=outs,
-        in_specs=[VMEM] * 2,
+        in_specs=[VMEM] * 3,
         out_specs=[VMEM] * len(outs),
         compiler_params=ROOM,
-        name="end_lines_field" if with_edges else "end_lines_metric",
-    )(*near(ends, own))
+        name="end_lines_field" if field_too else "end_lines_metric",
+    )(*near(low, high, own))
 
 
 def apply_local(derivative, folded, below, above, low, high, geometry, field, image):
@@ -633,20 +679,18 @@
     depth = lax.axis_size("gz")
     sizes = (lax.axis_size("gx"), lax.axis_size("gy"))
     spot = jnp.stack([lax.axis_index(a).astype(jnp.int32) for a in ("gx", "gy", "gz")])
-    ends = 8 * REACH
     lines = right_side.reshape(64, LANES)
     metric_lines = geometry.reshape(256, LANES)
-    class_lines = jnp.broadcast_to(
-        jnp.repeat(element_shape_class.reshape(1, -1), 8, axis=1).astype(jnp.float32),
-        (8, 8 * count),
-    )
-    stack = jnp.concatenate([lines, class_lines, metric_lines], axis=0)
-    low, high = swap(stack[:, :ends], stack[:, -ends:], "gz")
+    flat_class = element_shape_class.reshape(1, count)
+    before, after = swap(*end_messages(lines, metric_lines, flat_class), "gz")
     own_field, own_metric = own_lines(lines, metric_lines)
-    outer = jnp.concatenate([low, high], axis=1)
     deep_class = jnp.concatenate(
-        [low[64, ::8], element_shape_class.reshape(-1).astype(jnp.float32), high[64, ::8]]
-    ).astype(jnp.int32)
+        [
+            before[48, count - REACH : count].astype(jnp.int32),
+            flat_class[0],
+            after[48, :REACH].astype(jnp.int32),
+        ]
+    )
     deep_class = jnp.pad(deep_class, (0, LANES - deep_class.shape[0]))
     element = jnp.arange(LANES, dtype=jnp.int32) - REACH + spot[2] * count
     valid = ((element >= 0) & (element < depth * count)).astype(jnp.float32)[None, :]
@@ -659,9 +703,9 @@
     table = lax.dot_general(
         entries, onehot, (((0,), (0,)), ((), ())), precision=HIGHEST
     )
-    field, backward, forward = end_lines(outer[:64], own_field, count, True)
+    field, backward, forward = end_lines(before, after, own_field, count, True)
     low, high = swap(backward, forward, "gx")
-    (metric,) = end_lines(outer[72:], own_metric, count, False)
+    (metric,) = end_lines(before, after, own_metric, count, False)
     low, high, metric, table = lax.optimization_barrier((low, high, metric, table))
     below, above = swap(*second_edges(field, low, high, False), "gy")
     folded, rims, backward, forward, rho = block_solve(

time: 140 us -> 139 us (level)
  local copies, waits for them, and re-layouts: 0.7 us -> 2.56 us
  waiting for transfers between devices: 27.1 us -> 25.4 us
  other arithmetic: 1.93 us -> 0.25 us
    unnamed x10 -> x14, local copies, waits for them, and re-layouts: 0.05 us -> 2.35 us
    ppermute x9, waiting for transfers between devices: 27.1 us -> 25.4 us  [swap(): lax.ppermute(backward_part, axis, backward)]
where the time goes in v5:
time: 139 us; the launch traced here: 138 us
  starting transfers between devices  51.7 us (37%)
  blocking collectives  42.8 us (31%)
  waiting for transfers between devices  25.4 us (18%)
  Pallas kernels  13.9 us (10%)
  local copies, waits for them, and re-layouts  2.56 us (2%)
    all_to_all x2, blocking collectives, exchange(): return lax.all_to_all(rows, axes, 0, 0, tiled=True)  42.8 us
    ppermute x9, starting transfers between devices, swap(): lax.ppermute(forward_part, axis, forward)  33.1 us
    ppermute x9, waiting for transfers between devices, swap(): lax.ppermute(backward_part, axis, backward)  25.4 us
    ppermute x9, starting transfers between devices, swap(): lax.ppermute(backward_part, axis, backward)  18.6 us
    pallas_call x2, Pallas kernels, block_solve(): pl.pallas_call(functools.partial(solve_kernel, count, shared), out_shape=...  5.23 us
  transfers between devices with their start and end apart: 18, of which 8 were waited for; matrix products, arithmetic and copies ran while one was open for 1% of the time, Pallas kernels for 1%

profile of v5, /device:TPU:1, one launch (start us, length us, event | category | flops | bytes accessed | tf_op | source)
XLA Modules:
  0.0 138.0 jit_solution(18310894101303055720)
XLA Ops:
  3.1 4.8 %collective-permute-start = (f32[56,128]{1,0:T(8,128)S(1)}, f32[56,128]{1,0:T(8,128)S(1)}, u32[]{:S(2)}, u32[]{:S(2)}) collective-permute-start(f32[56,128]{1,0:T(8,128)S(1)} %get-tuple-element.47), channel_id=1, source_target_pairs={{0,1},{1,2},{2,3},{3,4},{4,5},{5,6},{6,7},{7,8},{8,9},{9,10},{10,1... | collective-permute-start | bytes 86024 | tf_op jit(solution)/shard_map/ppermute | solution.py:25
  7.9 1.3 collective-permute-start.1
  10.3 2.9 %collective-permute-done.1.high = f32[56,128]{1,0:T(8,128)S(1)} collective-permute-done((f32[56,128]{1,0:T(8,128)S(1)}, f32[56,128]{1,0:T(8,128)S(1)}, u32[]{:S(2)}, u32[]{:S(2)}) %collective-permute-start.1) | collective-permute-done | bytes 28704 | tf_op jit(solution)/shard_map/ppermute | solution.py:25
  13.6 4.8 %collective-permute-start.2 = (f32[4,8,128]{2,1,0:T(8,128)S(1)}, f32[4,8,128]{2,1,0:T(8,128)S(1)}, u32[]{:S(2)}, u32[]{:S(2)}) collective-permute-start(f32[4,8,128]{2,1,0:T(8,128)S(1)} %get-tuple-element.51), channel_id=1, source_target_pairs={{0,96},{96,192},{192,288},{288,384},{384,480},{480,576},{576,672},... | collective-permute-start | bytes 49160 | tf_op jit(solution)/shard_map/ppermute | solution.py:25
  18.4 5.9 %collective-permute-start.3 = (f32[4,8,128]{2,1,0:T(8,128)S(1)}, f32[4,8,128]{2,1,0:T(8,128)S(1)}, u32[]{:S(2)}, u32[]{:S(2)}) collective-permute-start(f32[4,8,128]{2,1,0:T(8,128)S(1)} %get-tuple-element.52), channel_id=1, source_target_pairs={{96,0},{192,96},{288,192},{384,288},{480,384},{576,480},{672,576},... | collective-permute-start | bytes 49160 | tf_op jit(solution)/shard_map/ppermute | solution.py:25
  25.8 1.3 collective-permute-start.4
  27.1 1.3 collective-permute-start.5
  28.4 3.2 %collective-permute-done.5.above = f32[5,8,128]{2,1,0:T(8,128)S(1)} collective-permute-done((f32[5,8,128]{2,1,0:T(8,128)S(1)}, f32[5,8,128]{2,1,0:T(8,128)S(1)}, u32[]{:S(2)}, u32[]{:S(2)}) %collective-permute-start.5) | collective-permute-done | bytes 20512 | tf_op jit(solution)/shard_map/ppermute | solution.py:25
  31.6 2.5 %block_solve_first.1 = (f32[10,10,8,128]{3,2,1,0:T(8,128)S(1)}, f32[4,10,8,128]{3,2,1,0:T(8,128)S(1)}, f32[5,8,128]{2,1,0:T(8,128)S(1)}, f32[5,8,128]{2,1,0:T(8,128)S(1)}, f32[1,128]{1,0:T(1,128)S(1)}) custom-call(f32[512,128]{1,0:T(8,128)S(1)} %get-tuple-element.50.field, f32[4,8,128]{2,1,0:T(8,128)S(1)} %collective-permute-done.2.low, ...), custom_call_target="tpu_custom_call" | custom-call | tf_op jit(solution)/shard_map/block_solve_first/pallas_call | solution.py:216
  34.2 3.0 %collective-permute-start.6 = (f32[5,8,128]{2,1,0:T(8,128)S(1)}, f32[5,8,128]{2,1,0:T(8,128)S(1)}, u32[]{:S(2)}, u32[]{:S(2)}) collective-permute-start(f32[5,8,128]{2,1,0:T(8,128)S(1)} %get-tuple-element.60), channel_id=1, source_target_pairs={{0,12},{12,24},{24,36},{36,48},{48,60},{60,72},{72,84},{1,13},{13,... | collective-permute-start | bytes 61448 | tf_op jit(solution)/shard_map/ppermute | solution.py:25
  37.1 1.3 collective-permute-start.7
  38.4 4.1 %collective-permute-done.7.above = f32[5,8,128]{2,1,0:T(8,128)S(1)} collective-permute-done((f32[5,8,128]{2,1,0:T(8,128)S(1)}, f32[5,8,128]{2,1,0:T(8,128)S(1)}, u32[]{:S(2)}, u32[]{:S(2)}) %collective-permute-start.7) | collective-permute-done | bytes 20512 | tf_op jit(solution)/shard_map/ppermute | solution.py:25
  42.7 4.2 %collective-permute-start.8 = (f32[4,8,128]{2,1,0:T(8,128)S(1)}, f32[4,8,128]{2,1,0:T(8,128)S(1)}, u32[]{:S(2)}, u32[]{:S(2)}) collective-permute-start(f32[4,8,128]{2,1,0:T(8,128)S(1)} %get-tuple-element.63), channel_id=1, source_target_pairs={{0,96},{96,192},{192,288},{288,384},{384,480},{480,576},{576,672},... | collective-permute-start | bytes 49160 | tf_op jit(solution)/shard_map/ppermute | solution.py:25
  47.0 1.9 %collective-permute-start.9 = (f32[4,8,128]{2,1,0:T(8,128)S(1)}, f32[4,8,128]{2,1,0:T(8,128)S(1)}, u32[]{:S(2)}, u32[]{:S(2)}) collective-permute-start(f32[4,8,128]{2,1,0:T(8,128)S(1)} %get-tuple-element.64), channel_id=1, source_target_pairs={{96,0},{192,96},{288,192},{384,288},{480,384},{576,480},{672,576},... | collective-permute-start | bytes 49160 | tf_op jit(solution)/shard_map/ppermute | solution.py:25
  48.9 3.1 %collective-permute-done.9.high = f32[4,8,128]{2,1,0:T(8,128)S(1)} collective-permute-done((f32[4,8,128]{2,1,0:T(8,128)S(1)}, f32[4,8,128]{2,1,0:T(8,128)S(1)}, u32[]{:S(2)}, u32[]{:S(2)}) %collective-permute-start.9) | collective-permute-done | bytes 16416 | tf_op jit(solution)/shard_map/ppermute | solution.py:25
  53.1 1.9 %collective-permute-start.10 = (f32[4,8,128]{2,1,0:T(8,128)S(1)}, f32[4,8,128]{2,1,0:T(8,128)S(1)}, u32[]{:S(2)}, u32[]{:S(2)}) collective-permute-start(f32[4,8,128]{2,1,0:T(8,128)S(1)} %get-tuple-element.67), channel_id=1, source_target_pairs={{0,96},{96,192},{192,288},{288,384},{384,480},{480,576},{576,672},... | collective-permute-start | bytes 49160 | tf_op jit(solution)/shard_map/ppermute | solution.py:25
  55.1 2.4 %collective-permute-start.11 = (f32[4,8,128]{2,1,0:T(8,128)S(1)}, f32[4,8,128]{2,1,0:T(8,128)S(1)}, u32[]{:S(2)}, u32[]{:S(2)}) collective-permute-start(f32[4,8,128]{2,1,0:T(8,128)S(1)} %get-tuple-element.68), channel_id=1, source_target_pairs={{96,0},{192,96},{288,192},{384,288},{480,384},{576,480},{672,576},... | collective-permute-start | bytes 49160 | tf_op jit(solution)/shard_map/ppermute | solution.py:25
  57.5 2.6 %collective-permute-done.11.high = f32[4,8,128]{2,1,0:T(8,128)S(1)} collective-permute-done((f32[4,8,128]{2,1,0:T(8,128)S(1)}, f32[4,8,128]{2,1,0:T(8,128)S(1)}, u32[]{:S(2)}, u32[]{:S(2)}) %collective-permute-start.11) | collective-permute-done | bytes 16416 | tf_op jit(solution)/shard_map/ppermute | solution.py:25
  60.3 4.9 %collective-permute-start.12 = (f32[5,8,128]{2,1,0:T(8,128)S(1)}, f32[5,8,128]{2,1,0:T(8,128)S(1)}, u32[]{:S(2)}, u32[]{:S(2)}) collective-permute-start(f32[5,8,128]{2,1,0:T(8,128)S(1)} %get-tuple-element.69), channel_id=1, source_target_pairs={{0,12},{12,24},{24,36},{36,48},{48,60},{60,72},{72,84},{1,13},{13,... | collective-permute-start | bytes 61448 | tf_op jit(solution)/shard_map/ppermute | solution.py:25
  65.2 1.3 collective-permute-start.13
  66.5 3.5 %collective-permute-done.13.above = f32[5,8,128]{2,1,0:T(8,128)S(1)} collective-permute-done((f32[5,8,128]{2,1,0:T(8,128)S(1)}, f32[5,8,128]{2,1,0:T(8,128)S(1)}, u32[]{:S(2)}, u32[]{:S(2)}) %collective-permute-start.13) | collective-permute-done | bytes 20512 | tf_op jit(solution)/shard_map/ppermute | solution.py:25
  70.0 2.7 %block_solve_shared.1 = (f32[10,10,8,128]{3,2,1,0:T(8,128)S(1)}, f32[4,10,8,128]{3,2,1,0:T(8,128)S(1)}, f32[5,8,128]{2,1,0:T(8,128)S(1)}, f32[5,8,128]{2,1,0:T(8...) custom-call(f32[512,128]{1,0:T(8,128)S(1)} %get-tuple-element.66.field, ...), custom_call_target="tpu_custom_call" | custom-call | tf_op jit(solution)/shard_map/block_solve_shared/pallas_call | solution.py:216
  72.7 3.4 %collective-permute-start.14 = (f32[5,8,128]{2,1,0:T(8,128)S(1)}, f32[5,8,128]{2,1,0:T(8,128)S(1)}, u32[]{:S(2)}, u32[]{:S(2)}) collective-permute-start(f32[5,8,128]{2,1,0:T(8,128)S(1)} %get-tuple-element.72), channel_id=1, source_target_pairs={{0,12},{12,24},{24,36},{36,48},{48,60},{60,72},{72,84},{1,13},{13,... | collective-permute-start | bytes 61448 | tf_op jit(solution)/shard_map/ppermute | solution.py:25
  76.0 1.3 collective-permute-start.15
  77.7 2.8 %collective-permute-done.15.above = f32[5,8,128]{2,1,0:T(8,128)S(1)} collective-permute-done((f32[5,8,128]{2,1,0:T(8,128)S(1)}, f32[5,8,128]{2,1,0:T(8,128)S(1)}, u32[]{:S(2)}, u32[]{:S(2)}) %collective-permute-start.15) | collective-permute-done | bytes 20512 | tf_op jit(solution)/shard_map/ppermute | solution.py:25
  80.7 4.8 %collective-permute-start.16 = (f32[4,8,128]{2,1,0:T(8,128)S(1)}, f32[4,8,128]{2,1,0:T(8,128)S(1)}, u32[]{:S(2)}, u32[]{:S(2)}) collective-permute-start(f32[4,8,128]{2,1,0:T(8,128)S(1)} %get-tuple-element.79), channel_id=1, source_target_pairs={{0,96},{96,192},{192,288},{288,384},{384,480},{480,576},{576,672},... | collective-permute-start | bytes 49160 | tf_op jit(solution)/shard_map/ppermute | solution.py:25
  85.5 1.9 %collective-permute-start.17 = (f32[4,8,128]{2,1,0:T(8,128)S(1)}, f32[4,8,128]{2,1,0:T(8,128)S(1)}, u32[]{:S(2)}, u32[]{:S(2)}) collective-permute-start(f32[4,8,128]{2,1,0:T(8,128)S(1)} %get-tuple-element.80), channel_id=1, source_target_pairs={{96,0},{192,96},{288,192},{384,288},{480,384},{576,480},{672,576},... | collective-permute-start | bytes 49160 | tf_op jit(solution)/shard_map/ppermute | solution.py:25
  87.5 3.0 %collective-permute-done.17.high = f32[4,8,128]{2,1,0:T(8,128)S(1)} collective-permute-done((f32[4,8,128]{2,1,0:T(8,128)S(1)}, f32[4,8,128]{2,1,0:T(8,128)S(1)}, u32[]{:S(2)}, u32[]{:S(2)}) %collective-permute-start.17) | collective-permute-done | bytes 16416 | tf_op jit(solution)/shard_map/ppermute | solution.py:25
  90.6 2.0 %second_operator.1 = (f32[128,128]{1,0:T(8,128)S(1)}, f32[12,1,128]{2,1,0:T(1,128)S(1)}) custom-call(s32[3]{0:T(128)S(1)} %pad_add_fusion.spot, f32[10,10,8,128]{3,2,1,0:T(8,128)S(1)} %get-tuple-element.71.folded, f32[5,8,128]{2,1,0:T(8,128)S(1)} %collective-permute-done.14.below, f32[5,8,128]{2,1,0:T(8,128)S(1)} %collective-permute-done.15.above, ...), custom_call_target="tpu_custom_call" | custom-call | tf_op jit(solution)/shard_map/second_operator/pallas_call | solution.py:514
  92.6 23.5 %all_to_all.16.gathered = f32[12,1,128]{2,1,0:T(1,128)S(1)} all-to-all(f32[12,1,128]{2,1,0:T(1,128)S(1)} %get-tuple-element.85), channel_id=1, replica_groups=mesh['gx'=8,'gy'=8,'gz'=12] {'gz'}, dimensions={0} | all-to-all | bytes 12288 | tf_op jit(solution)/shard_map/all_to_all | solution.py:673
  117.1 19.3 %all_to_all.17 = f32[64,8,128]{2,1,0:T(8,128)S(1)} all-to-all(f32[64,8,128]{2,1,0:T(8,128)S(1)} %bitcast.25), channel_id=1, replica_groups=mesh['gx'=8,'gy'=8,'gz'=12] {'gx','gy'}, dimensions={0} | all-to-all | bytes 524288 | tf_op jit(solution)/shard_map/all_to_all | solution.py:673
  136.4 1.5 %finish.1 = (f32[64,128]{1,0:T(8,128)}, f32[64,128]{1,0:T(8,128)}) custom-call(s32[3]{0:T(128)S(1)} %pad_add_fusion.spot, f32[512,128]{1,0:T(8,128)S(1)} %bitcast.19, f32[64,128]{1,0:T(8,128)S(1)} %get-tuple-element.88.image, f32[128,128]{1,0:T(8,128)S(1)} %get-tuple-element.86.lines.second, f32[128,128]{1,0:T(8,128)S(1)} %as_lines.1.first, ...), custom_call_target="tpu_custom_call" | custom-call | tf_op jit(solution)/shard_map/finish/pallas_call | solution.py:661
  (46 shorter events, 8.3 us)
Async XLA Ops:
  0.6 0.7 copy-start.3
  1.3 0.9 copy-start
  2.2 0.8 copy-start.1
  3.0 7.2 %copy-start.4 = (f32[32,3,10,10]{0,1,3,2:T(4,128)S(1)}, f32[32,3,10,10]{0,1,3,2:T(4,128)}, u32[]{:S(2)}) copy-start(f32[32,3,10,10]{0,1,3,2:T(4,128)} %param.8) | copy-start | bytes 115204
  3.1 7.2 %collective-permute-start = (f32[56,128]{1,0:T(8,128)S(1)}, f32[56,128]{1,0:T(8,128)S(1)}, u32[]{:S(2)}, u32[]{:S(2)}) collective-permute-start(f32[56,128]{1,0:T(8,128)S(1)} %get-tuple-element.47), channel_id=1, source_target_pairs={{0,1},{1,2},{2,3},{3,4},{4,5},{5,6},{6,7},{7,8},{8,9},{9,10},{10,1... | collective-permute-start | bytes 86024 | tf_op jit(solution)/shard_map/ppermute | solution.py:25
  7.9 5.3 %collective-permute-start.1 = (f32[56,128]{1,0:T(8,128)S(1)}, f32[56,128]{1,0:T(8,128)S(1)}, u32[]{:S(2)}, u32[]{:S(2)}) collective-permute-start(f32[56,128]{1,0:T(8,128)S(1)} %get-tuple-element.48), channel_id=1, source_target_pairs={{1,0},{2,1},{3,2},{4,3},{5,4},{6,5},{7,6},{8,7},{9,8},{10,9},{11,1... | collective-permute-start | bytes 86024 | tf_op jit(solution)/shard_map/ppermute | solution.py:25
  9.2 0.8 copy-start.5
  13.6 12.0 %collective-permute-start.2 = (f32[4,8,128]{2,1,0:T(8,128)S(1)}, f32[4,8,128]{2,1,0:T(8,128)S(1)}, u32[]{:S(2)}, u32[]{:S(2)}) collective-permute-start(f32[4,8,128]{2,1,0:T(8,128)S(1)} %get-tuple-element.51), channel_id=1, source_target_pairs={{0,96},{96,192},{192,288},{288,384},{384,480},{480,576},{576,672},... | collective-permute-start | bytes 49160 | tf_op jit(solution)/shard_map/ppermute | solution.py:25
  18.4 7.2 %collective-permute-start.3 = (f32[4,8,128]{2,1,0:T(8,128)S(1)}, f32[4,8,128]{2,1,0:T(8,128)S(1)}, u32[]{:S(2)}, u32[]{:S(2)}) collective-permute-start(f32[4,8,128]{2,1,0:T(8,128)S(1)} %get-tuple-element.52), channel_id=1, source_target_pairs={{96,0},{192,96},{288,192},{384,288},{480,384},{576,480},{672,576},... | collective-permute-start | bytes 49160 | tf_op jit(solution)/shard_map/ppermute | solution.py:25
  25.8 2.6 %collective-permute-start.4 = (f32[5,8,128]{2,1,0:T(8,128)S(1)}, f32[5,8,128]{2,1,0:T(8,128)S(1)}, u32[]{:S(2)}, u32[]{:S(2)}) collective-permute-start(f32[5,8,128]{2,1,0:T(8,128)S(1)} %get-tuple-element.56), channel_id=1, source_target_pairs={{0,12},{12,24},{24,36},{36,48},{48,60},{60,72},{72,84},{1,13},{13,... | collective-permute-start | bytes 61448 | tf_op jit(solution)/shard_map/ppermute | solution.py:25
  27.1 4.5 %collective-permute-start.5 = (f32[5,8,128]{2,1,0:T(8,128)S(1)}, f32[5,8,128]{2,1,0:T(8,128)S(1)}, u32[]{:S(2)}, u32[]{:S(2)}) collective-permute-start(f32[5,8,128]{2,1,0:T(8,128)S(1)} %get-tuple-element.57), channel_id=1, source_target_pairs={{12,0},{24,12},{36,24},{48,36},{60,48},{72,60},{84,72},{13,1},{25,... | collective-permute-start | bytes 61448 | tf_op jit(solution)/shard_map/ppermute | solution.py:25
  34.2 4.3 %collective-permute-start.6 = (f32[5,8,128]{2,1,0:T(8,128)S(1)}, f32[5,8,128]{2,1,0:T(8,128)S(1)}, u32[]{:S(2)}, u32[]{:S(2)}) collective-permute-start(f32[5,8,128]{2,1,0:T(8,128)S(1)} %get-tuple-element.60), channel_id=1, source_target_pairs={{0,12},{12,24},{24,36},{36,48},{48,60},{60,72},{72,84},{1,13},{13,... | collective-permute-start | bytes 61448 | tf_op jit(solution)/shard_map/ppermute | solution.py:25
  37.1 5.4 %collective-permute-start.7 = (f32[5,8,128]{2,1,0:T(8,128)S(1)}, f32[5,8,128]{2,1,0:T(8,128)S(1)}, u32[]{:S(2)}, u32[]{:S(2)}) collective-permute-start(f32[5,8,128]{2,1,0:T(8,128)S(1)} %get-tuple-element.61), channel_id=1, source_target_pairs={{12,0},{24,12},{36,24},{48,36},{60,48},{72,60},{84,72},{13,1},{25,... | collective-permute-start | bytes 61448 | tf_op jit(solution)/shard_map/ppermute | solution.py:25
  42.7 6.2 %collective-permute-start.8 = (f32[4,8,128]{2,1,0:T(8,128)S(1)}, f32[4,8,128]{2,1,0:T(8,128)S(1)}, u32[]{:S(2)}, u32[]{:S(2)}) collective-permute-start(f32[4,8,128]{2,1,0:T(8,128)S(1)} %get-tuple-element.63), channel_id=1, source_target_pairs={{0,96},{96,192},{192,288},{288,384},{384,480},{480,576},{576,672},... | collective-permute-start | bytes 49160 | tf_op jit(solution)/shard_map/ppermute | solution.py:25
  47.0 5.1 %collective-permute-start.9 = (f32[4,8,128]{2,1,0:T(8,128)S(1)}, f32[4,8,128]{2,1,0:T(8,128)S(1)}, u32[]{:S(2)}, u32[]{:S(2)}) collective-permute-start(f32[4,8,128]{2,1,0:T(8,128)S(1)} %get-tuple-element.64), channel_id=1, source_target_pairs={{96,0},{192,96},{288,192},{384,288},{480,384},{576,480},{672,576},... | collective-permute-start | bytes 49160 | tf_op jit(solution)/shard_map/ppermute | solution.py:25
  53.1 4.3 %collective-permute-start.10 = (f32[4,8,128]{2,1,0:T(8,128)S(1)}, f32[4,8,128]{2,1,0:T(8,128)S(1)}, u32[]{:S(2)}, u32[]{:S(2)}) collective-permute-start(f32[4,8,128]{2,1,0:T(8,128)S(1)} %get-tuple-element.67), channel_id=1, source_target_pairs={{0,96},{96,192},{192,288},{288,384},{384,480},{480,576},{576,672},... | collective-permute-start | bytes 49160 | tf_op jit(solution)/shard_map/ppermute | solution.py:25
  55.1 5.1 %collective-permute-start.11 = (f32[4,8,128]{2,1,0:T(8,128)S(1)}, f32[4,8,128]{2,1,0:T(8,128)S(1)}, u32[]{:S(2)}, u32[]{:S(2)}) collective-permute-start(f32[4,8,128]{2,1,0:T(8,128)S(1)} %get-tuple-element.68), channel_id=1, source_target_pairs={{96,0},{192,96},{288,192},{384,288},{480,384},{576,480},{672,576},... | collective-permute-start | bytes 49160 | tf_op jit(solution)/shard_map/ppermute | solution.py:25
  60.3 6.2 %collective-permute-start.12 = (f32[5,8,128]{2,1,0:T(8,128)S(1)}, f32[5,8,128]{2,1,0:T(8,128)S(1)}, u32[]{:S(2)}, u32[]{:S(2)}) collective-permute-start(f32[5,8,128]{2,1,0:T(8,128)S(1)} %get-tuple-element.69), channel_id=1, source_target_pairs={{0,12},{12,24},{24,36},{36,48},{48,60},{60,72},{72,84},{1,13},{13,... | collective-permute-start | bytes 61448 | tf_op jit(solution)/shard_map/ppermute | solution.py:25
  65.2 4.8 %collective-permute-start.13 = (f32[5,8,128]{2,1,0:T(8,128)S(1)}, f32[5,8,128]{2,1,0:T(8,128)S(1)}, u32[]{:S(2)}, u32[]{:S(2)}) collective-permute-start(f32[5,8,128]{2,1,0:T(8,128)S(1)} %get-tuple-element.70), channel_id=1, source_target_pairs={{12,0},{24,12},{36,24},{48,36},{60,48},{72,60},{84,72},{13,1},{25,... | collective-permute-start | bytes 61448 | tf_op jit(solution)/shard_map/ppermute | solution.py:25
  72.7 5.0 %collective-permute-start.14 = (f32[5,8,128]{2,1,0:T(8,128)S(1)}, f32[5,8,128]{2,1,0:T(8,128)S(1)}, u32[]{:S(2)}, u32[]{:S(2)}) collective-permute-start(f32[5,8,128]{2,1,0:T(8,128)S(1)} %get-tuple-element.72), channel_id=1, source_target_pairs={{0,12},{12,24},{24,36},{36,48},{48,60},{60,72},{72,84},{1,13},{13,... | collective-permute-start | bytes 61448 | tf_op jit(solution)/shard_map/ppermute | solution.py:25
  76.0 4.5 %collective-permute-start.15 = (f32[5,8,128]{2,1,0:T(8,128)S(1)}, f32[5,8,128]{2,1,0:T(8,128)S(1)}, u32[]{:S(2)}, u32[]{:S(2)}) collective-permute-start(f32[5,8,128]{2,1,0:T(8,128)S(1)} %get-tuple-element.73), channel_id=1, source_target_pairs={{12,0},{24,12},{36,24},{48,36},{60,48},{72,60},{84,72},{13,1},{25,... | collective-permute-start | bytes 61448 | tf_op jit(solution)/shard_map/ppermute | solution.py:25
  80.7 6.8 %collective-permute-start.16 = (f32[4,8,128]{2,1,0:T(8,128)S(1)}, f32[4,8,128]{2,1,0:T(8,128)S(1)}, u32[]{:S(2)}, u32[]{:S(2)}) collective-permute-start(f32[4,8,128]{2,1,0:T(8,128)S(1)} %get-tuple-element.79), channel_id=1, source_target_pairs={{0,96},{96,192},{192,288},{288,384},{384,480},{480,576},{576,672},... | collective-permute-start | bytes 49160 | tf_op jit(solution)/shard_map/ppermute | solution.py:25
  85.5 5.1 %collective-permute-start.17 = (f32[4,8,128]{2,1,0:T(8,128)S(1)}, f32[4,8,128]{2,1,0:T(8,128)S(1)}, u32[]{:S(2)}, u32[]{:S(2)}) collective-permute-start(f32[4,8,128]{2,1,0:T(8,128)S(1)} %get-tuple-element.80), channel_id=1, source_target_pairs={{96,0},{192,96},{288,192},{384,288},{480,384},{576,480},{672,576},... | collective-permute-start | bytes 49160 | tf_op jit(solution)/shard_map/ppermute | solution.py:25
  117.1 19.3 %copy-start.2 = (f32[8,8,128]{2,1,0:T(8,128)S(1)}, f32[8,8,128]{2,1,0:T(8,128)}, u32[]{:S(2)}) copy-start(f32[8,8,128]{2,1,0:T(8,128)} %param.5) | copy-start | bytes 98308

commit v6 on v5

--- a/solution.py
+++ b/solution.py
@@ -344,7 +344,12 @@
         out_specs=[VMEM] * 2,
         compiler_params=ROOM,
         name="end_messages",
-    )(*near(right_side, geometry, classes))
+    )(
+        *[
+            pltpu.with_memory_space_constraint(array, pltpu.HBM)
+            for array in (right_side, geometry, classes)
+        ]
+    )
 
 
 def received_lines(low, high, first, rows, width):

time: 139 us -> 138 us (level)
  no operation moved by 1% of the time
where the time goes in v6:
time: 138 us; the launch traced here: 137 us
  starting transfers between devices  51.4 us (37%)
  blocking collectives  42.6 us (31%)
  waiting for transfers between devices  24.9 us (18%)
  Pallas kernels  14.8 us (11%)
  local copies, waits for them, and re-layouts  1.63 us (1%)
    all_to_all x2, blocking collectives, exchange(): return lax.all_to_all(rows, axes, 0, 0, tiled=True)  42.6 us
    ppermute x9, starting transfers between devices, swap(): lax.ppermute(forward_part, axis, forward)  32.8 us
    ppermute x9, waiting for transfers between devices, swap(): lax.ppermute(backward_part, axis, backward)  24.9 us
    ppermute x9, starting transfers between devices, swap(): lax.ppermute(backward_part, axis, backward)  18.6 us
    pallas_call x2, Pallas kernels, block_solve(): pl.pallas_call(functools.partial(solve_kernel, count, shared), out_shape=...  5.23 us
  transfers between devices with their start and end apart: 18, of which 8 were waited for; matrix products, arithmetic and copies ran while one was open for 1% of the time, Pallas kernels for 1%

profile of v6, /device:TPU:1, one launch (start us, length us, event | category | flops | bytes accessed | tf_op | source)
XLA Modules:
  0.0 136.9 jit_solution(94709311646439872)
XLA Ops:
  1.8 4.8 %collective-permute-start = (f32[56,128]{1,0:T(8,128)S(1)}, f32[56,128]{1,0:T(8,128)S(1)}, u32[]{:S(2)}, u32[]{:S(2)}) collective-permute-start(f32[56,128]{1,0:T(8,128)S(1)} %get-tuple-element.47), channel_id=1, source_target_pairs={{0,1},{1,2},{2,3},{3,4},{4,5},{5,6},{6,7},{7,8},{8,9},{9,10},{10,1... | collective-permute-start | bytes 86024 | tf_op jit(solution)/shard_map/ppermute | solution.py:25
  6.6 1.3 collective-permute-start.1
  9.7 2.2 %collective-permute-done.1.high = f32[56,128]{1,0:T(8,128)S(1)} collective-permute-done((f32[56,128]{1,0:T(8,128)S(1)}, f32[56,128]{1,0:T(8,128)S(1)}, u32[]{:S(2)}, u32[]{:S(2)}) %collective-permute-start.1) | collective-permute-done | bytes 28704 | tf_op jit(solution)/shard_map/ppermute | solution.py:25
  12.3 4.8 %collective-permute-start.2 = (f32[4,8,128]{2,1,0:T(8,128)S(1)}, f32[4,8,128]{2,1,0:T(8,128)S(1)}, u32[]{:S(2)}, u32[]{:S(2)}) collective-permute-start(f32[4,8,128]{2,1,0:T(8,128)S(1)} %get-tuple-element.51), channel_id=1, source_target_pairs={{0,96},{96,192},{192,288},{288,384},{384,480},{480,576},{576,672},... | collective-permute-start | bytes 49160 | tf_op jit(solution)/shard_map/ppermute | solution.py:25
  17.1 5.9 %collective-permute-start.3 = (f32[4,8,128]{2,1,0:T(8,128)S(1)}, f32[4,8,128]{2,1,0:T(8,128)S(1)}, u32[]{:S(2)}, u32[]{:S(2)}) collective-permute-start(f32[4,8,128]{2,1,0:T(8,128)S(1)} %get-tuple-element.52), channel_id=1, source_target_pairs={{96,0},{192,96},{288,192},{384,288},{480,384},{576,480},{672,576},... | collective-permute-start | bytes 49160 | tf_op jit(solution)/shard_map/ppermute | solution.py:25
  25.1 1.3 collective-permute-start.4
  26.4 1.3 collective-permute-start.5
  27.7 3.4 %collective-permute-done.5.above = f32[5,8,128]{2,1,0:T(8,128)S(1)} collective-permute-done((f32[5,8,128]{2,1,0:T(8,128)S(1)}, f32[5,8,128]{2,1,0:T(8,128)S(1)}, u32[]{:S(2)}, u32[]{:S(2)}) %collective-permute-start.5) | collective-permute-done | bytes 20512 | tf_op jit(solution)/shard_map/ppermute | solution.py:25
  31.1 2.5 %block_solve_first.1 = (f32[10,10,8,128]{3,2,1,0:T(8,128)S(1)}, f32[4,10,8,128]{3,2,1,0:T(8,128)S(1)}, f32[5,8,128]{2,1,0:T(8,128)S(1)}, f32[5,8,128]{2,1,0:T(8,128)S(1)}, f32[1,128]{1,0:T(1,128)S(1)}) custom-call(f32[512,128]{1,0:T(8,128)S(1)} %get-tuple-element.50.field, f32[4,8,128]{2,1,0:T(8,128)S(1)} %collective-permute-done.2.low, ...), custom_call_target="tpu_custom_call" | custom-call | tf_op jit(solution)/shard_map/block_solve_first/pallas_call | solution.py:216
  33.7 2.1 %collective-permute-start.6 = (f32[5,8,128]{2,1,0:T(8,128)S(1)}, f32[5,8,128]{2,1,0:T(8,128)S(1)}, u32[]{:S(2)}, u32[]{:S(2)}) collective-permute-start(f32[5,8,128]{2,1,0:T(8,128)S(1)} %get-tuple-element.60), channel_id=1, source_target_pairs={{0,12},{12,24},{24,36},{36,48},{48,60},{60,72},{72,84},{1,13},{13,... | collective-permute-start | bytes 61448 | tf_op jit(solution)/shard_map/ppermute | solution.py:25
  35.8 1.3 collective-permute-start.7
  37.1 4.1 %collective-permute-done.7.above = f32[5,8,128]{2,1,0:T(8,128)S(1)} collective-permute-done((f32[5,8,128]{2,1,0:T(8,128)S(1)}, f32[5,8,128]{2,1,0:T(8,128)S(1)}, u32[]{:S(2)}, u32[]{:S(2)}) %collective-permute-start.7) | collective-permute-done | bytes 20512 | tf_op jit(solution)/shard_map/ppermute | solution.py:25
  41.4 5.0 %collective-permute-start.8 = (f32[4,8,128]{2,1,0:T(8,128)S(1)}, f32[4,8,128]{2,1,0:T(8,128)S(1)}, u32[]{:S(2)}, u32[]{:S(2)}) collective-permute-start(f32[4,8,128]{2,1,0:T(8,128)S(1)} %get-tuple-element.63), channel_id=1, source_target_pairs={{0,96},{96,192},{192,288},{288,384},{384,480},{480,576},{576,672},... | collective-permute-start | bytes 49160 | tf_op jit(solution)/shard_map/ppermute | solution.py:25
  46.4 1.9 %collective-permute-start.9 = (f32[4,8,128]{2,1,0:T(8,128)S(1)}, f32[4,8,128]{2,1,0:T(8,128)S(1)}, u32[]{:S(2)}, u32[]{:S(2)}) collective-permute-start(f32[4,8,128]{2,1,0:T(8,128)S(1)} %get-tuple-element.64), channel_id=1, source_target_pairs={{96,0},{192,96},{288,192},{384,288},{480,384},{576,480},{672,576},... | collective-permute-start | bytes 49160 | tf_op jit(solution)/shard_map/ppermute | solution.py:25
  48.3 3.1 %collective-permute-done.9.high = f32[4,8,128]{2,1,0:T(8,128)S(1)} collective-permute-done((f32[4,8,128]{2,1,0:T(8,128)S(1)}, f32[4,8,128]{2,1,0:T(8,128)S(1)}, u32[]{:S(2)}, u32[]{:S(2)}) %collective-permute-start.9) | collective-permute-done | bytes 16416 | tf_op jit(solution)/shard_map/ppermute | solution.py:25
  52.5 1.9 %collective-permute-start.10 = (f32[4,8,128]{2,1,0:T(8,128)S(1)}, f32[4,8,128]{2,1,0:T(8,128)S(1)}, u32[]{:S(2)}, u32[]{:S(2)}) collective-permute-start(f32[4,8,128]{2,1,0:T(8,128)S(1)} %get-tuple-element.67), channel_id=1, source_target_pairs={{0,96},{96,192},{192,288},{288,384},{384,480},{480,576},{576,672},... | collective-permute-start | bytes 49160 | tf_op jit(solution)/shard_map/ppermute | solution.py:25
  54.5 2.4 %collective-permute-start.11 = (f32[4,8,128]{2,1,0:T(8,128)S(1)}, f32[4,8,128]{2,1,0:T(8,128)S(1)}, u32[]{:S(2)}, u32[]{:S(2)}) collective-permute-start(f32[4,8,128]{2,1,0:T(8,128)S(1)} %get-tuple-element.68), channel_id=1, source_target_pairs={{96,0},{192,96},{288,192},{384,288},{480,384},{576,480},{672,576},... | collective-permute-start | bytes 49160 | tf_op jit(solution)/shard_map/ppermute | solution.py:25
  56.9 2.6 %collective-permute-done.11.high = f32[4,8,128]{2,1,0:T(8,128)S(1)} collective-permute-done((f32[4,8,128]{2,1,0:T(8,128)S(1)}, f32[4,8,128]{2,1,0:T(8,128)S(1)}, u32[]{:S(2)}, u32[]{:S(2)}) %collective-permute-start.11) | collective-permute-done | bytes 16416 | tf_op jit(solution)/shard_map/ppermute | solution.py:25
  59.7 4.7 %collective-permute-start.12 = (f32[5,8,128]{2,1,0:T(8,128)S(1)}, f32[5,8,128]{2,1,0:T(8,128)S(1)}, u32[]{:S(2)}, u32[]{:S(2)}) collective-permute-start(f32[5,8,128]{2,1,0:T(8,128)S(1)} %get-tuple-element.69), channel_id=1, source_target_pairs={{0,12},{12,24},{24,36},{36,48},{48,60},{60,72},{72,84},{1,13},{13,... | collective-permute-start | bytes 61448 | tf_op jit(solution)/shard_map/ppermute | solution.py:25
  64.4 1.3 collective-permute-start.13
  65.7 3.5 %collective-permute-done.13.above = f32[5,8,128]{2,1,0:T(8,128)S(1)} collective-permute-done((f32[5,8,128]{2,1,0:T(8,128)S(1)}, f32[5,8,128]{2,1,0:T(8,128)S(1)}, u32[]{:S(2)}, u32[]{:S(2)}) %collective-permute-start.13) | collective-permute-done | bytes 20512 | tf_op jit(solution)/shard_map/ppermute | solution.py:25
  69.2 2.7 %block_solve_shared.1 = (f32[10,10,8,128]{3,2,1,0:T(8,128)S(1)}, f32[4,10,8,128]{3,2,1,0:T(8,128)S(1)}, f32[5,8,128]{2,1,0:T(8,128)S(1)}, f32[5,8,128]{2,1,0:T(8...) custom-call(f32[512,128]{1,0:T(8,128)S(1)} %get-tuple-element.66.field, ...), custom_call_target="tpu_custom_call" | custom-call | tf_op jit(solution)/shard_map/block_solve_shared/pallas_call | solution.py:216
  71.9 3.4 %collective-permute-start.14 = (f32[5,8,128]{2,1,0:T(8,128)S(1)}, f32[5,8,128]{2,1,0:T(8,128)S(1)}, u32[]{:S(2)}, u32[]{:S(2)}) collective-permute-start(f32[5,8,128]{2,1,0:T(8,128)S(1)} %get-tuple-element.72), channel_id=1, source_target_pairs={{0,12},{12,24},{24,36},{36,48},{48,60},{60,72},{72,84},{1,13},{13,... | collective-permute-start | bytes 61448 | tf_op jit(solution)/shard_map/ppermute | solution.py:25
  75.2 1.3 collective-permute-start.15
  76.9 2.8 %collective-permute-done.15.above = f32[5,8,128]{2,1,0:T(8,128)S(1)} collective-permute-done((f32[5,8,128]{2,1,0:T(8,128)S(1)}, f32[5,8,128]{2,1,0:T(8,128)S(1)}, u32[]{:S(2)}, u32[]{:S(2)}) %collective-permute-start.15) | collective-permute-done | bytes 20512 | tf_op jit(solution)/shard_map/ppermute | solution.py:25
  79.9 4.8 %collective-permute-start.16 = (f32[4,8,128]{2,1,0:T(8,128)S(1)}, f32[4,8,128]{2,1,0:T(8,128)S(1)}, u32[]{:S(2)}, u32[]{:S(2)}) collective-permute-start(f32[4,8,128]{2,1,0:T(8,128)S(1)} %get-tuple-element.79), channel_id=1, source_target_pairs={{0,96},{96,192},{192,288},{288,384},{384,480},{480,576},{576,672},... | collective-permute-start | bytes 49160 | tf_op jit(solution)/shard_map/ppermute | solution.py:25
  84.7 1.9 %collective-permute-start.17 = (f32[4,8,128]{2,1,0:T(8,128)S(1)}, f32[4,8,128]{2,1,0:T(8,128)S(1)}, u32[]{:S(2)}, u32[]{:S(2)}) collective-permute-start(f32[4,8,128]{2,1,0:T(8,128)S(1)} %get-tuple-element.80), channel_id=1, source_target_pairs={{96,0},{192,96},{288,192},{384,288},{480,384},{576,480},{672,576},... | collective-permute-start | bytes 49160 | tf_op jit(solution)/shard_map/ppermute | solution.py:25
  86.7 3.0 %collective-permute-done.17.high = f32[4,8,128]{2,1,0:T(8,128)S(1)} collective-permute-done((f32[4,8,128]{2,1,0:T(8,128)S(1)}, f32[4,8,128]{2,1,0:T(8,128)S(1)}, u32[]{:S(2)}, u32[]{:S(2)}) %collective-permute-start.17) | collective-permute-done | bytes 16416 | tf_op jit(solution)/shard_map/ppermute | solution.py:25
  89.8 2.0 %second_operator.1 = (f32[128,128]{1,0:T(8,128)S(1)}, f32[12,1,128]{2,1,0:T(1,128)S(1)}) custom-call(s32[3]{0:T(128)S(1)} %pad_add_fusion.spot, f32[10,10,8,128]{3,2,1,0:T(8,128)S(1)} %get-tuple-element.71.folded, f32[5,8,128]{2,1,0:T(8,128)S(1)} %collective-permute-done.14.below, f32[5,8,128]{2,1,0:T(8,128)S(1)} %collective-permute-done.15.above, ...), custom_call_target="tpu_custom_call" | custom-call | tf_op jit(solution)/shard_map/second_operator/pallas_call | solution.py:519
  91.8 23.5 %all_to_all.16.gathered = f32[12,1,128]{2,1,0:T(1,128)S(1)} all-to-all(f32[12,1,128]{2,1,0:T(1,128)S(1)} %get-tuple-element.85), channel_id=1, replica_groups=mesh['gx'=8,'gy'=8,'gz'=12] {'gz'}, dimensions={0} | all-to-all | bytes 12288 | tf_op jit(solution)/shard_map/all_to_all | solution.py:678
  116.3 19.0 %all_to_all.17 = f32[64,8,128]{2,1,0:T(8,128)S(1)} all-to-all(f32[64,8,128]{2,1,0:T(8,128)S(1)} %bitcast.25), channel_id=1, replica_groups=mesh['gx'=8,'gy'=8,'gz'=12] {'gx','gy'}, dimensions={0} | all-to-all | bytes 524288 | tf_op jit(solution)/shard_map/all_to_all | solution.py:678
  135.4 1.5 %finish.1 = (f32[64,128]{1,0:T(8,128)}, f32[64,128]{1,0:T(8,128)}) custom-call(s32[3]{0:T(128)S(1)} %pad_add_fusion.spot, f32[512,128]{1,0:T(8,128)S(1)} %bitcast.19, f32[64,128]{1,0:T(8,128)S(1)} %get-tuple-element.88.image, f32[128,128]{1,0:T(8,128)S(1)} %get-tuple-element.86.lines.second, f32[128,128]{1,0:T(8,128)S(1)} %as_lines.1.first, ...), custom_call_target="tpu_custom_call" | custom-call | tf_op jit(solution)/shard_map/finish/pallas_call | solution.py:666
  (42 shorter events, 8.4 us)
Async XLA Ops:
  0.6 7.3 %copy-start = (f32[4,8,8,128]{3,2,1,0:T(8,128)S(1)}, f32[4,8,8,128]{3,2,1,0:T(8,128)}, u32[]{:S(2)}) copy-start(f32[4,8,8,128]{3,2,1,0:T(8,128)} %param.6) | copy-start | bytes 393220
  0.6 7.3 %copy-start.1 = (f32[8,8,128]{2,1,0:T(8,128)S(1)}, f32[8,8,128]{2,1,0:T(8,128)}, u32[]{:S(2)}) copy-start(f32[8,8,128]{2,1,0:T(8,128)} %param.5) | copy-start | bytes 98308
  0.6 8.8 %copy-start.2 = (f32[32,3,10,10]{0,1,3,2:T(4,128)S(1)}, f32[32,3,10,10]{0,1,3,2:T(4,128)}, u32[]{:S(2)}) copy-start(f32[32,3,10,10]{0,1,3,2:T(4,128)} %param.8) | copy-start | bytes 115204
  1.8 7.9 %collective-permute-start = (f32[56,128]{1,0:T(8,128)S(1)}, f32[56,128]{1,0:T(8,128)S(1)}, u32[]{:S(2)}, u32[]{:S(2)}) collective-permute-start(f32[56,128]{1,0:T(8,128)S(1)} %get-tuple-element.47), channel_id=1, source_target_pairs={{0,1},{1,2},{2,3},{3,4},{4,5},{5,6},{6,7},{7,8},{8,9},{9,10},{10,1... | collective-permute-start | bytes 86024 | tf_op jit(solution)/shard_map/ppermute | solution.py:25
  6.6 5.3 %collective-permute-start.1 = (f32[56,128]{1,0:T(8,128)S(1)}, f32[56,128]{1,0:T(8,128)S(1)}, u32[]{:S(2)}, u32[]{:S(2)}) collective-permute-start(f32[56,128]{1,0:T(8,128)S(1)} %get-tuple-element.48), channel_id=1, source_target_pairs={{1,0},{2,1},{3,2},{4,3},{5,4},{6,5},{7,6},{8,7},{9,8},{10,9},{11,1... | collective-permute-start | bytes 86024 | tf_op jit(solution)/shard_map/ppermute | solution.py:25
  12.3 12.7 %collective-permute-start.2 = (f32[4,8,128]{2,1,0:T(8,128)S(1)}, f32[4,8,128]{2,1,0:T(8,128)S(1)}, u32[]{:S(2)}, u32[]{:S(2)}) collective-permute-start(f32[4,8,128]{2,1,0:T(8,128)S(1)} %get-tuple-element.51), channel_id=1, source_target_pairs={{0,96},{96,192},{192,288},{288,384},{384,480},{480,576},{576,672},... | collective-permute-start | bytes 49160 | tf_op jit(solution)/shard_map/ppermute | solution.py:25
  17.1 7.8 %collective-permute-start.3 = (f32[4,8,128]{2,1,0:T(8,128)S(1)}, f32[4,8,128]{2,1,0:T(8,128)S(1)}, u32[]{:S(2)}, u32[]{:S(2)}) collective-permute-start(f32[4,8,128]{2,1,0:T(8,128)S(1)} %get-tuple-element.52), channel_id=1, source_target_pairs={{96,0},{192,96},{288,192},{384,288},{480,384},{576,480},{672,576},... | collective-permute-start | bytes 49160 | tf_op jit(solution)/shard_map/ppermute | solution.py:25
  23.0 0.7 copy-start.3
  25.1 2.6 %collective-permute-start.4 = (f32[5,8,128]{2,1,0:T(8,128)S(1)}, f32[5,8,128]{2,1,0:T(8,128)S(1)}, u32[]{:S(2)}, u32[]{:S(2)}) collective-permute-start(f32[5,8,128]{2,1,0:T(8,128)S(1)} %get-tuple-element.56), channel_id=1, source_target_pairs={{0,12},{12,24},{24,36},{36,48},{48,60},{60,72},{72,84},{1,13},{13,... | collective-permute-start | bytes 61448 | tf_op jit(solution)/shard_map/ppermute | solution.py:25
  26.4 4.7 %collective-permute-start.5 = (f32[5,8,128]{2,1,0:T(8,128)S(1)}, f32[5,8,128]{2,1,0:T(8,128)S(1)}, u32[]{:S(2)}, u32[]{:S(2)}) collective-permute-start(f32[5,8,128]{2,1,0:T(8,128)S(1)} %get-tuple-element.57), channel_id=1, source_target_pairs={{12,0},{24,12},{36,24},{48,36},{60,48},{72,60},{84,72},{13,1},{25,... | collective-permute-start | bytes 61448 | tf_op jit(solution)/shard_map/ppermute | solution.py:25
  33.7 3.4 %collective-permute-start.6 = (f32[5,8,128]{2,1,0:T(8,128)S(1)}, f32[5,8,128]{2,1,0:T(8,128)S(1)}, u32[]{:S(2)}, u32[]{:S(2)}) collective-permute-start(f32[5,8,128]{2,1,0:T(8,128)S(1)} %get-tuple-element.60), channel_id=1, source_target_pairs={{0,12},{12,24},{24,36},{36,48},{48,60},{60,72},{72,84},{1,13},{13,... | collective-permute-start | bytes 61448 | tf_op jit(solution)/shard_map/ppermute | solution.py:25
  35.8 5.4 %collective-permute-start.7 = (f32[5,8,128]{2,1,0:T(8,128)S(1)}, f32[5,8,128]{2,1,0:T(8,128)S(1)}, u32[]{:S(2)}, u32[]{:S(2)}) collective-permute-start(f32[5,8,128]{2,1,0:T(8,128)S(1)} %get-tuple-element.61), channel_id=1, source_target_pairs={{12,0},{24,12},{36,24},{48,36},{60,48},{72,60},{84,72},{13,1},{25,... | collective-permute-start | bytes 61448 | tf_op jit(solution)/shard_map/ppermute | solution.py:25
  41.4 6.9 %collective-permute-start.8 = (f32[4,8,128]{2,1,0:T(8,128)S(1)}, f32[4,8,128]{2,1,0:T(8,128)S(1)}, u32[]{:S(2)}, u32[]{:S(2)}) collective-permute-start(f32[4,8,128]{2,1,0:T(8,128)S(1)} %get-tuple-element.63), channel_id=1, source_target_pairs={{0,96},{96,192},{192,288},{288,384},{384,480},{480,576},{576,672},... | collective-permute-start | bytes 49160 | tf_op jit(solution)/shard_map/ppermute | solution.py:25
  46.4 5.1 %collective-permute-start.9 = (f32[4,8,128]{2,1,0:T(8,128)S(1)}, f32[4,8,128]{2,1,0:T(8,128)S(1)}, u32[]{:S(2)}, u32[]{:S(2)}) collective-permute-start(f32[4,8,128]{2,1,0:T(8,128)S(1)} %get-tuple-element.64), channel_id=1, source_target_pairs={{96,0},{192,96},{288,192},{384,288},{480,384},{576,480},{672,576},... | collective-permute-start | bytes 49160 | tf_op jit(solution)/shard_map/ppermute | solution.py:25
  52.5 4.3 %collective-permute-start.10 = (f32[4,8,128]{2,1,0:T(8,128)S(1)}, f32[4,8,128]{2,1,0:T(8,128)S(1)}, u32[]{:S(2)}, u32[]{:S(2)}) collective-permute-start(f32[4,8,128]{2,1,0:T(8,128)S(1)} %get-tuple-element.67), channel_id=1, source_target_pairs={{0,96},{96,192},{192,288},{288,384},{384,480},{480,576},{576,672},... | collective-permute-start | bytes 49160 | tf_op jit(solution)/shard_map/ppermute | solution.py:25
  54.5 5.1 %collective-permute-start.11 = (f32[4,8,128]{2,1,0:T(8,128)S(1)}, f32[4,8,128]{2,1,0:T(8,128)S(1)}, u32[]{:S(2)}, u32[]{:S(2)}) collective-permute-start(f32[4,8,128]{2,1,0:T(8,128)S(1)} %get-tuple-element.68), channel_id=1, source_target_pairs={{96,0},{192,96},{288,192},{384,288},{480,384},{576,480},{672,576},... | collective-permute-start | bytes 49160 | tf_op jit(solution)/shard_map/ppermute | solution.py:25
  59.7 6.0 %collective-permute-start.12 = (f32[5,8,128]{2,1,0:T(8,128)S(1)}, f32[5,8,128]{2,1,0:T(8,128)S(1)}, u32[]{:S(2)}, u32[]{:S(2)}) collective-permute-start(f32[5,8,128]{2,1,0:T(8,128)S(1)} %get-tuple-element.69), channel_id=1, source_target_pairs={{0,12},{12,24},{24,36},{36,48},{48,60},{60,72},{72,84},{1,13},{13,... | collective-permute-start | bytes 61448 | tf_op jit(solution)/shard_map/ppermute | solution.py:25
  64.4 4.8 %collective-permute-start.13 = (f32[5,8,128]{2,1,0:T(8,128)S(1)}, f32[5,8,128]{2,1,0:T(8,128)S(1)}, u32[]{:S(2)}, u32[]{:S(2)}) collective-permute-start(f32[5,8,128]{2,1,0:T(8,128)S(1)} %get-tuple-element.70), channel_id=1, source_target_pairs={{12,0},{24,12},{36,24},{48,36},{60,48},{72,60},{84,72},{13,1},{25,... | collective-permute-start | bytes 61448 | tf_op jit(solution)/shard_map/ppermute | solution.py:25
  71.9 5.0 %collective-permute-start.14 = (f32[5,8,128]{2,1,0:T(8,128)S(1)}, f32[5,8,128]{2,1,0:T(8,128)S(1)}, u32[]{:S(2)}, u32[]{:S(2)}) collective-permute-start(f32[5,8,128]{2,1,0:T(8,128)S(1)} %get-tuple-element.72), channel_id=1, source_target_pairs={{0,12},{12,24},{24,36},{36,48},{48,60},{60,72},{72,84},{1,13},{13,... | collective-permute-start | bytes 61448 | tf_op jit(solution)/shard_map/ppermute | solution.py:25
  75.2 4.5 %collective-permute-start.15 = (f32[5,8,128]{2,1,0:T(8,128)S(1)}, f32[5,8,128]{2,1,0:T(8,128)S(1)}, u32[]{:S(2)}, u32[]{:S(2)}) collective-permute-start(f32[5,8,128]{2,1,0:T(8,128)S(1)} %get-tuple-element.73), channel_id=1, source_target_pairs={{12,0},{24,12},{36,24},{48,36},{60,48},{72,60},{84,72},{13,1},{25,... | collective-permute-start | bytes 61448 | tf_op jit(solution)/shard_map/ppermute | solution.py:25
  79.9 6.8 %collective-permute-start.16 = (f32[4,8,128]{2,1,0:T(8,128)S(1)}, f32[4,8,128]{2,1,0:T(8,128)S(1)}, u32[]{:S(2)}, u32[]{:S(2)}) collective-permute-start(f32[4,8,128]{2,1,0:T(8,128)S(1)} %get-tuple-element.79), channel_id=1, source_target_pairs={{0,96},{96,192},{192,288},{288,384},{384,480},{480,576},{576,672},... | collective-permute-start | bytes 49160 | tf_op jit(solution)/shard_map/ppermute | solution.py:25
  84.7 5.1 %collective-permute-start.17 = (f32[4,8,128]{2,1,0:T(8,128)S(1)}, f32[4,8,128]{2,1,0:T(8,128)S(1)}, u32[]{:S(2)}, u32[]{:S(2)}) collective-permute-start(f32[4,8,128]{2,1,0:T(8,128)S(1)} %get-tuple-element.80), channel_id=1, source_target_pairs={{96,0},{192,96},{288,192},{384,288},{480,384},{576,480},{672,576},... | collective-permute-start | bytes 49160 | tf_op jit(solution)/shard_map/ppermute | solution.py:25
